TPU v7x, 768 devices: a whole 4x8x12 slice. The times are simulated.
768 devices in a mesh: section: 3 (over z_lo), win: 64 (over x, y, core), dp: 4 (over z_hi).
Axes of the slice: x: 4, y: 8, z: 12 (z_hi: 4, z_lo: 3; z = z_hi * 3 + z_lo), core: 2. Of those that a mesh axis runs over, the one named last changes fastest.
Arguments:
- tokens: bfloat16 [2, 64, 4, 64, 1536], P(None, 'win', 'dp'), may hold values from -6 to 6
- regions: int32 [3, 64, 256], P('section', 'win'), may hold values from 0 to 3
- norm_gain: float32 [3, 1536], P('section'), may hold values from 0.1 to 1.9
- qkv_weight: bfloat16 [3, 1536, 3, 1024], P('section', None, None, 'dp'), as said below
- out_weight: bfloat16 [3, 1024, 1536], P('section', 'dp'), may hold values from -2 to 2
- final_gain: float32 [1536], replicated, may hold values from 0.1 to 1.9
- dec_weight: bfloat16 [1536, 1104], P(None, 'section'), may hold values from -0.15625 to 0.15625
Outputs:
- decoded: bfloat16 [2, 64, 4, 64, 1104], P(None, 'win', 'dp', None, 'section')
Inputs may be any that keep to these rules, and one draw needn't show every extreme that they name: `qkv_weight`: entries lie below 80 / sqrt(1536) in magnitude.
All inputs are finite; a program needn't handle non-finite values.
Results may differ from a plain program's by a relative error of at most 0.03.
Values may be sent and summed in bfloat16 or wider, within the bound.
No kernel may reach another device: no remote copies, remote signals or barrier semaphores. Data moves between devices by JAX's collectives and lax.ppermute only.
A program may use at most 32 MiB of HBM per device.

v0:
```python
import math

import jax
import jax.numpy as jnp
from jax import lax
from jax.sharding import PartitionSpec as P

HEAD_DIM = 64


def from_behind(value, axis, steps):
    count = lax.axis_size(axis)
    pairs = [(source, (source + steps) % count) for source in range(count)]
    return lax.ppermute(value, axis, pairs)


def shifted(value, axis, steps):
    count = lax.axis_size(axis)
    leading, last = (max(0, -steps), min(count, count - steps))
    return lax.ppermute(value, axis, [(source, source + steps) for source in range(leading, last)])


def from_root(block, axis, holder):
    block = jnp.where(lax.axis_index(axis) == holder, block, jnp.zeros_like(block))
    return lax.psum(block, axis)


def normalize(hidden, scales):
    values = hidden.astype(jnp.float32)
    center = values - jnp.mean(values, axis=-1, keepdims=True)
    spread = jnp.mean(center * center, axis=-1, keepdims=True)
    return (center * lax.rsqrt(spread + 1e-05) * scales).astype(jnp.bfloat16)


def rounded(values):
    return lax.optimization_barrier(values.astype(jnp.bfloat16)).astype(jnp.float32)


def attend(projected, labels, head_size):
    row_count = projected.shape[0]
    inner_width = projected.shape[2]
    head_count = inner_width // head_size
    queries = projected[:, 0].reshape(row_count, head_count, head_size)
    keys_all = projected[:, 1].reshape(row_count, head_count, head_size)
    values_all = projected[:, 2].reshape(row_count, head_count, head_size)
    scores = jnp.einsum(
        "qhe,khe->hqk", queries, keys_all, preferred_element_type=jnp.float32
    ) / math.sqrt(head_size)
    allowed = labels[:, None] == labels[None, :]
    scores = jnp.where(allowed[None], scores, -jnp.inf)
    largest = jnp.max(scores, axis=-1, keepdims=True)
    weights = jnp.exp(scores - largest)
    shares = (weights / jnp.sum(weights, axis=-1, keepdims=True)).astype(jnp.bfloat16)
    blended = jnp.einsum("hqk,khe->qhe", shares, values_all, preferred_element_type=jnp.float32)
    return blended.astype(jnp.bfloat16).reshape(row_count, inner_width)


def body(tokens, regions, norm_gain, qkv_weight, out_weight, final_gain, dec_weight):
    sections = lax.axis_size("section")
    section_index = lax.axis_index("section")
    micro_count = tokens.shape[0]
    quad_rows = tokens.shape[3]
    half_rows = quad_rows // 2
    labels = regions[0, 0]
    layer_gain = norm_gain[0]
    projection = qkv_weight[0]
    out_local = out_weight[0]
    empty = jnp.zeros(tokens.shape[3:], jnp.bfloat16)
    incoming = empty
    finished = []
    for moment in range(micro_count + sections - 1):
        fresh = tokens[moment, 0, 0] if moment < micro_count else empty
        current = jnp.where(section_index == 0, fresh, incoming)
        normed = normalize(current, layer_gain)
        projected = jnp.einsum(
            "td,dcf->tcf",
            lax.all_gather(normed, "dp", axis=0, tiled=True),
            projection,
            preferred_element_type=jnp.float32,
        ).astype(jnp.bfloat16)
        blended = attend(projected, labels, HEAD_DIM)
        update = lax.psum_scatter(
            rounded(jnp.dot(blended, out_local, preferred_element_type=jnp.float32)).astype(
                jnp.bfloat16
            ),
            "dp",
            scatter_dimension=0,
            tiled=True,
        ).astype(jnp.float32)
        hidden = (current.astype(jnp.float32) + update).astype(jnp.bfloat16)
        arriving = from_behind(hidden[:half_rows], "win", -1)
        result = jnp.concatenate([hidden[half_rows:], arriving], axis=0)
        if moment >= sections - 1:
            finished.append(result)
        if moment < micro_count + sections - 2:
            incoming = shifted(result, "section", 1)
    collected = jnp.stack(finished)
    final = normalize(collected, final_gain)
    shared = from_root(final, "section", sections - 1)
    decoded = jnp.einsum(
        "mtd,dc->mtc", shared, dec_weight, preferred_element_type=jnp.float32
    ).astype(jnp.bfloat16)
    return decoded[:, None, None]


def solution(mesh):
    return jax.shard_map(
        body,
        mesh=mesh,
        in_specs=(
            P(None, "win", "dp", None, None),
            P("section", "win", None),
            P("section", None),
            P("section", None, None, "dp"),
            P("section", "dp", None),
            P(),
            P(None, "section"),
        ),
        out_specs=P(None, "win", "dp", None, "section"),
        check_vma=False,
    )
```

profile of v0, /device:TPU:1, one launch (start us, length us, event | category | flops | bytes accessed | tf_op | source)
XLA Modules:
  0.0 445.7 jit_solution(12540194457908775404)
XLA Ops:
  11.6 33.4 %all_gather.12 = bf16[256,1536]{1,0:T(8,128)(2,1)S(1)} all-gather(bf16[64,1536]{1,0:T(8,128)(2,1)S(1)} %fusion.74), channel_id=1, replica_groups=mesh['section'=3,'win'=64,'dp'=4] {'dp'}, dimensions={0}, use_global_device_ids=true | all-gather | bytes 983040 | tf_op jit(solution)/shard_map/all_gather | solution.py:77
  47.9 2.6 convolution_convert_fusion.7
  52.9 45.4 %reduce-scatter.5.cloned.1.call-done = bf16[64,1536]{1,0:T(8,128)(2,1)} async-done(((bf16[256,1536]{1,0:T(8,128)(2,1)}), bf16[64,1536]{1,0:T(8,128)(2,1)}) %reduce-scatter.5.cloned.1.call-update) | async-done | bytes 196624 | tf_op jit(solution)/shard_map/reduce_scatter | solution.py:82
  99.3 3.1 collective-permute-start
  102.4 3.1 collective-permute-done
  105.5 3.0 collective-permute-start.1
  108.5 2.6 collective-permute-done.1
  112.6 21.2 %all_gather.13 = bf16[256,1536]{1,0:T(8,128)(2,1)S(1)} all-gather(bf16[64,1536]{1,0:T(8,128)(2,1)S(1)} %fusion.71), channel_id=1, replica_groups=mesh['section'=3,'win'=64,'dp'=4] {'dp'}, dimensions={0}, use_global_device_ids=true | all-gather | bytes 983040 | tf_op jit(solution)/shard_map/all_gather | solution.py:77
  142.6 48.6 %reduce-scatter.7.cloned.1.call-done = bf16[64,1536]{1,0:T(8,128)(2,1)} async-done(((bf16[256,1536]{1,0:T(8,128)(2,1)}), bf16[64,1536]{1,0:T(8,128)(2,1)}) %reduce-scatter.7.cloned.1.call-update) | async-done | bytes 196624 | tf_op jit(solution)/shard_map/reduce_scatter | solution.py:82
  192.2 3.0 collective-permute-start.2
  195.2 3.4 collective-permute-done.2
  201.0 2.6 collective-permute-done.3
  204.1 21.0 %all_gather.14 = bf16[256,1536]{1,0:T(8,128)(2,1)S(1)} all-gather(bf16[64,1536]{1,0:T(8,128)(2,1)S(1)} %fusion.68), channel_id=1, replica_groups=mesh['section'=3,'win'=64,'dp'=4] {'dp'}, dimensions={0}, use_global_device_ids=true | all-gather | bytes 983040 | tf_op jit(solution)/shard_map/all_gather | solution.py:77
  233.9 48.8 %reduce-scatter.9.cloned.1.call-done = bf16[64,1536]{1,0:T(8,128)(2,1)} async-done(((bf16[256,1536]{1,0:T(8,128)(2,1)}), bf16[64,1536]{1,0:T(8,128)(2,1)}) %reduce-scatter.9.cloned.1.call-update) | async-done | bytes 196624 | tf_op jit(solution)/shard_map/reduce_scatter | solution.py:82
  283.7 3.5 collective-permute-start.4
  287.2 3.0 collective-permute-done.4
  290.2 3.2 collective-permute-start.5
  293.5 2.6 collective-permute-done.5
  296.5 21.9 %all_gather.15 = bf16[256,1536]{1,0:T(8,128)(2,1)S(1)} all-gather(bf16[64,1536]{1,0:T(8,128)(2,1)S(1)} %fusion.65), channel_id=1, replica_groups=mesh['section'=3,'win'=64,'dp'=4] {'dp'}, dimensions={0}, use_global_device_ids=true | all-gather | bytes 983040 | tf_op jit(solution)/shard_map/all_gather | solution.py:77
  324.0 2.6 convolution_convert_fusion.4
  328.9 47.6 %reduce-scatter.11.cloned.1.call-done = bf16[64,1536]{1,0:T(8,128)(2,1)} async-done(((bf16[256,1536]{1,0:T(8,128)(2,1)}), bf16[64,1536]{1,0:T(8,128)(2,1)}) %reduce-scatter.11.cloned.1.call-update) | async-done | bytes 196624 | tf_op jit(solution)/shard_map/reduce_scatter | solution.py:82
  377.5 3.1 collective-permute-start.6
  380.6 3.6 collective-permute-done.6
  385.7 51.0 %all-reduce.2.cloned.1.call-done = bf16[2,64,1536]{2,1,0:T(8,128)(2,1)} async-done(((bf16[2,64,1536]{2,1,0:T(8,128)(2,1)}), bf16[2,64,1536]{2,1,0:T(8,128)(2,1)}) %all-reduce.2.cloned.1.call-update) | async-done | bytes 393232 | tf_op jit(solution)/shard_map/psum | solution.py:25
  (85 shorter events, 48.6 us)
Async XLA Ops:
  6.5 38.4 %copy-start = (bf16[1,1536,3,256]{3,1,2,0:T(8,128)(2,1)S(1)}, bf16[1,1536,3,256]{3,1,2,0:T(8,128)(2,1)}, u32[]{:S(2)}) copy-start(bf16[1,1536,3,256]{3,1,2,0:T(8,128)(2,1)} %param.10) | copy-start | bytes 7077892
  6.5 91.7 %reduce-scatter.5.cloned.1.call-start = ((), (), s32[]{:S(2)}) async-start(), calls=%async_computation.4 | async-start | bytes 983040 | tf_op jit(solution)/shard_map/reduce_scatter | solution.py:82
  9.8 36.8 %copy-start.3 = (pred[256,256]{0,1:T(8,128)(4,1)}, pred[256,256]{0,1:T(8,128)(4,1)S(1)}, u32[]{:S(2)}) copy-start(pred[256,256]{0,1:T(8,128)(4,1)S(1)} %broadcast_compare_fusion) | copy-start | bytes 196612
  47.9 2.7 copy-start.1
  50.6 47.7 %copy-start.2 = (bf16[2,1,1,64,1536]{4,3,2,1,0:T(8,128)(2,1)S(1)}, bf16[2,1,1,64,1536]{4,3,2,1,0:T(8,128)(2,1)}, u32[]{:S(2)}) copy-start(bf16[2,1,1,64,1536]{4,3,2,1,0:T(8,128)(2,1)} %param.7) | copy-start | bytes 1179652
  52.8 138.3 %reduce-scatter.7.cloned.1.call-start = ((), (), s32[]{:S(2)}) async-start(), calls=%async_computation.5 | async-start | bytes 983040 | tf_op jit(solution)/shard_map/reduce_scatter | solution.py:82
  99.3 6.2 %collective-permute-start = (bf16[32,1536]{1,0:T(8,128)(2,1)S(1)}, bf16[32,1536]{1,0:T(8,128)(2,1)S(1)}, u32[]{:S(2)}, u32[]{:S(2)}) collective-permute-start(bf16[32,1536]{1,0:T(8,128)(2,1)S(1)} %get-tuple-element.28), channel_id=1, source_target_pairs={{0,252},{4,0},{8,4},{12,8},{16,12},{20,16},{24,20},{28,24},{32,28}... | collective-permute-start | bytes 294920 | tf_op jit(solution)/shard_map/ppermute | solution.py:14
  105.5 5.6 %collective-permute-start.1 = (bf16[64,1536]{1,0:T(8,128)(2,1)S(1)}, bf16[64,1536]{1,0:T(8,128)(2,1)S(1)}, u32[]{:S(2)}, u32[]{:S(2)}) collective-permute-start(bf16[64,1536]{1,0:T(8,128)(2,1)S(1)} %pad_maximum_fusion.1), channel_id=1, source_target_pairs={{0,256},{256,512},{1,257},{257,513},{2,258},{258,514},{3,259},{259... | collective-permute-start | bytes 589832 | tf_op jit(solution)/shard_map/ppermute | solution.py:20
  133.8 1.8 copy-start.4
  142.5 140.1 %reduce-scatter.9.cloned.1.call-start = ((), (), s32[]{:S(2)}) async-start(), calls=%async_computation.6 | async-start | bytes 983040 | tf_op jit(solution)/shard_map/reduce_scatter | solution.py:82
  192.2 6.4 %collective-permute-start.2 = (bf16[32,1536]{1,0:T(8,128)(2,1)S(1)}, bf16[32,1536]{1,0:T(8,128)(2,1)S(1)}, u32[]{:S(2)}, u32[]{:S(2)}) collective-permute-start(bf16[32,1536]{1,0:T(8,128)(2,1)S(1)} %get-tuple-element.26), channel_id=1, source_target_pairs={{0,252},{4,0},{8,4},{12,8},{16,12},{20,16},{24,20},{28,24},{32,28}... | collective-permute-start | bytes 294920 | tf_op jit(solution)/shard_map/ppermute | solution.py:14
  198.6 5.0 %collective-permute-start.3 = (bf16[64,1536]{1,0:T(8,128)(2,1)S(1)}, bf16[64,1536]{1,0:T(8,128)(2,1)S(1)}, u32[]{:S(2)}, u32[]{:S(2)}) collective-permute-start(bf16[64,1536]{1,0:T(8,128)(2,1)S(1)} %pad_maximum_fusion.2), channel_id=1, source_target_pairs={{0,256},{256,512},{1,257},{257,513},{2,258},{258,514},{3,259},{259... | collective-permute-start | bytes 589832 | tf_op jit(solution)/shard_map/ppermute | solution.py:20
  233.8 142.7 %reduce-scatter.11.cloned.1.call-start = ((), (), s32[]{:S(2)}) async-start(), calls=%async_computation.7 | async-start | bytes 983040 | tf_op jit(solution)/shard_map/reduce_scatter | solution.py:82
  283.7 6.5 %collective-permute-start.4 = (bf16[32,1536]{1,0:T(8,128)(2,1)S(1)}, bf16[32,1536]{1,0:T(8,128)(2,1)S(1)}, u32[]{:S(2)}, u32[]{:S(2)}) collective-permute-start(bf16[32,1536]{1,0:T(8,128)(2,1)S(1)} %get-tuple-element.24), channel_id=1, source_target_pairs={{0,252},{4,0},{8,4},{12,8},{16,12},{20,16},{24,20},{28,24},{32,28}... | collective-permute-start | bytes 294920 | tf_op jit(solution)/shard_map/ppermute | solution.py:14
  290.2 5.8 %collective-permute-start.5 = (bf16[64,1536]{1,0:T(8,128)(2,1)S(1)}, bf16[64,1536]{1,0:T(8,128)(2,1)S(1)}, u32[]{:S(2)}, u32[]{:S(2)}) collective-permute-start(bf16[64,1536]{1,0:T(8,128)(2,1)S(1)} %get-tuple-element.20), channel_id=1, source_target_pairs={{0,256},{256,512},{1,257},{257,513},{2,258},{258,514},{3,259},{259... | collective-permute-start | bytes 589832 | tf_op jit(solution)/shard_map/ppermute | solution.py:20
  326.6 58.0 %copy-start.5 = (f32[1536]{0:T(1024)S(1)}, f32[1536]{0:T(1024)}, u32[]{:S(2)}) copy-start(f32[1536]{0:T(1024)} %param.12) | copy-start | bytes 18436
  328.8 107.8 %all-reduce.2.cloned.1.call-start = ((), (), s32[]{:S(2)}) async-start(), calls=%async_computation.8 | async-start | bytes 786432 | tf_op jit(solution)/shard_map/psum | solution.py:25
  377.5 6.7 %collective-permute-start.6 = (bf16[32,1536]{1,0:T(8,128)(2,1)S(1)}, bf16[32,1536]{1,0:T(8,128)(2,1)S(1)}, u32[]{:S(2)}, u32[]{:S(2)}) collective-permute-start(bf16[32,1536]{1,0:T(8,128)(2,1)S(1)} %get-tuple-element.22), channel_id=1, source_target_pairs={{0,252},{4,0},{8,4},{12,8},{16,12},{20,16},{24,20},{28,24},{32,28}... | collective-permute-start | bytes 294920 | tf_op jit(solution)/shard_map/ppermute | solution.py:14
Sparse Core Ops, SparseCore 0:
  52.9 45.2 reduce-scatter.4
  142.7 48.4 reduce-scatter.6
  233.9 48.7 reduce-scatter.8
  329.0 47.4 reduce-scatter.10
  385.8 50.8 all-reduce.1
where the time goes:
time: 447 us; the launch traced here: 446 us
  waiting for transfers between devices  262 us (59%)
  blocking collectives  97.4 us (22%)
  matrix products  35.9 us (8%)
  starting transfers between devices  21.5 us (5%)
  between operations  13.4 us (3%)
  other arithmetic  13 us (3%)
    reduce_scatter x4, waiting for transfers between devices, body(): lax.psum_scatter(rounded(jnp.dot(blended, out_local, preferred_element_ty...  190 us
    all_gather x4, blocking collectives, body(): lax.all_gather(normed, 'dp', axis=0, tiled=True)  97.4 us
    psum x1, waiting for transfers between devices, from_root(): return lax.psum(block, axis)  51 us
    ppermute x4, waiting for transfers between devices, from_behind(): return lax.ppermute(value, axis, pairs)  13.1 us
    ppermute x4, starting transfers between devices, from_behind(): return lax.ppermute(value, axis, pairs)  12.8 us
    dot_general x4, matrix products, attend(): jnp.einsum('hqk,khe->qhe', shares, values_all, preferred_element_type=jnp...  9.22 us
  transfers between devices with their start and end apart: 12, of which 12 were waited for; matrix products, arithmetic and copies ran while one was open for 0% of the time, Pallas kernels for 0%

commit v1 on v0

v1 whole, which is shorter than its diff:
```python
import jax
import jax.numpy as jnp
import numpy as np
from jax import lax
from jax.experimental import pallas as pl
from jax.experimental.pallas import tpu as pltpu
from jax.sharding import Mesh
from jax.sharding import PartitionSpec as P

HEAD = 64
AXES = ("section", "x", "y", "core", "dp")
WIN = ("x", "y", "core")


def chip_of(parity, micro):
    return 2 * micro + (parity ^ micro)


def parity_of(chip):
    return (chip ^ (chip >> 1)) & 1


def norm(values, gain):
    center = values - jnp.mean(values, axis=-1, keepdims=True)
    spread = jnp.mean(center * center, axis=-1, keepdims=True)
    return (center * lax.rsqrt(spread + 1e-05) * gain).astype(jnp.bfloat16)


def layer_kernel(lq, lk, gain, own_a, own_b, far_a, far_b, native, others, out_a, out_b, held, normed, acc, sems):
    quarters = held.shape[0]
    slices, per, width = held.shape[1:]
    inner = width // 3
    rows = per * 3 // 4
    orows = per // 8
    copies = [pltpu.make_async_copy(native, held.at[0], sems.at[0])]
    for step in range(1, quarters):
        copies.append(pltpu.make_async_copy(others.at[:, step - 1], held.at[step], sems.at[step]))
    for copy in copies:
        copy.start()
    part = own_a.shape[0]
    half = 2 * part
    for index, ref in enumerate((own_a, own_b, far_a, far_b)):
        normed[index * part:(index + 1) * part, :] = norm(ref[...].astype(jnp.float32), gain[...])
    allowed = lq[...] == lk[...]
    for step in range(quarters):
        copies[step].wait()
        weight = held[step, :, :rows, :].reshape(slices * rows, width)
        keyval = jnp.dot(normed[...], weight[:, inner:], preferred_element_type=jnp.float32).astype(jnp.bfloat16)
        query = jnp.dot(normed[:half, :], weight[:, :inner], preferred_element_type=jnp.float32).astype(jnp.bfloat16)
        parts = []
        for head in range(inner // HEAD):
            at = head * HEAD
            scores = lax.dot_general(
                query[:, at:at + HEAD], keyval[:, at:at + HEAD],
                (((1,), (1,)), ((), ())), preferred_element_type=jnp.float32,
            ) * (HEAD ** -0.5)
            scores = jnp.where(allowed, scores, -jnp.inf)
            weights = jnp.exp(scores - jnp.max(scores, axis=-1, keepdims=True))
            shares = (weights / jnp.sum(weights, axis=-1, keepdims=True)).astype(jnp.bfloat16)
            parts.append(jnp.dot(shares, keyval[:, inner + at:inner + at + HEAD], preferred_element_type=jnp.float32))
        blended = jnp.concatenate(parts, axis=-1).astype(jnp.bfloat16)
        for side in range(2):
            low = rows + side * orows
            matrix = held[step, :, low:low + orows, :].reshape(slices * orows, width)
            update = jnp.dot(blended, matrix, preferred_element_type=jnp.float32).astype(jnp.bfloat16).astype(jnp.float32)
            cols = slice(side * width, (side + 1) * width)
            if step == 0:
                acc[:, cols] = update
            else:
                acc[:, cols] += update
    out_a[...] = (own_a[...].astype(jnp.float32) + acc[:part, :]).astype(jnp.bfloat16)
    out_b[...] = (own_b[...].astype(jnp.float32) + acc[part:, :]).astype(jnp.bfloat16)


def layer(lq, lk, gain, own_a, own_b, far_a, far_b, native, others):
    part, depth = own_a.shape
    quarters = others.shape[1] + 1
    vmem = pl.BlockSpec(memory_space=pltpu.VMEM)
    hbm = pl.BlockSpec(memory_space=pl.ANY)
    shape = jax.ShapeDtypeStruct((part, depth), jnp.bfloat16)
    return pl.pallas_call(
        layer_kernel,
        out_shape=(shape, shape),
        in_specs=[vmem] * 7 + [hbm] * 2,
        out_specs=(vmem, vmem),
        scratch_shapes=[
            pltpu.VMEM((quarters,) + native.shape, jnp.bfloat16),
            pltpu.VMEM((4 * part, depth), jnp.bfloat16),
            pltpu.VMEM((2 * part, depth), jnp.float32),
            pltpu.SemaphoreType.DMA((quarters,)),
        ],
        compiler_params=pltpu.CompilerParams(vmem_limit_bytes=40 << 20),
        cost_estimate=pl.CostEstimate(flops=2_600_000_000, bytes_accessed=14_000_000, transcendentals=524288),
        name="layer",
    )(lq, lk, gain, own_a, own_b, far_a, far_b, native, others)


def decode_kernel(gain, part_a, part_b, matrix, out):
    rows = jnp.concatenate([part_a[...], part_b[...]], axis=0).astype(jnp.float32)
    final = norm(rows, gain[...])
    slices, sections, per, width = matrix.shape
    for section in range(sections):
        weight = matrix[:, section].reshape(slices * per, width)
        out[section] = jnp.dot(final, weight, preferred_element_type=jnp.float32).astype(jnp.bfloat16)


def decode(gain, part_a, part_b, matrix):
    vmem = pl.BlockSpec(memory_space=pltpu.VMEM)
    return pl.pallas_call(
        decode_kernel,
        out_shape=jax.ShapeDtypeStruct((matrix.shape[1], 2 * part_a.shape[0], matrix.shape[3]), jnp.bfloat16),
        in_specs=[vmem] * 4,
        out_specs=vmem,
        compiler_params=pltpu.CompilerParams(vmem_limit_bytes=24 << 20),
        cost_estimate=pl.CostEstimate(flops=450_000_000, bytes_accessed=4_500_000, transcendentals=0),
        name="decode",
    )(gain, part_a, part_b, matrix)


def solution(mesh):
    sections, windows, bands = (mesh.shape[name] for name in ("section", "win", "dp"))
    fine = Mesh(np.asarray(mesh.devices).reshape(sections, windows // 16, 8, 2, bands), AXES)
    chips = windows // 2

    def place(section, window, chip):
        return (section * windows + window % windows) * bands + chip

    def send(value, route, sources):
        pairs = []
        for section in sources:
            for window in range(windows):
                for chip in range(bands):
                    target = route(section, window, chip)
                    if target is not None:
                        pairs.append((place(section, window, chip), place(*target)))
        return lax.ppermute(value, AXES, pairs)

    def to_other_core(value, sources):
        return send(value, lambda s, w, d: (s, w ^ 1, d), sources)

    def body(tokens, regions, norm_gain, qkv_weight, out_weight, final_gain, dec_weight):
        section = lax.axis_index("section")
        core = lax.axis_index("core")
        chip = lax.axis_index("dp")
        mine = lax.axis_index("y") * 2 + core
        depth = tokens.shape[-1]
        quad = tokens.shape[3]
        half = quad // 2
        micro = chip >> 1
        parity = (chip ^ (chip >> 1)) & 1
        width = qkv_weight.shape[2] * qkv_weight.shape[3]

        native = jnp.concatenate(
            [
                qkv_weight[0].reshape(16, depth // 16, width),
                out_weight[0].reshape(16, -1, 2, width)[:, :, 0],
                out_weight[0].reshape(16, -1, 2, width)[:, :, 1],
            ],
            axis=1,
        )
        piece = lax.dynamic_index_in_dim(native, mine, 0, keepdims=False)
        column = lax.all_gather(piece, "dp", axis=0)
        rolled = lax.dynamic_slice_in_dim(jnp.concatenate([column, column], axis=0), chip + 1, bands - 1, 0)
        others = lax.all_gather(rolled, ("y", "core"), axis=0)
        strip = lax.dynamic_index_in_dim(dec_weight.reshape(16, depth // 16, -1), mine, 0, keepdims=False)
        matrix = lax.all_gather(lax.all_gather(strip, "section", axis=0), ("y", "core"), axis=0)

        labels = regions[0, 0]
        labels = jnp.where(parity == core, labels, to_other_core(labels, range(sections)))
        labels = labels.reshape(2, 2, 2, half)
        labels = jnp.where(core == 0, labels, labels[::-1]).transpose(0, 2, 1, 3).reshape(-1)
        lk = labels[None, :]
        lq = labels[:quad * 2, None]

        even = chip % 2 == 0
        tokens = tokens[:, 0, 0]

        def first(flip):
            def route(s, w, d):
                return (s, (w // 2) * 2 + d // 2, chip_of(w % 2, d % 2 ^ flip))
            payload = jnp.where(even if flip == 0 else jnp.logical_not(even), tokens[0], tokens[1])
            return send(payload, route, (0,))

        near, far = first(0), first(1)
        band0 = jnp.where(micro == 0, near, far)
        band1 = jnp.where(micro == 0, far, near)
        own_a = jnp.concatenate([band0[:half], band1[:half]], axis=0)
        own_b = jnp.concatenate([band0[half:], band1[half:]], axis=0)

        def same(s, w, d):
            return (s + 1, w, d)

        def behind(s, w, d):
            window = (w // 2) * 2 + parity_of(d) - 1
            return (s + 1, (window % windows) // 2 * 2 + w % 2, chip_of(window % 2, d >> 1))

        for step in range(sections):
            far_a = to_other_core(own_a, (step,))
            far_b = to_other_core(own_b, (step,))
            out_a, out_b = layer(lq, lk, norm_gain, own_a, own_b, far_a, far_b, native, others)
            if step + 1 < sections:
                own_a = send(out_b, same, (step,))
                own_b = send(out_a, behind, (step,))
        last = sections - 1
        values = decode(final_gain[None, :], out_a, out_b, matrix)

        flipped = micro == 1

        def home(flip, shift):
            def route(s, w, d):
                window = (w // 2) * 2 + parity_of(d) - shift
                return (s, window % windows, 2 * (w % 2) + ((d >> 1) ^ flip))
            low = 0 if shift else quad
            pieces = values[:, low:low + half], values[:, low + half:low + quad]
            swap = flipped if flip == 0 else jnp.logical_not(flipped)
            return send(jnp.where(swap, pieces[1], pieces[0]), route, (last,))

        arrived = [[home(flip, shift) for shift in (0, 1)] for flip in (0, 1)]
        arrived = [jnp.concatenate(pair, axis=1) for pair in arrived]
        first_micro = jnp.where(even, arrived[0], arrived[1])
        second_micro = jnp.where(even, arrived[1], arrived[0])
        result = jnp.stack([first_micro, second_micro], axis=1)
        shown = result[last]
        for target in range(last):
            there = send(result[target], lambda s, w, d: (target, w, d), (last,))
            shown = jnp.where(section == target, there, shown)
        return shown[:, None, None]

    return jax.shard_map(
        body,
        mesh=fine,
        in_specs=(
            P(None, WIN, "dp", None, None),
            P("section", WIN, None),
            P("section", None),
            P("section", None, None, "dp"),
            P("section", "dp", None),
            P(),
            P(None, "section"),
        ),
        out_specs=P(None, WIN, "dp", None, "section"),
        check_vma=False,
    )
```

time: 447 us -> 261 us (0.58)
  waiting for transfers between devices: 262 us -> 83.7 us
  blocking collectives: 97.4 us -> 44.2 us
  local copies, waits for them, and re-layouts: 2.38 us -> 39.6 us
  matrix products: 35.9 us -> 0 us
  Pallas kernels: 0 us -> 34.2 us
  starting transfers between devices: 21.5 us -> 42.9 us
  other arithmetic: 13 us -> 2.21 us
    reduce_scatter x4 -> x0, waiting for transfers between devices: 190 us -> none  [body(): lax.psum_scatter(rounded(jnp.dot(blended, out_local, preferred_element_ty...]
    all_gather x4 -> x2, blocking collectives: 97.4 us -> 44.2 us  [the longest x1 33.3 us: body(): column = lax.all_gather(piece, 'dp', axis=0)]
    psum x1 -> x0, waiting for transfers between devices: 51 us -> none  [from_root(): return lax.psum(block, axis)]
    pallas_call x0 -> x4, Pallas kernels: none -> 34.2 us  [the longest x3 33.1 us: layer(): pl.pallas_call(layer_kernel, out_shape=(shape, shape), in_specs=[vmem] *...]
    ppermute x7 -> x19, waiting for transfers between devices: 20.8 us -> 54.2 us  [send(): return lax.ppermute(value, AXES, pairs)]
    dot_general x17 -> x0, matrix products: 31 us -> none  [the longest x4 9.22 us: attend(): jnp.einsum('hqk,khe->qhe', shares, values_all, preferred_element_type=jnp...]
    all_gather x0 -> x2, waiting for transfers between devices: none -> 29.5 us  [the longest x1 29.5 us: body(): others = lax.all_gather(rolled, ('y', 'core'), axis=0)]
    ppermute x7 -> x19, starting transfers between devices: 21.3 us -> 42.9 us  [send(): return lax.ppermute(value, AXES, pairs)]
  transfers between devices with their start and end apart: 12 -> 21, of which waited for: 12 -> 6; matrix products, arithmetic and copies ran while one was open for 0% -> 0% of each run, Pallas kernels for 0% -> 13%
where the time goes in v1:
time: 261 us
  waiting for transfers between devices  83.7 us (32%)
  blocking collectives  44.2 us (17%)
  starting transfers between devices  42.9 us (16%)
  local copies, waits for them, and re-layouts  39.6 us (15%)
  Pallas kernels  34.2 us (13%)
  between operations  14 us (5%)
    ppermute x19, waiting for transfers between devices, send(): return lax.ppermute(value, AXES, pairs)  54.2 us
    ppermute x19, starting transfers between devices, send(): return lax.ppermute(value, AXES, pairs)  42.9 us
    all_gather x1, blocking collectives, body(): column = lax.all_gather(piece, 'dp', axis=0)  33.3 us
    pallas_call x3, Pallas kernels, layer(): pl.pallas_call(layer_kernel, out_shape=(shape, shape), in_specs=[vmem] *...  33.1 us
    all_gather x1, waiting for transfers between devices, body(): others = lax.all_gather(rolled, ('y', 'core'), axis=0)  29.5 us
    another operation x2, local copies, waits for them, and re-layouts, body(): qkv_weight[0].reshape(16, depth // 16, width)  16.5 us
    unnamed x29, local copies, waits for them, and re-layouts  16 us
    all_gather x1, blocking collectives, body(): lax.all_gather(strip, 'section', axis=0)  10.8 us
  transfers between devices with their start and end apart: 21, of which 6 were waited for; matrix products, arithmetic and copies ran while one was open for 0% of the time, Pallas kernels for 13%

profile of v1, /device:TPU:1, one launch (start us, length us, event | category | flops | bytes accessed | tf_op | source)
XLA Modules:
  0.0 260.8 jit_solution(10721560604429241485)
XLA Ops:
  6.5 2.3 reshape_squeeze.8
  8.8 2.8 %fusion.10 = (bf16[16,16,1,768]{3,2,1,0:T(2,128)(2,1)}, bf16[16,16,1,768]{3,2,1,0:T(2,128)(2,1)}) fusion(bf16[16,16,2,768]{3,2,1,0:T(2,128)(2,1)S(1)} %reshape_squeeze.8), kind=kLoop, calls=%fused_computation.38 | loop fusion | bytes 1572864 | tf_op jit(solution)/shard_map/slice | solution.py:156
  11.6 12.0 %copy.42 = bf16[1,1536,3,256]{3,2,1,0:T(4,128)(2,1)S(1)} copy(bf16[1,1536,3,256]{3,1,2,0:T(8,128)(2,1)S(1)} %copy-done.9) | data formatting | bytes 4718592 | tf_op jit(solution)/shard_map/reshape;squeeze | solution.py:155
  23.6 4.6 %reshape.131 = bf16[16,96,768]{2,1,0:T(8,128)(2,1)} reshape(bf16[1,1536,3,256]{3,2,1,0:T(4,128)(2,1)S(1)} %copy.42) | data formatting | bytes 4718592 | tf_op jit(solution)/shard_map/reshape;squeeze | solution.py:155
  32.3 33.3 %all_gather.20 = bf16[4,128,768]{2,1,0:T(8,128)(2,1)S(1)} all-gather(bf16[1,128,768]{2,1,0:T(8,128)(2,1)S(1)} %constant_dynamic-slice_fusion.1), channel_id=1, replica_groups=mesh['section'=3,'x'=4,'y'=8,'core'=2,'dp'=4] {'dp'}, dimensions={0}, use_global_device_ids=true | all-gather | bytes 983040 | tf_op jit(solution)/shard_map/all_gather | solution.py:162
  67.5 10.8 %all_gather.23 = bf16[3,96,368]{2,1,0:T(8,128)(2,1)} all-gather(bf16[1,96,368]{2,1,0:T(8,128)(2,1)S(1)} %constant_dynamic-slice_fusion), channel_id=1, replica_groups=mesh['section'=3,'x'=4,'y'=8,'core'=2,'dp'=4] {'section'}, dimensions={0}, use_global_device_ids=true | all-gather | bytes 282624 | tf_op jit(solution)/shard_map/all_gather | solution.py:166
  78.4 5.6 %collective-permute-start = (s32[256]{0:T(256)S(1)}, s32[256]{0:T(256)S(1)}, u32[]{:S(2)}, u32[]{:S(2)}) collective-permute-start(s32[256]{0:T(256)S(1)} %bitcast.47), channel_id=1, source_target_pairs={{0,4},{1,5},{2,6},{3,7},{4,0},{5,1},{6,2},{7,3},{8,12},{9,13},{10,... | collective-permute-start | bytes 3080 | tf_op jit(solution)/shard_map/ppermute | solution.py:136
  84.0 5.6 %collective-permute-start.1 = (bf16[64,1536]{1,0:T(8,128)(2,1)S(1)}, bf16[64,1536]{1,0:T(8,128)(2,1)S(1)}, u32[]{:S(2)}, u32[]{:S(2)}) collective-permute-start(bf16[64,1536]{1,0:T(8,128)(2,1)S(1)} %get-tuple-element.21), channel_id=1, source_target_pairs={{0,0},{1,3},{2,4},{3,7},{4,1},{5,2},{6,5},{7,6},{8,8},{9,11},{10,1... | collective-permute-start | bytes 589832 | tf_op jit(solution)/shard_map/ppermute | solution.py:136
  89.6 6.3 %collective-permute-start.2 = (bf16[64,1536]{1,0:T(8,128)(2,1)S(1)}, bf16[64,1536]{1,0:T(8,128)(2,1)S(1)}, u32[]{:S(2)}, u32[]{:S(2)}) collective-permute-start(bf16[64,1536]{1,0:T(8,128)(2,1)S(1)} %get-tuple-element.22), channel_id=1, source_target_pairs={{0,3},{1,0},{2,7},{3,4},{4,2},{5,1},{6,6},{7,5},{8,11},{9,8},{10,1... | collective-permute-start | bytes 589832 | tf_op jit(solution)/shard_map/ppermute | solution.py:136
  97.3 2.3 collective-permute-done.2
  99.7 1.9 collective-permute-start.4
  101.7 2.4 collective-permute-start.3
  105.1 29.5 %all-gather.5.cloned.1.call-done = bf16[48,128,768]{2,1,0:T(8,128)(2,1)} async-done(((bf16[3,128,768]{2,1,0:T(8,128)(2,1)}), bf16[48,128,768]{2,1,0:T(8,128)(2,1)}) %all-gather.5.cloned.1.call-update) | async-done | bytes 9437200 | tf_op jit(solution)/shard_map/all_gather | solution.py:164
  134.7 3.7 %copy-done = bf16[48,128,768]{2,1,0:T(8,128)(2,1)S(1)} copy-done((bf16[48,128,768]{2,1,0:T(8,128)(2,1)S(1)}, bf16[48,128,768]{2,1,0:T(8,128)(2,1)}, u32[]{:S(2)}) %copy-start) | copy-done | bytes 9437208
  140.2 11.0 %layer.3 = (bf16[64,1536]{1,0:T(8,128)(2,1)S(1)}, bf16[64,1536]{1,0:T(8,128)(2,1)S(1)}) custom-call(s32[128,1]{1,0:T(8,128)S(1)} %broadcast_in_dim.12.lq, s32[1,256]{1,0:T(1,128)S(1)} %broadcast_in_dim_reshape.3.lk, f32[1,1536]{1,0:T(1,128)S(1)} %copy-done.7, bf16[64,1536]{1,0:T(8,128)(2,1)S(1)} %pad_maximum_fusion.1.own_a, ...), custom_call_target="tpu_custom_call" | custom-call | flops 2600000000 | bytes 14000000 | tf_op jit(solution)/shard_map/layer/pallas_call | solution.py:81
  151.3 3.3 %collective-permute-start.5 = (bf16[64,1536]{1,0:T(8,128)(2,1)S(1)}, bf16[64,1536]{1,0:T(8,128)(2,1)S(1)}, u32[]{:S(2)}, u32[]{:S(2)}) collective-permute-start(bf16[64,1536]{1,0:T(8,128)(2,1)S(1)} %get-tuple-element.11), channel_id=1, source_target_pairs={{0,256},{1,257},{2,258},{3,259},{4,260},{5,261},{6,262},{7,263},{8... | collective-permute-start | bytes 589832 | tf_op jit(solution)/shard_map/ppermute | solution.py:136
  154.6 8.8 %collective-permute-start.6 = (bf16[64,1536]{1,0:T(8,128)(2,1)S(1)}, bf16[64,1536]{1,0:T(8,128)(2,1)S(1)}, u32[]{:S(2)}, u32[]{:S(2)}) collective-permute-start(bf16[64,1536]{1,0:T(8,128)(2,1)S(1)} %get-tuple-element.12), channel_id=1, source_target_pairs={{0,505},{1,256},{2,259},{3,506},{4,509},{5,260},{6,263},{7,510},{8... | collective-permute-start | bytes 589832 | tf_op jit(solution)/shard_map/ppermute | solution.py:136
  164.0 3.3 %collective-permute-done.6.own_b = bf16[64,1536]{1,0:T(8,128)(2,1)S(1)} collective-permute-done((bf16[64,1536]{1,0:T(8,128)(2,1)S(1)}, bf16[64,1536]{1,0:T(8,128)(2,1)S(1)}, u32[]{:S(2)}, u32[]{:S(2)}) %collective-permute-start.6) | collective-permute-done | bytes 196640 | tf_op jit(solution)/shard_map/ppermute | solution.py:136
  168.3 11.0 %layer.4 = (bf16[64,1536]{1,0:T(8,128)(2,1)S(1)}, bf16[64,1536]{1,0:T(8,128)(2,1)S(1)}) custom-call(s32[128,1]{1,0:T(8,128)S(1)} %broadcast_in_dim.12.lq, s32[1,256]{1,0:T(1,128)S(1)} %broadcast_in_dim_reshape.3.lk, f32[1,1536]{1,0:T(1,128)S(1)} %copy-done.7, bf16[64,1536]{1,0:T(8,128)(2,1)S(1)} %collective-permute-done.5.own_a, ...), custom_call_target="tpu_custom_call" | custom-call | flops 2600000000 | bytes 14000000 | tf_op jit(solution)/shard_map/layer/pallas_call | solution.py:81
  182.3 3.7 %copy-done.2 = bf16[48,128,768]{2,1,0:T(8,128)(2,1)S(1)} copy-done((bf16[48,128,768]{2,1,0:T(8,128)(2,1)S(1)}, bf16[48,128,768]{2,1,0:T(8,128)(2,1)}, u32[]{:S(2)}) %copy-start.2) | copy-done | bytes 9437208
  186.0 1.9 copy-done.5
  187.9 11.0 %layer.5 = (bf16[64,1536]{1,0:T(8,128)(2,1)S(1)}, bf16[64,1536]{1,0:T(8,128)(2,1)S(1)}) custom-call(s32[128,1]{1,0:T(8,128)S(1)} %broadcast_in_dim.12.lq, s32[1,256]{1,0:T(1,128)S(1)} %broadcast_in_dim_reshape.3.lk, f32[1,1536]{1,0:T(1,128)S(1)} %copy-done.7, bf16[64,1536]{1,0:T(8,128)(2,1)S(1)} %collective-permute-done.9.own_a, ...), custom_call_target="tpu_custom_call" | custom-call | flops 2600000000 | bytes 14000000 | tf_op jit(solution)/shard_map/layer/pallas_call | solution.py:81
  199.0 2.0 copy-done.6
  207.0 46.4 %collective-permute-done.18 = bf16[2,64,368]{2,1,0:T(8,128)(2,1)S(1)} collective-permute-done((bf16[2,64,368]{2,1,0:T(8,128)(2,1)S(1)}, bf16[2,64,368]{2,1,0:T(8,128)(2,1)S(1)}, u32[]{:S(2)}, u32[]{:S(2)}) %collective-permute-start.18) | collective-permute-done | bytes 94240 | tf_op jit(solution)/shard_map/ppermute | solution.py:136
  (82 shorter events, 21.3 us)
Async XLA Ops:
  6.5 128.1 %all-gather.5.cloned.1.call-start = ((), (), s32[]{:S(2)}) async-start(), calls=%async_computation | async-start | bytes 10027008 | tf_op jit(solution)/shard_map/all_gather | solution.py:164
  30.6 47.8 %copy-start.13 = (s32[1,1,256]{2,1,0:T(1,128)S(1)}, s32[1,1,256]{2,1,0:T(1,128)}, u32[]{:S(2)}) copy-start(s32[1,1,256]{2,1,0:T(1,128)} %param.8) | copy-start | bytes 3076
  30.6 53.4 %copy-start.11 = (bf16[2,1,1,64,1536]{4,3,2,1,0:T(8,128)(2,1)S(1)}, bf16[2,1,1,64,1536]{4,3,2,1,0:T(8,128)(2,1)}, u32[]{:S(2)}) copy-start(bf16[2,1,1,64,1536]{4,3,2,1,0:T(8,128)(2,1)} %param.7) | copy-start | bytes 1179652
  66.7 68.0 %copy-start.7 = (f32[1,1536]{1,0:T(1,128)S(1)}, f32[1,1536]{1,0:T(1,128)}, u32[]{:S(2)}) copy-start(f32[1,1536]{1,0:T(1,128)} %gain.5) | copy-start | bytes 18436
  66.7 132.3 %all-gather.7.cloned.1.call-start = ((), (), s32[]{:S(2)}) async-start(), calls=%async_computation.1 | async-start | bytes 3760128 | tf_op jit(solution)/shard_map/all_gather | solution.py:166
  78.4 17.6 %collective-permute-start = (s32[256]{0:T(256)S(1)}, s32[256]{0:T(256)S(1)}, u32[]{:S(2)}, u32[]{:S(2)}) collective-permute-start(s32[256]{0:T(256)S(1)} %bitcast.47), channel_id=1, source_target_pairs={{0,4},{1,5},{2,6},{3,7},{4,0},{5,1},{6,2},{7,3},{8,12},{9,13},{10,... | collective-permute-start | bytes 3080 | tf_op jit(solution)/shard_map/ppermute | solution.py:136
  84.0 13.3 %collective-permute-start.1 = (bf16[64,1536]{1,0:T(8,128)(2,1)S(1)}, bf16[64,1536]{1,0:T(8,128)(2,1)S(1)}, u32[]{:S(2)}, u32[]{:S(2)}) collective-permute-start(bf16[64,1536]{1,0:T(8,128)(2,1)S(1)} %get-tuple-element.21), channel_id=1, source_target_pairs={{0,0},{1,3},{2,4},{3,7},{4,1},{5,2},{6,5},{7,6},{8,8},{9,11},{10,1... | collective-permute-start | bytes 589832 | tf_op jit(solution)/shard_map/ppermute | solution.py:136
  89.6 10.0 %collective-permute-start.2 = (bf16[64,1536]{1,0:T(8,128)(2,1)S(1)}, bf16[64,1536]{1,0:T(8,128)(2,1)S(1)}, u32[]{:S(2)}, u32[]{:S(2)}) collective-permute-start(bf16[64,1536]{1,0:T(8,128)(2,1)S(1)} %get-tuple-element.22), channel_id=1, source_target_pairs={{0,3},{1,0},{2,7},{3,4},{4,2},{5,1},{6,6},{7,5},{8,11},{9,8},{10,1... | collective-permute-start | bytes 589832 | tf_op jit(solution)/shard_map/ppermute | solution.py:136
  99.7 4.6 %collective-permute-start.4 = (bf16[64,1536]{1,0:T(8,128)(2,1)S(1)}, bf16[64,1536]{1,0:T(8,128)(2,1)S(1)}, u32[]{:S(2)}, u32[]{:S(2)}) collective-permute-start(bf16[64,1536]{1,0:T(8,128)(2,1)S(1)} %pad_maximum_fusion.2.own_b), channel_id=1, source_target_pairs={{0,4},{1,5},{2,6},{3,7},{4,0},{5,1},{6,2},{7,3},{8,12},{9,13},{10,... | collective-permute-start | bytes 589832 | tf_op jit(solution)/shard_map/ppermute | solution.py:136
  101.7 3.5 %collective-permute-start.3 = (bf16[64,1536]{1,0:T(8,128)(2,1)S(1)}, bf16[64,1536]{1,0:T(8,128)(2,1)S(1)}, u32[]{:S(2)}, u32[]{:S(2)}) collective-permute-start(bf16[64,1536]{1,0:T(8,128)(2,1)S(1)} %pad_maximum_fusion.1.own_a), channel_id=1, source_target_pairs={{0,4},{1,5},{2,6},{3,7},{4,0},{5,1},{6,2},{7,3},{8,12},{9,13},{10,... | collective-permute-start | bytes 589832 | tf_op jit(solution)/shard_map/ppermute | solution.py:136
  151.3 12.1 %collective-permute-start.5 = (bf16[64,1536]{1,0:T(8,128)(2,1)S(1)}, bf16[64,1536]{1,0:T(8,128)(2,1)S(1)}, u32[]{:S(2)}, u32[]{:S(2)}) collective-permute-start(bf16[64,1536]{1,0:T(8,128)(2,1)S(1)} %get-tuple-element.11), channel_id=1, source_target_pairs={{0,256},{1,257},{2,258},{3,259},{4,260},{5,261},{6,262},{7,263},{8... | collective-permute-start | bytes 589832 | tf_op jit(solution)/shard_map/ppermute | solution.py:136
  154.6 12.8 %collective-permute-start.6 = (bf16[64,1536]{1,0:T(8,128)(2,1)S(1)}, bf16[64,1536]{1,0:T(8,128)(2,1)S(1)}, u32[]{:S(2)}, u32[]{:S(2)}) collective-permute-start(bf16[64,1536]{1,0:T(8,128)(2,1)S(1)} %get-tuple-element.12), channel_id=1, source_target_pairs={{0,505},{1,256},{2,259},{3,506},{4,509},{5,260},{6,263},{7,510},{8... | collective-permute-start | bytes 589832 | tf_op jit(solution)/shard_map/ppermute | solution.py:136
  163.4 4.9 %collective-permute-start.7 = (bf16[64,1536]{1,0:T(8,128)(2,1)S(1)}, bf16[64,1536]{1,0:T(8,128)(2,1)S(1)}, u32[]{:S(2)}, u32[]{:S(2)}) collective-permute-start(bf16[64,1536]{1,0:T(8,128)(2,1)S(1)} %collective-permute-done.5.own_a), channel_id=1, source_target_pairs={{256,260},{257,261},{258,262},{259,263},{260,256},{261,257},{262,2... | collective-permute-start | bytes 589832 | tf_op jit(solution)/shard_map/ppermute | solution.py:136
  167.4 0.9 collective-permute-start.8
  179.3 1.4 collective-permute-start.9
  180.0 1.4 collective-permute-start.10
  180.7 1.6 collective-permute-start.11
  181.4 0.9 collective-permute-start.12
  202.1 2.7 %collective-permute-start.14 = (bf16[3,32,368]{2,1,0:T(8,128)(2,1)S(1)}, bf16[3,32,368]{2,1,0:T(8,128)(2,1)S(1)}, u32[]{:S(2)}, u32[]{:S(2)}) collective-permute-start(bf16[3,32,368]{2,1,0:T(8,128)(2,1)S(1)} %get-tuple-element.30), channel_id=1, source_target_pairs={{512,764},{513,512},{514,513},{515,765},{516,766},{517,514},{518,5... | collective-permute-start | bytes 211976 | tf_op jit(solution)/shard_map/ppermute | solution.py:136
  202.8 2.0 collective-permute-start.15
  203.5 1.4 collective-permute-start.16
  204.1 0.7 collective-permute-start.13
  205.0 2.0 collective-permute-start.17
  205.6 47.7 %collective-permute-start.18 = (bf16[2,64,368]{2,1,0:T(8,128)(2,1)S(1)}, bf16[2,64,368]{2,1,0:T(8,128)(2,1)S(1)}, u32[]{:S(2)}, u32[]{:S(2)}) collective-permute-start(bf16[2,64,368]{2,1,0:T(8,128)(2,1)S(1)} %get-tuple-element.23), channel_id=1, source_target_pairs={{512,0},{513,1},{514,2},{515,3},{516,4},{517,5},{518,6},{519,7},{5... | collective-permute-start | bytes 282632 | tf_op jit(solution)/shard_map/ppermute | solution.py:136
  (11 other events, 111.6 us)
Sparse Core Ops, SparseCore 0:
  66.8 67.8 all-gather.4
  137.1 45.7 all-gather.6

commit v2 on v1

--- a/solution.py
+++ b/solution.py
@@ -26,43 +26,43 @@
     return (center * lax.rsqrt(spread + 1e-05) * gain).astype(jnp.bfloat16)
 
 
-def layer_kernel(lq, lk, gain, own_a, own_b, far_a, far_b, native, others, out_a, out_b, held, normed, acc, sems):
-    quarters = held.shape[0]
-    slices, per, width = held.shape[1:]
+def layer_kernel(lq, lk, gain, own_a, own_b, far_a, far_b, native, others, out_a, out_b, normed, acc):
+    slices, per, width = native.shape
     inner = width // 3
+    heads = inner // HEAD
     rows = per * 3 // 4
     orows = per // 8
-    copies = [pltpu.make_async_copy(native, held.at[0], sems.at[0])]
-    for step in range(1, quarters):
-        copies.append(pltpu.make_async_copy(others.at[:, step - 1], held.at[step], sems.at[step]))
-    for copy in copies:
-        copy.start()
     part = own_a.shape[0]
     half = 2 * part
     for index, ref in enumerate((own_a, own_b, far_a, far_b)):
         normed[index * part:(index + 1) * part, :] = norm(ref[...].astype(jnp.float32), gain[...])
     allowed = lq[...] == lk[...]
-    for step in range(quarters):
-        copies[step].wait()
-        weight = held[step, :, :rows, :].reshape(slices * rows, width)
+    head_of = lax.broadcasted_iota(jnp.int32, (half, inner), 1) // HEAD
+    for step in range(others.shape[1] + 1):
+        def block(low, count):
+            value = native[:, low:low + count, :] if step == 0 else others[:, step - 1, low:low + count, :]
+            return value.reshape(slices * count, width)
+
+        weight = block(0, rows)
         keyval = jnp.dot(normed[...], weight[:, inner:], preferred_element_type=jnp.float32).astype(jnp.bfloat16)
-        query = jnp.dot(normed[:half, :], weight[:, :inner], preferred_element_type=jnp.float32).astype(jnp.bfloat16)
-        parts = []
-        for head in range(inner // HEAD):
-            at = head * HEAD
-            scores = lax.dot_general(
-                query[:, at:at + HEAD], keyval[:, at:at + HEAD],
-                (((1,), (1,)), ((), ())), preferred_element_type=jnp.float32,
-            ) * (HEAD ** -0.5)
-            scores = jnp.where(allowed, scores, -jnp.inf)
-            weights = jnp.exp(scores - jnp.max(scores, axis=-1, keepdims=True))
-            shares = (weights / jnp.sum(weights, axis=-1, keepdims=True)).astype(jnp.bfloat16)
-            parts.append(jnp.dot(shares, keyval[:, inner + at:inner + at + HEAD], preferred_element_type=jnp.float32))
-        blended = jnp.concatenate(parts, axis=-1).astype(jnp.bfloat16)
+        query = jnp.dot(normed[:half, :], weight[:, :inner], preferred_element_type=jnp.float32)
+        query = (query * (HEAD ** -0.5)).astype(jnp.bfloat16)
+        key, value = keyval[:, :inner], keyval[:, inner:]
+        stacked = jnp.concatenate(
+            [jnp.where(head_of == head, query, jnp.zeros_like(query)) for head in range(heads)], axis=0
+        )
+        scores = lax.dot_general(stacked, key, (((1,), (1,)), ((), ())), preferred_element_type=jnp.float32)
+        scores = jnp.where(jnp.concatenate([allowed] * heads, axis=0), scores, -jnp.inf)
+        weights = jnp.exp(scores - jnp.max(scores, axis=-1, keepdims=True))
+        total = jnp.sum(weights, axis=-1, keepdims=True)
+        mixed = jnp.dot(weights.astype(jnp.bfloat16), value, preferred_element_type=jnp.float32) / total
+        blended = mixed[:half]
+        for head in range(1, heads):
+            blended = jnp.where(head_of == head, mixed[head * half:(head + 1) * half], blended)
+        blended = blended.astype(jnp.bfloat16)
         for side in range(2):
-            low = rows + side * orows
-            matrix = held[step, :, low:low + orows, :].reshape(slices * orows, width)
-            update = jnp.dot(blended, matrix, preferred_element_type=jnp.float32).astype(jnp.bfloat16).astype(jnp.float32)
+            update = jnp.dot(blended, block(rows + side * orows, orows), preferred_element_type=jnp.float32)
+            update = update.astype(jnp.bfloat16).astype(jnp.float32)
             cols = slice(side * width, (side + 1) * width)
             if step == 0:
                 acc[:, cols] = update
@@ -74,22 +74,18 @@
 
 def layer(lq, lk, gain, own_a, own_b, far_a, far_b, native, others):
     part, depth = own_a.shape
-    quarters = others.shape[1] + 1
     vmem = pl.BlockSpec(memory_space=pltpu.VMEM)
-    hbm = pl.BlockSpec(memory_space=pl.ANY)
     shape = jax.ShapeDtypeStruct((part, depth), jnp.bfloat16)
     return pl.pallas_call(
         layer_kernel,
         out_shape=(shape, shape),
-        in_specs=[vmem] * 7 + [hbm] * 2,
+        in_specs=[vmem] * 9,
         out_specs=(vmem, vmem),
         scratch_shapes=[
-            pltpu.VMEM((quarters,) + native.shape, jnp.bfloat16),
             pltpu.VMEM((4 * part, depth), jnp.bfloat16),
             pltpu.VMEM((2 * part, depth), jnp.float32),
-            pltpu.SemaphoreType.DMA((quarters,)),
         ],
-        compiler_params=pltpu.CompilerParams(vmem_limit_bytes=40 << 20),
+        compiler_params=pltpu.CompilerParams(vmem_limit_bytes=14 << 20),
         cost_estimate=pl.CostEstimate(flops=2_600_000_000, bytes_accessed=14_000_000, transcendentals=524288),
         name="layer",
     )(lq, lk, gain, own_a, own_b, far_a, far_b, native, others)
@@ -150,19 +146,24 @@
         parity = (chip ^ (chip >> 1)) & 1
         width = qkv_weight.shape[2] * qkv_weight.shape[3]
 
-        native = jnp.concatenate(
-            [
-                qkv_weight[0].reshape(16, depth // 16, width),
-                out_weight[0].reshape(16, -1, 2, width)[:, :, 0],
-                out_weight[0].reshape(16, -1, 2, width)[:, :, 1],
-            ],
-            axis=1,
-        )
-        piece = lax.dynamic_index_in_dim(native, mine, 0, keepdims=False)
+        low = mine * (depth // 16)
+        orows = out_weight.shape[1] // 16
+
+        def slab(rows, outs):
+            return jnp.concatenate([rows, outs[..., :width], outs[..., width:]], axis=-2)
+
+        piece = slab(
+            lax.dynamic_slice_in_dim(qkv_weight[0], low, depth // 16, 0).reshape(-1, width),
+            lax.dynamic_slice_in_dim(out_weight[0], mine * orows, orows, 0),
+        )
         column = lax.all_gather(piece, "dp", axis=0)
         rolled = lax.dynamic_slice_in_dim(jnp.concatenate([column, column], axis=0), chip + 1, bands - 1, 0)
         others = lax.all_gather(rolled, ("y", "core"), axis=0)
-        strip = lax.dynamic_index_in_dim(dec_weight.reshape(16, depth // 16, -1), mine, 0, keepdims=False)
+        qkv_weight, out_weight, dec_weight, tokens, regions, _ = lax.optimization_barrier(
+            (qkv_weight, out_weight, dec_weight, tokens, regions, rolled)
+        )
+        native = slab(qkv_weight[0].reshape(16, depth // 16, width), out_weight[0].reshape(16, orows, 2 * width))
+        strip = lax.dynamic_slice_in_dim(dec_weight, low, depth // 16, 0)
         matrix = lax.all_gather(lax.all_gather(strip, "section", axis=0), ("y", "core"), axis=0)
 
         labels = regions[0, 0]
@@ -204,26 +205,27 @@
         last = sections - 1
         values = decode(final_gain[None, :], out_a, out_b, matrix)
 
+        values = values.reshape(sections, 2, 2, half, -1)
         flipped = micro == 1
 
-        def home(flip, shift):
+        def home(flip):
             def route(s, w, d):
-                window = (w // 2) * 2 + parity_of(d) - shift
-                return (s, window % windows, 2 * (w % 2) + ((d >> 1) ^ flip))
-            low = 0 if shift else quad
-            pieces = values[:, low:low + half], values[:, low + half:low + quad]
+                return (s, (w // 2) * 2 + parity_of(d), 2 * (w % 2) + ((d >> 1) ^ flip))
             swap = flipped if flip == 0 else jnp.logical_not(flipped)
-            return send(jnp.where(swap, pieces[1], pieces[0]), route, (last,))
-
-        arrived = [[home(flip, shift) for shift in (0, 1)] for flip in (0, 1)]
-        arrived = [jnp.concatenate(pair, axis=1) for pair in arrived]
-        first_micro = jnp.where(even, arrived[0], arrived[1])
-        second_micro = jnp.where(even, arrived[1], arrived[0])
-        result = jnp.stack([first_micro, second_micro], axis=1)
-        shown = result[last]
-        for target in range(last):
-            there = send(result[target], lambda s, w, d: (target, w, d), (last,))
-            shown = jnp.where(section == target, there, shown)
+            return send(jnp.where(swap, values[:, :, 1], values[:, :, 0]), route, (last,))
+
+        straight, crossed = home(0), home(1)
+        result = jnp.stack(
+            [jnp.where(even, straight, crossed), jnp.where(even, crossed, straight)], axis=1
+        )
+        shown = None
+        for target in range(sections):
+            ahead = send(result[target, :, 0], lambda s, w, d: (target, w - 1, d), (last,))
+            kept = result[target, :, 1]
+            if target != last:
+                kept = send(kept, lambda s, w, d: (target, w, d), (last,))
+            here = jnp.concatenate([kept, ahead], axis=1)
+            shown = here if shown is None else jnp.where(section == target, here, shown)
         return shown[:, None, None]
 
     return jax.shard_map(

time: 261 us -> 222 us (0.85); the launches traced: 261 us -> 218 us
  waiting for transfers between devices: 83.7 us -> 62.9 us
  local copies, waits for them, and re-layouts: 39.6 us -> 25.9 us
  Pallas kernels: 34.2 us -> 20.6 us
  other arithmetic: 2.21 us -> 6.81 us
    pallas_call x3, Pallas kernels: 33.1 us -> 19.5 us  [layer(): pl.pallas_call(layer_kernel, out_shape=(shape, shape), in_specs=[vmem] *...]
    ppermute x19 -> x20, waiting for transfers between devices: 54.2 us -> 42.4 us  [send(): return lax.ppermute(value, AXES, pairs)]
    all_gather x1, waiting for transfers between devices: 29.5 us -> 20.5 us  [body(): others = lax.all_gather(rolled, ('y', 'core'), axis=0)]
    another operation x2, local copies, waits for them, and re-layouts: 16.5 us -> 8.95 us  [body(): qkv_weight[0].reshape(16, depth // 16, width)]
    unnamed x29 -> x27, local copies, waits for them, and re-layouts: 16 us -> 12.7 us
    ppermute x19 -> x20, starting transfers between devices: 42.9 us -> 43.3 us  [send(): return lax.ppermute(value, AXES, pairs)]
  transfers between devices with their start and end apart: 21 -> 22, of which waited for: 6 -> 5; matrix products, arithmetic and copies ran while one was open for 0% -> 7% of each run, Pallas kernels for 13% -> 9%
where the time goes in v2:
time: 222 us; the launch traced here: 218 us
  waiting for transfers between devices  62.9 us (28%)
  blocking collectives  44.3 us (20%)
  starting transfers between devices  43.3 us (20%)
  local copies, waits for them, and re-layouts  25.9 us (12%)
  Pallas kernels  20.6 us (9%)
  between operations  13.9 us (6%)
  other arithmetic  6.81 us (3%)
    ppermute x20, starting transfers between devices, send(): return lax.ppermute(value, AXES, pairs)  43.3 us
    ppermute x20, waiting for transfers between devices, send(): return lax.ppermute(value, AXES, pairs)  42.4 us
    all_gather x1, blocking collectives, body(): column = lax.all_gather(piece, 'dp', axis=0)  33.5 us
    all_gather x1, waiting for transfers between devices, body(): others = lax.all_gather(rolled, ('y', 'core'), axis=0)  20.5 us
    pallas_call x3, Pallas kernels, layer(): pl.pallas_call(layer_kernel, out_shape=(shape, shape), in_specs=[vmem] *...  19.5 us
    unnamed x27, local copies, waits for them, and re-layouts  12.7 us
    all_gather x1, blocking collectives, body(): lax.all_gather(strip, 'section', axis=0)  10.8 us
    another operation x2, local copies, waits for them, and re-layouts, body(): qkv_weight[0].reshape(16, depth // 16, width)  8.95 us
  transfers between devices with their start and end apart: 22, of which 5 were waited for; matrix products, arithmetic and copies ran while one was open for 7% of the time, Pallas kernels for 9%

profile of v2, /device:TPU:1, one launch (start us, length us, event | category | flops | bytes accessed | tf_op | source)
XLA Modules:
  0.0 217.7 jit_solution(9603528271246572291)
XLA Ops:
  8.6 33.5 %all-gather = bf16[512,768]{1,0:T(8,128)(2,1)S(1)} all-gather(bf16[128,768]{1,0:T(8,128)(2,1)S(1)} %pad_maximum_fusion.1), channel_id=2, replica_groups=mesh['section'=3,'x'=4,'y'=8,'core'=2,'dp'=4] {'dp'}, dimensions={0}, use_global_device_ids=true | all-gather | bytes 983040 | tf_op jit(solution)/shard_map/all_gather | solution.py:159
  44.0 10.8 %all-gather.2 = bf16[288,368]{1,0:T(8,128)(2,1)} all-gather(bf16[96,368]{1,0:T(8,128)(2,1)S(1)} %constant_dynamic-slice_fusion), channel_id=4, replica_groups=mesh['section'=3,'x'=4,'y'=8,'core'=2,'dp'=4] {'section'}, dimensions={0}, use_global_device_ids=true | all-gather | bytes 282624 | tf_op jit(solution)/shard_map/all_gather | solution.py:167
  55.6 9.3 %collective-permute-start.1 = (bf16[64,1536]{1,0:T(8,128)(2,1)}, bf16[64,1536]{1,0:T(8,128)(2,1)S(1)}, u32[]{:S(2)}, u32[]{:S(2)}) collective-permute-start(bf16[64,1536]{1,0:T(8,128)(2,1)} %get-tuple-element.31), channel_id=1, source_target_pairs={{0,0},{1,3},{2,4},{3,7},{4,1},{5,2},{6,5},{7,6},{8,8},{9,11},{10,1... | collective-permute-start | bytes 589832 | tf_op jit(solution)/shard_map/ppermute | solution.py:132
  64.8 3.6 %collective-permute-start.2 = (bf16[64,1536]{1,0:T(8,128)(2,1)S(1)}, bf16[64,1536]{1,0:T(8,128)(2,1)}, u32[]{:S(2)}, u32[]{:S(2)}) collective-permute-start(bf16[64,1536]{1,0:T(8,128)(2,1)S(1)} %get-tuple-element.32), channel_id=1, source_target_pairs={{0,3},{1,0},{2,7},{3,4},{4,2},{5,1},{6,6},{7,5},{8,11},{9,8},{10,1... | collective-permute-start | bytes 589832 | tf_op jit(solution)/shard_map/ppermute | solution.py:132
  68.5 1.9 collective-permute-start
  70.4 4.3 %copy.49 = bf16[1,1536,3,256]{3,2,1,0:T(4,128)(2,1)S(1)} copy(bf16[1,1536,3,256]{3,1,2,0:T(8,128)(2,1)} %param.10) | data formatting | bytes 4718592 | tf_op jit(solution)/shard_map/reshape;squeeze | solution.py:165
  74.7 4.6 %reshape.119 = bf16[16,96,768]{2,1,0:T(8,128)(2,1)} reshape(bf16[1,1536,3,256]{3,2,1,0:T(4,128)(2,1)S(1)} %copy.49) | data formatting | bytes 4718592 | tf_op jit(solution)/shard_map/reshape;squeeze | solution.py:165
  80.6 1.9 pad_maximum_fusion.native
  84.3 1.9 collective-permute-start.4
  86.9 2.4 %collective-permute-start.3 = (bf16[64,1536]{1,0:T(8,128)(2,1)}, bf16[64,1536]{1,0:T(8,128)(2,1)}, u32[]{:S(2)}, u32[]{:S(2)}) collective-permute-start(bf16[64,1536]{1,0:T(8,128)(2,1)} %pad_maximum_fusion.2.own_a), channel_id=1, source_target_pairs={{0,4},{1,5},{2,6},{3,7},{4,0},{5,1},{6,2},{7,3},{8,12},{9,13},{10,... | collective-permute-start | bytes 589832 | tf_op jit(solution)/shard_map/ppermute | solution.py:132
  90.7 20.5 %all-gather.7.cloned.1.call-done = bf16[48,128,768]{2,1,0:T(8,128)(2,1)} async-done(((bf16[3,128,768]{2,1,0:T(8,128)(2,1)}), bf16[48,128,768]{2,1,0:T(8,128)(2,1)}) %all-gather.7.cloned.1.call-update) | async-done | bytes 9437200 | tf_op jit(solution)/shard_map/all_gather | solution.py:161
  111.1 3.7 %copy-done = bf16[48,128,768]{2,1,0:T(8,128)(2,1)S(1)} copy-done((bf16[48,128,768]{2,1,0:T(8,128)(2,1)S(1)}, bf16[48,128,768]{2,1,0:T(8,128)(2,1)}, u32[]{:S(2)}) %copy-start) | copy-done | bytes 9437208
  114.8 7.0 %layer.3 = (bf16[64,1536]{1,0:T(8,128)(2,1)S(1)}, bf16[64,1536]{1,0:T(8,128)(2,1)S(1)}) custom-call(s32[128,1]{1,0:T(8,128)S(1)} %broadcast_in_dim.9.lq, s32[1,256]{1,0:T(1,128)S(1)} %broadcast_in_dim_reshape.3.lk, f32[1,1536]{1,0:T(1,128)S(1)} %copy-done.8, bf16[64,1536]{1,0:T(8,128)(2,1)} %pad_maximum_fusion.2.own_a, ...), custom_call_target="tpu_custom_call" | custom-call | flops 2600000000 | bytes 14000000 | tf_op jit(solution)/shard_map/layer/pallas_call | solution.py:79
  121.8 3.3 %collective-permute-start.5 = (bf16[64,1536]{1,0:T(8,128)(2,1)S(1)}, bf16[64,1536]{1,0:T(8,128)(2,1)S(1)}, u32[]{:S(2)}, u32[]{:S(2)}) collective-permute-start(bf16[64,1536]{1,0:T(8,128)(2,1)S(1)} %get-tuple-element.20), channel_id=1, source_target_pairs={{0,256},{1,257},{2,258},{3,259},{4,260},{5,261},{6,262},{7,263},{8... | collective-permute-start | bytes 589832 | tf_op jit(solution)/shard_map/ppermute | solution.py:132
  125.1 8.8 %collective-permute-start.6 = (bf16[64,1536]{1,0:T(8,128)(2,1)S(1)}, bf16[64,1536]{1,0:T(8,128)(2,1)S(1)}, u32[]{:S(2)}, u32[]{:S(2)}) collective-permute-start(bf16[64,1536]{1,0:T(8,128)(2,1)S(1)} %get-tuple-element.21), channel_id=1, source_target_pairs={{0,505},{1,256},{2,259},{3,506},{4,509},{5,260},{6,263},{7,510},{8... | collective-permute-start | bytes 589832 | tf_op jit(solution)/shard_map/ppermute | solution.py:132
  134.6 3.3 %collective-permute-done.6.own_b = bf16[64,1536]{1,0:T(8,128)(2,1)S(1)} collective-permute-done((bf16[64,1536]{1,0:T(8,128)(2,1)S(1)}, bf16[64,1536]{1,0:T(8,128)(2,1)S(1)}, u32[]{:S(2)}, u32[]{:S(2)}) %collective-permute-start.6) | collective-permute-done | bytes 196640 | tf_op jit(solution)/shard_map/ppermute | solution.py:132
  138.8 5.7 %layer.4 = (bf16[64,1536]{1,0:T(8,128)(2,1)S(1)}, bf16[64,1536]{1,0:T(8,128)(2,1)S(1)}) custom-call(s32[128,1]{1,0:T(8,128)S(1)} %broadcast_in_dim.9.lq, s32[1,256]{1,0:T(1,128)S(1)} %broadcast_in_dim_reshape.3.lk, f32[1,1536]{1,0:T(1,128)S(1)} %copy-done.8, bf16[64,1536]{1,0:T(8,128)(2,1)S(1)} %collective-permute-done.5.own_a, ...), custom_call_target="tpu_custom_call" | custom-call | flops 2600000000 | bytes 14000000 | tf_op jit(solution)/shard_map/layer/pallas_call | solution.py:79
  145.2 1.3 collective-permute-start.10
  148.5 1.3 collective-permute-start.12
  149.9 3.8 %copy-done.2 = bf16[48,128,768]{2,1,0:T(8,128)(2,1)S(1)} copy-done((bf16[48,128,768]{2,1,0:T(8,128)(2,1)S(1)}, bf16[48,128,768]{2,1,0:T(8,128)(2,1)}, u32[]{:S(2)}) %copy-start.2) | copy-done | bytes 9437208
  154.6 6.8 %layer.5 = (bf16[64,1536]{1,0:T(8,128)(2,1)S(1)}, bf16[64,1536]{1,0:T(8,128)(2,1)S(1)}) custom-call(s32[128,1]{1,0:T(8,128)S(1)} %broadcast_in_dim.9.lq, s32[1,256]{1,0:T(1,128)S(1)} %broadcast_in_dim_reshape.3.lk, f32[1,1536]{1,0:T(1,128)S(1)} %copy-done.8, bf16[64,1536]{1,0:T(8,128)(2,1)S(1)} %copy-done.7, bf16[64,1536]{1,0:T(8,128)(2,1)} %collective-permute-done.10.own_b, ...), custom_call_target="tpu_custom_call" | custom-call | flops 2600000000 | bytes 14000000 | tf_op jit(solution)/shard_map/layer/pallas_call | solution.py:79
  162.1 2.0 copy-done.3
  172.3 34.8 %collective-permute-done.18 = bf16[2,32,368]{2,1,0:T(8,128)(2,1)S(1)} collective-permute-done((bf16[2,32,368]{2,1,0:T(8,128)(2,1)S(1)}, bf16[2,32,368]{2,1,0:T(8,128)(2,1)S(1)}, u32[]{:S(2)}, u32[]{:S(2)}) %collective-permute-start.18) | collective-permute-done | bytes 47136 | tf_op jit(solution)/shard_map/ppermute | solution.py:132
  207.1 3.0 %collective-permute-done.19 = bf16[2,32,368]{2,1,0:T(8,128)(2,1)S(1)} collective-permute-done((bf16[2,32,368]{2,1,0:T(8,128)(2,1)S(1)}, bf16[2,32,368]{2,1,0:T(8,128)(2,1)S(1)}, u32[]{:S(2)}, u32[]{:S(2)}) %collective-permute-start.19) | collective-permute-done | bytes 47136 | tf_op jit(solution)/shard_map/ppermute | solution.py:132
  (85 shorter events, 24.2 us)
Async XLA Ops:
  6.5 104.6 %all-gather.7.cloned.1.call-start = ((), (), s32[]{:S(2)}) async-start(), calls=%async_computation | async-start | bytes 10027008 | tf_op jit(solution)/shard_map/all_gather | solution.py:161
  8.5 46.3 %copy-start.10 = (bf16[2,1,1,64,1536]{4,3,2,1,0:T(8,128)(2,1)S(1)}, bf16[2,1,1,64,1536]{4,3,2,1,0:T(8,128)(2,1)}, u32[]{:S(2)}) copy-start(bf16[2,1,1,64,1536]{4,3,2,1,0:T(8,128)(2,1)} %param.7) | copy-start | bytes 1179652
  8.6 59.9 %copy-start.12 = (s32[1,1,256]{2,1,0:T(1,128)S(1)}, s32[1,1,256]{2,1,0:T(1,128)}, u32[]{:S(2)}) copy-start(s32[1,1,256]{2,1,0:T(1,128)} %param.8) | copy-start | bytes 3076
  43.1 119.0 %all-gather.9.cloned.1.call-start = ((), (), s32[]{:S(2)}) async-start(), calls=%async_computation.1 | async-start | bytes 3760128 | tf_op jit(solution)/shard_map/all_gather | solution.py:167
  55.6 27.7 %collective-permute-start.1 = (bf16[64,1536]{1,0:T(8,128)(2,1)}, bf16[64,1536]{1,0:T(8,128)(2,1)S(1)}, u32[]{:S(2)}, u32[]{:S(2)}) collective-permute-start(bf16[64,1536]{1,0:T(8,128)(2,1)} %get-tuple-element.31), channel_id=1, source_target_pairs={{0,0},{1,3},{2,4},{3,7},{4,1},{5,2},{6,5},{7,6},{8,8},{9,11},{10,1... | collective-permute-start | bytes 589832 | tf_op jit(solution)/shard_map/ppermute | solution.py:132
  64.8 18.4 %collective-permute-start.2 = (bf16[64,1536]{1,0:T(8,128)(2,1)S(1)}, bf16[64,1536]{1,0:T(8,128)(2,1)}, u32[]{:S(2)}, u32[]{:S(2)}) collective-permute-start(bf16[64,1536]{1,0:T(8,128)(2,1)S(1)} %get-tuple-element.32), channel_id=1, source_target_pairs={{0,3},{1,0},{2,7},{3,4},{4,2},{5,1},{6,6},{7,5},{8,11},{9,8},{10,1... | collective-permute-start | bytes 589832 | tf_op jit(solution)/shard_map/ppermute | solution.py:132
  68.5 14.0 %collective-permute-start = (s32[256]{0:T(256)S(1)}, s32[256]{0:T(256)}, u32[]{:S(2)}, u32[]{:S(2)}) collective-permute-start(s32[256]{0:T(256)S(1)} %bitcast.84), channel_id=1, source_target_pairs={{0,4},{1,5},{2,6},{3,7},{4,0},{5,1},{6,2},{7,3},{8,12},{9,13},{10,... | collective-permute-start | bytes 3080 | tf_op jit(solution)/shard_map/ppermute | solution.py:132
  84.3 5.3 %collective-permute-start.4 = (bf16[64,1536]{1,0:T(8,128)(2,1)S(1)}, bf16[64,1536]{1,0:T(8,128)(2,1)}, u32[]{:S(2)}, u32[]{:S(2)}) collective-permute-start(bf16[64,1536]{1,0:T(8,128)(2,1)S(1)} %pad_maximum_fusion.3.own_b), channel_id=1, source_target_pairs={{0,4},{1,5},{2,6},{3,7},{4,0},{5,1},{6,2},{7,3},{8,12},{9,13},{10,... | collective-permute-start | bytes 589832 | tf_op jit(solution)/shard_map/ppermute | solution.py:132
  86.9 3.8 %collective-permute-start.3 = (bf16[64,1536]{1,0:T(8,128)(2,1)}, bf16[64,1536]{1,0:T(8,128)(2,1)}, u32[]{:S(2)}, u32[]{:S(2)}) collective-permute-start(bf16[64,1536]{1,0:T(8,128)(2,1)} %pad_maximum_fusion.2.own_a), channel_id=1, source_target_pairs={{0,4},{1,5},{2,6},{3,7},{4,0},{5,1},{6,2},{7,3},{8,12},{9,13},{10,... | collective-permute-start | bytes 589832 | tf_op jit(solution)/shard_map/ppermute | solution.py:132
  121.8 12.1 %collective-permute-start.5 = (bf16[64,1536]{1,0:T(8,128)(2,1)S(1)}, bf16[64,1536]{1,0:T(8,128)(2,1)S(1)}, u32[]{:S(2)}, u32[]{:S(2)}) collective-permute-start(bf16[64,1536]{1,0:T(8,128)(2,1)S(1)} %get-tuple-element.20), channel_id=1, source_target_pairs={{0,256},{1,257},{2,258},{3,259},{4,260},{5,261},{6,262},{7,263},{8... | collective-permute-start | bytes 589832 | tf_op jit(solution)/shard_map/ppermute | solution.py:132
  125.1 12.8 %collective-permute-start.6 = (bf16[64,1536]{1,0:T(8,128)(2,1)S(1)}, bf16[64,1536]{1,0:T(8,128)(2,1)S(1)}, u32[]{:S(2)}, u32[]{:S(2)}) collective-permute-start(bf16[64,1536]{1,0:T(8,128)(2,1)S(1)} %get-tuple-element.21), channel_id=1, source_target_pairs={{0,505},{1,256},{2,259},{3,506},{4,509},{5,260},{6,263},{7,510},{8... | collective-permute-start | bytes 589832 | tf_op jit(solution)/shard_map/ppermute | solution.py:132
  133.9 4.9 %collective-permute-start.7 = (bf16[64,1536]{1,0:T(8,128)(2,1)S(1)}, bf16[64,1536]{1,0:T(8,128)(2,1)S(1)}, u32[]{:S(2)}, u32[]{:S(2)}) collective-permute-start(bf16[64,1536]{1,0:T(8,128)(2,1)S(1)} %collective-permute-done.5.own_a), channel_id=1, source_target_pairs={{256,260},{257,261},{258,262},{259,263},{260,256},{261,257},{262,2... | collective-permute-start | bytes 589832 | tf_op jit(solution)/shard_map/ppermute | solution.py:132
  137.9 0.9 collective-permute-start.8
  144.5 2.0 collective-permute-start.9
  145.2 3.3 %collective-permute-start.10 = (bf16[64,1536]{1,0:T(8,128)(2,1)S(1)}, bf16[64,1536]{1,0:T(8,128)(2,1)}, u32[]{:S(2)}, u32[]{:S(2)}) collective-permute-start(bf16[64,1536]{1,0:T(8,128)(2,1)S(1)} %get-tuple-element.23), channel_id=1, source_target_pairs={{256,761},{257,512},{258,515},{259,762},{260,765},{261,516},{262,5... | collective-permute-start | bytes 589832 | tf_op jit(solution)/shard_map/ppermute | solution.py:132
  146.5 3.3 %collective-permute-start.11 = (bf16[64,1536]{1,0:T(8,128)(2,1)S(1)}, bf16[64,1536]{1,0:T(8,128)(2,1)}, u32[]{:S(2)}, u32[]{:S(2)}) collective-permute-start(bf16[64,1536]{1,0:T(8,128)(2,1)S(1)} %collective-permute-done.9.own_a), channel_id=1, source_target_pairs={{512,516},{513,517},{514,518},{515,519},{516,512},{517,513},{518,5... | collective-permute-start | bytes 589832 | tf_op jit(solution)/shard_map/ppermute | solution.py:132
  148.5 1.4 collective-permute-start.12
  166.1 1.4 collective-permute-start.13
  166.8 0.7 collective-permute-start.14
  167.6 4.6 %collective-permute-start.15 = (bf16[2,32,368]{2,1,0:T(8,128)(2,1)S(1)}, bf16[2,32,368]{2,1,0:T(8,128)(2,1)S(1)}, u32[]{:S(2)}, u32[]{:S(2)}) collective-permute-start(bf16[2,32,368]{2,1,0:T(8,128)(2,1)S(1)} %get-tuple-element.35), channel_id=1, source_target_pairs={{512,764},{513,765},{514,766},{515,767},{516,512},{517,513},{518,5... | collective-permute-start | bytes 141320 | tf_op jit(solution)/shard_map/ppermute | solution.py:132
  168.3 4.0 %collective-permute-start.16 = (bf16[2,32,368]{2,1,0:T(8,128)(2,1)S(1)}, bf16[2,32,368]{2,1,0:T(8,128)(2,1)S(1)}, u32[]{:S(2)}, u32[]{:S(2)}) collective-permute-start(bf16[2,32,368]{2,1,0:T(8,128)(2,1)S(1)} %get-tuple-element.36), channel_id=1, source_target_pairs={{512,256},{513,257},{514,258},{515,259},{516,260},{517,261},{518,2... | collective-permute-start | bytes 141320 | tf_op jit(solution)/shard_map/ppermute | solution.py:132
  169.0 3.3 %collective-permute-start.17 = (bf16[2,32,368]{2,1,0:T(8,128)(2,1)S(1)}, bf16[2,32,368]{2,1,0:T(8,128)(2,1)S(1)}, u32[]{:S(2)}, u32[]{:S(2)}) collective-permute-start(bf16[2,32,368]{2,1,0:T(8,128)(2,1)S(1)} %get-tuple-element.37), channel_id=1, source_target_pairs={{512,508},{513,509},{514,510},{515,511},{516,256},{517,257},{518,2... | collective-permute-start | bytes 141320 | tf_op jit(solution)/shard_map/ppermute | solution.py:132
  169.6 37.5 %collective-permute-start.18 = (bf16[2,32,368]{2,1,0:T(8,128)(2,1)S(1)}, bf16[2,32,368]{2,1,0:T(8,128)(2,1)S(1)}, u32[]{:S(2)}, u32[]{:S(2)}) collective-permute-start(bf16[2,32,368]{2,1,0:T(8,128)(2,1)S(1)} %get-tuple-element.33), channel_id=1, source_target_pairs={{512,0},{513,1},{514,2},{515,3},{516,4},{517,5},{518,6},{519,7},{5... | collective-permute-start | bytes 141320 | tf_op jit(solution)/shard_map/ppermute | solution.py:132
  170.9 39.2 %collective-permute-start.19 = (bf16[2,32,368]{2,1,0:T(8,128)(2,1)S(1)}, bf16[2,32,368]{2,1,0:T(8,128)(2,1)S(1)}, u32[]{:S(2)}, u32[]{:S(2)}) collective-permute-start(bf16[2,32,368]{2,1,0:T(8,128)(2,1)S(1)} %get-tuple-element.38), channel_id=1, source_target_pairs={{512,252},{513,253},{514,254},{515,255},{516,0},{517,1},{518,2},{5... | collective-permute-start | bytes 141320 | tf_op jit(solution)/shard_map/ppermute | solution.py:132
  (11 other events, 128.6 us)
Sparse Core Ops, SparseCore 0:
  43.3 67.8 all-gather.6
  113.6 45.7 all-gather.8

commit v3 on v2

--- a/solution.py
+++ b/solution.py
@@ -156,15 +156,27 @@
             lax.dynamic_slice_in_dim(qkv_weight[0], low, depth // 16, 0).reshape(-1, width),
             lax.dynamic_slice_in_dim(out_weight[0], mine * orows, orows, 0),
         )
-        column = lax.all_gather(piece, "dp", axis=0)
-        rolled = lax.dynamic_slice_in_dim(jnp.concatenate([column, column], axis=0), chip + 1, bands - 1, 0)
+
+        def upward(value, sources):
+            routes = [
+                (lambda s, w, d, turn=turn: (s, w, (d - turn) % bands)) for turn in (bands - 1, 1, *range(2, bands - 1))
+            ]
+            got = [send(value, route, sources) for route in routes]
+            return jnp.stack([got[1], *got[2:], got[0]])
+
+        later = tuple(range(1, sections))
+        lead = upward(piece, (0,))
+        mark = lead[-1, :16, :128] + lead[0, :16, :128] + lead[1, :16, :128]
+        heard = jnp.zeros_like(mark)
+        for target in later:
+            heard += send(mark, lambda s, w, d: (target, w, d), (0,))
+        piece = jnp.where(heard[:1, :1] > 1e30, jnp.zeros_like(piece), piece)
+        rolled = jnp.where(section == 0, lead, upward(piece, later))
         others = lax.all_gather(rolled, ("y", "core"), axis=0)
         qkv_weight, out_weight, dec_weight, tokens, regions, _ = lax.optimization_barrier(
             (qkv_weight, out_weight, dec_weight, tokens, regions, rolled)
         )
         native = slab(qkv_weight[0].reshape(16, depth // 16, width), out_weight[0].reshape(16, orows, 2 * width))
-        strip = lax.dynamic_slice_in_dim(dec_weight, low, depth // 16, 0)
-        matrix = lax.all_gather(lax.all_gather(strip, "section", axis=0), ("y", "core"), axis=0)
 
         labels = regions[0, 0]
         labels = jnp.where(parity == core, labels, to_other_core(labels, range(sections)))
@@ -187,6 +199,10 @@
         band1 = jnp.where(micro == 0, far, near)
         own_a = jnp.concatenate([band0[:half], band1[:half]], axis=0)
         own_b = jnp.concatenate([band0[half:], band1[half:]], axis=0)
+
+        dec_weight, own_a, own_b = lax.optimization_barrier((dec_weight, own_a, own_b))
+        strip = lax.dynamic_slice_in_dim(dec_weight, low, depth // 16, 0)
+        matrix = lax.all_gather(lax.all_gather(strip, "section", axis=0), ("y", "core"), axis=0)
 
         def same(s, w, d):
             return (s + 1, w, d)

time: 222 us -> 253 us (1.14)
  the two profiles are of different devices: /device:TPU:1 before, /device:TPU:192 now
where the time goes in v3:
time: 253 us; the launch traced here: 252 us
  waiting for transfers between devices  116 us (46%)
  starting transfers between devices  57.7 us (23%)
  local copies, waits for them, and re-layouts  27 us (11%)
  Pallas kernels  20.6 us (8%)
  between operations  15.3 us (6%)
  blocking collectives  11.5 us (5%)
  other arithmetic  4.38 us (2%)
    ppermute x28, waiting for transfers between devices, send(): return lax.ppermute(value, AXES, pairs)  78.5 us
    ppermute x28, starting transfers between devices, send(): return lax.ppermute(value, AXES, pairs)  57.7 us
    all_gather x1, waiting for transfers between devices, body(): others = lax.all_gather(rolled, ('y', 'core'), axis=0)  33.6 us
    pallas_call x3, Pallas kernels, layer(): pl.pallas_call(layer_kernel, out_shape=(shape, shape), in_specs=[vmem] *...  19.5 us
    unnamed x27, local copies, waits for them, and re-layouts  12.7 us
    all_gather x1, blocking collectives, body(): lax.all_gather(strip, 'section', axis=0)  11.5 us
    another operation x2, local copies, waits for them, and re-layouts, body(): qkv_weight[0].reshape(16, depth // 16, width)  9.08 us
  transfers between devices with their start and end apart: 30, of which 12 were waited for; matrix products, arithmetic and copies ran while one was open for 6% of the time, Pallas kernels for 8%

profile of v3, /device:TPU:192, one launch (start us, length us, event | category | flops | bytes accessed | tf_op | source)
XLA Modules:
  0.0 252.3 jit_solution(14742212616497903955)
XLA Ops:
  8.5 9.2 %collective-permute-start.7 = (bf16[128,768]{1,0:T(8,128)(2,1)S(1)}, bf16[128,768]{1,0:T(8,128)(2,1)S(1)}, u32[]{:S(2)}, u32[]{:S(2)}) collective-permute-start(bf16[128,768]{1,0:T(8,128)(2,1)S(1)} %pad_maximum_fusion.3), channel_id=1, source_target_pairs={{0,1},{1,2},{2,3},{3,0},{4,5},{5,6},{6,7},{7,4},{8,9},{9,10},{10,1... | collective-permute-start | bytes 589832 | tf_op jit(solution)/shard_map/ppermute | solution.py:132
  17.8 6.6 %collective-permute-start.6 = (bf16[128,768]{1,0:T(8,128)(2,1)S(1)}, bf16[128,768]{1,0:T(8,128)(2,1)S(1)}, u32[]{:S(2)}, u32[]{:S(2)}) collective-permute-start(bf16[128,768]{1,0:T(8,128)(2,1)S(1)} %pad_maximum_fusion.3), channel_id=1, source_target_pairs={{0,2},{1,3},{2,0},{3,1},{4,6},{5,7},{6,4},{7,5},{8,10},{9,11},{10,... | collective-permute-start | bytes 589832 | tf_op jit(solution)/shard_map/ppermute | solution.py:132
  24.4 4.9 %collective-permute-start.5 = (bf16[128,768]{1,0:T(8,128)(2,1)S(1)}, bf16[128,768]{1,0:T(8,128)(2,1)S(1)}, u32[]{:S(2)}, u32[]{:S(2)}) collective-permute-start(bf16[128,768]{1,0:T(8,128)(2,1)S(1)} %pad_maximum_fusion.3), channel_id=1, source_target_pairs={{0,3},{1,0},{2,1},{3,2},{4,7},{5,4},{6,5},{7,6},{8,11},{9,8},{10,9... | collective-permute-start | bytes 589832 | tf_op jit(solution)/shard_map/ppermute | solution.py:132
  29.4 4.4 %collective-permute-done.6 = bf16[128,768]{1,0:T(8,128)(2,1)S(1)} collective-permute-done((bf16[128,768]{1,0:T(8,128)(2,1)S(1)}, bf16[128,768]{1,0:T(8,128)(2,1)S(1)}, u32[]{:S(2)}, u32[]{:S(2)}) %collective-permute-start.6) | collective-permute-done | bytes 196640 | tf_op jit(solution)/shard_map/ppermute | solution.py:132
  33.8 2.7 %collective-permute-done.5 = bf16[128,768]{1,0:T(8,128)(2,1)S(1)} collective-permute-done((bf16[128,768]{1,0:T(8,128)(2,1)S(1)}, bf16[128,768]{1,0:T(8,128)(2,1)S(1)}, u32[]{:S(2)}, u32[]{:S(2)}) %collective-permute-start.5) | collective-permute-done | bytes 196640 | tf_op jit(solution)/shard_map/ppermute | solution.py:132
  45.5 5.9 %collective-permute-start.1 = (bf16[64,1536]{1,0:T(8,128)(2,1)S(1)}, bf16[64,1536]{1,0:T(8,128)(2,1)S(1)}, u32[]{:S(2)}, u32[]{:S(2)}) collective-permute-start(bf16[64,1536]{1,0:T(8,128)(2,1)S(1)} %get-tuple-element.37), channel_id=1, source_target_pairs={{0,0},{1,3},{2,4},{3,7},{4,1},{5,2},{6,5},{7,6},{8,8},{9,11},{10,1... | collective-permute-start | bytes 589832 | tf_op jit(solution)/shard_map/ppermute | solution.py:132
  53.4 18.2 %collective-permute-done.1 = bf16[64,1536]{1,0:T(8,128)(2,1)S(1)} collective-permute-done((bf16[64,1536]{1,0:T(8,128)(2,1)S(1)}, bf16[64,1536]{1,0:T(8,128)(2,1)S(1)}, u32[]{:S(2)}, u32[]{:S(2)}) %collective-permute-start.1) | collective-permute-done | bytes 196640 | tf_op jit(solution)/shard_map/ppermute | solution.py:132
  71.6 2.1 collective-permute-done.2
  75.2 11.5 %all-gather = bf16[288,368]{1,0:T(8,128)(2,1)} all-gather(bf16[96,368]{1,0:T(8,128)(2,1)S(1)} %constant_dynamic-slice_fusion), channel_id=2, replica_groups=mesh['section'=3,'x'=4,'y'=8,'core'=2,'dp'=4] {'section'}, dimensions={0}, use_global_device_ids=true | all-gather | bytes 282624 | tf_op jit(solution)/shard_map/all_gather | solution.py:205
  88.7 4.5 %copy.50 = bf16[1,1536,3,256]{3,2,1,0:T(4,128)(2,1)S(1)} copy(bf16[1,1536,3,256]{3,1,2,0:T(8,128)(2,1)} %param.10) | data formatting | bytes 4718592 | tf_op jit(solution)/shard_map/reshape;squeeze | solution.py:179
  93.2 4.6 %reshape.206 = bf16[16,96,768]{2,1,0:T(8,128)(2,1)} reshape(bf16[1,1536,3,256]{3,2,1,0:T(4,128)(2,1)S(1)} %copy.50) | data formatting | bytes 4718592 | tf_op jit(solution)/shard_map/reshape;squeeze | solution.py:179
  100.9 2.4 collective-permute-start.3
  107.0 33.6 %all-gather.5.cloned.1.call-done.others = bf16[16,3,128,768]{3,2,1,0:T(8,128)(2,1)} async-done(((bf16[1,3,128,768]{3,2,1,0:T(8,128)(2,1)}), bf16[16,3,128,768]{3,2,1,0:T(8,128)(2,1)}) %all-gather.5.cloned.1.call-update) | async-done | bytes 9437200 | tf_op jit(solution)/shard_map/all_gather | solution.py:175
  140.5 3.7 %copy-done = bf16[16,3,128,768]{3,2,1,0:T(8,128)(2,1)S(1)} copy-done((bf16[16,3,128,768]{3,2,1,0:T(8,128)(2,1)S(1)}, bf16[16,3,128,768]{3,2,1,0:T(8,128)(2,1)}, u32[]{:S(2)}) %copy-start) | copy-done | bytes 9437208
  144.2 7.0 %layer.3 = (bf16[64,1536]{1,0:T(8,128)(2,1)S(1)}, bf16[64,1536]{1,0:T(8,128)(2,1)S(1)}) custom-call(s32[128,1]{1,0:T(8,128)S(1)} %broadcast_in_dim.25.lq, s32[1,256]{1,0:T(1,128)S(1)} %broadcast_in_dim_reshape.3.lk, f32[1,1536]{1,0:T(1,128)S(1)} %copy-done.8, bf16[64,1536]{1,0:T(8,128)(2,1)S(1)} %pad_maximum_fusion.1.own_a, ...), custom_call_target="tpu_custom_call" | custom-call | flops 2600000000 | bytes 14000000 | tf_op jit(solution)/shard_map/layer/pallas_call | solution.py:79
  151.2 4.8 %collective-permute-start.13 = (bf16[64,1536]{1,0:T(8,128)(2,1)S(1)}, bf16[64,1536]{1,0:T(8,128)(2,1)S(1)}, u32[]{:S(2)}, u32[]{:S(2)}) collective-permute-start(bf16[64,1536]{1,0:T(8,128)(2,1)S(1)} %get-tuple-element.26), channel_id=1, source_target_pairs={{0,256},{1,257},{2,258},{3,259},{4,260},{5,261},{6,262},{7,263},{8... | collective-permute-start | bytes 589832 | tf_op jit(solution)/shard_map/ppermute | solution.py:132
  157.3 3.2 %collective-permute-done.13.own_a = bf16[64,1536]{1,0:T(8,128)(2,1)S(1)} collective-permute-done((bf16[64,1536]{1,0:T(8,128)(2,1)S(1)}, bf16[64,1536]{1,0:T(8,128)(2,1)S(1)}, u32[]{:S(2)}, u32[]{:S(2)}) %collective-permute-start.13) | collective-permute-done | bytes 196640 | tf_op jit(solution)/shard_map/ppermute | solution.py:132
  162.7 5.7 %layer.4 = (bf16[64,1536]{1,0:T(8,128)(2,1)S(1)}, bf16[64,1536]{1,0:T(8,128)(2,1)S(1)}) custom-call(s32[128,1]{1,0:T(8,128)S(1)} %broadcast_in_dim.25.lq, s32[1,256]{1,0:T(1,128)S(1)} %broadcast_in_dim_reshape.3.lk, f32[1,1536]{1,0:T(1,128)S(1)} %copy-done.8, bf16[64,1536]{1,0:T(8,128)(2,1)S(1)} %collective-permute-done.13.own_a, ...), custom_call_target="tpu_custom_call" | custom-call | flops 2600000000 | bytes 14000000 | tf_op jit(solution)/shard_map/layer/pallas_call | solution.py:79
  173.2 3.7 %copy-done.2 = bf16[16,3,128,768]{3,2,1,0:T(8,128)(2,1)S(1)} copy-done((bf16[16,3,128,768]{3,2,1,0:T(8,128)(2,1)S(1)}, bf16[16,3,128,768]{3,2,1,0:T(8,128)(2,1)}, u32[]{:S(2)}) %copy-start.2) | copy-done | bytes 9437208
  176.9 6.8 %layer.5 = (bf16[64,1536]{1,0:T(8,128)(2,1)S(1)}, bf16[64,1536]{1,0:T(8,128)(2,1)S(1)}) custom-call(s32[128,1]{1,0:T(8,128)S(1)} %broadcast_in_dim.25.lq, s32[1,256]{1,0:T(1,128)S(1)} %broadcast_in_dim_reshape.3.lk, f32[1,1536]{1,0:T(1,128)S(1)} %copy-done.8, bf16[64,1536]{1,0:T(8,128)(2,1)S(1)} %collective-permute-done.17.own_a, ...), custom_call_target="tpu_custom_call" | custom-call | flops 2600000000 | bytes 14000000 | tf_op jit(solution)/shard_map/layer/pallas_call | solution.py:79
  185.1 3.7 %all-gather.7.cloned.1.call-done = bf16[48,96,368]{2,1,0:T(8,128)(2,1)} async-done(((bf16[3,96,368]{2,1,0:T(8,128)(2,1)}), bf16[48,96,368]{2,1,0:T(8,128)(2,1)}) %all-gather.7.cloned.1.call-update) | async-done | bytes 3391504 | tf_op jit(solution)/shard_map/all_gather | solution.py:205
  188.8 2.0 copy-done.3
  199.9 36.9 %collective-permute-done.27 = bf16[2,32,368]{2,1,0:T(8,128)(2,1)S(1)} collective-permute-done((bf16[2,32,368]{2,1,0:T(8,128)(2,1)S(1)}, bf16[2,32,368]{2,1,0:T(8,128)(2,1)S(1)}, u32[]{:S(2)}, u32[]{:S(2)}) %collective-permute-start.27) | collective-permute-done | bytes 47136 | tf_op jit(solution)/shard_map/ppermute | solution.py:132
  236.8 8.0 %collective-permute-done.26 = bf16[2,32,368]{2,1,0:T(8,128)(2,1)S(1)} collective-permute-done((bf16[2,32,368]{2,1,0:T(8,128)(2,1)S(1)}, bf16[2,32,368]{2,1,0:T(8,128)(2,1)S(1)}, u32[]{:S(2)}, u32[]{:S(2)}) %collective-permute-start.26) | collective-permute-done | bytes 47136 | tf_op jit(solution)/shard_map/ppermute | solution.py:132
  (104 shorter events, 40.7 us)
Async XLA Ops:
  6.5 134.0 %all-gather.5.cloned.1.call-start = ((), (), s32[]{:S(2)}) async-start(), calls=%async_computation | async-start | bytes 10027008 | tf_op jit(solution)/shard_map/all_gather | solution.py:175
  8.5 20.8 %collective-permute-start.7 = (bf16[128,768]{1,0:T(8,128)(2,1)S(1)}, bf16[128,768]{1,0:T(8,128)(2,1)S(1)}, u32[]{:S(2)}, u32[]{:S(2)}) collective-permute-start(bf16[128,768]{1,0:T(8,128)(2,1)S(1)} %pad_maximum_fusion.3), channel_id=1, source_target_pairs={{0,1},{1,2},{2,3},{3,0},{4,5},{5,6},{6,7},{7,4},{8,9},{9,10},{10,1... | collective-permute-start | bytes 589832 | tf_op jit(solution)/shard_map/ppermute | solution.py:132
  17.8 16.0 %collective-permute-start.6 = (bf16[128,768]{1,0:T(8,128)(2,1)S(1)}, bf16[128,768]{1,0:T(8,128)(2,1)S(1)}, u32[]{:S(2)}, u32[]{:S(2)}) collective-permute-start(bf16[128,768]{1,0:T(8,128)(2,1)S(1)} %pad_maximum_fusion.3), channel_id=1, source_target_pairs={{0,2},{1,3},{2,0},{3,1},{4,6},{5,7},{6,4},{7,5},{8,10},{9,11},{10,... | collective-permute-start | bytes 589832 | tf_op jit(solution)/shard_map/ppermute | solution.py:132
  24.4 12.1 %collective-permute-start.5 = (bf16[128,768]{1,0:T(8,128)(2,1)S(1)}, bf16[128,768]{1,0:T(8,128)(2,1)S(1)}, u32[]{:S(2)}, u32[]{:S(2)}) collective-permute-start(bf16[128,768]{1,0:T(8,128)(2,1)S(1)} %pad_maximum_fusion.3), channel_id=1, source_target_pairs={{0,3},{1,0},{2,1},{3,2},{4,7},{5,4},{6,5},{7,6},{8,11},{9,8},{10,9... | collective-permute-start | bytes 589832 | tf_op jit(solution)/shard_map/ppermute | solution.py:132
  36.6 2.6 %collective-permute-start.8 = (bf16[16,128]{1,0:T(8,128)(2,1)S(1)}, bf16[16,128]{1,0:T(8,128)(2,1)S(1)}, u32[]{:S(2)}, u32[]{:S(2)}) collective-permute-start(bf16[16,128]{1,0:T(8,128)(2,1)S(1)} %fusion.14), channel_id=1, source_target_pairs={{0,256},{1,257},{2,258},{3,259},{4,260},{5,261},{6,262},{7,263},{8... | collective-permute-start | bytes 12296 | tf_op jit(solution)/shard_map/ppermute | solution.py:132
  37.8 2.6 %collective-permute-start.9 = (bf16[16,128]{1,0:T(8,128)(2,1)S(1)}, bf16[16,128]{1,0:T(8,128)(2,1)S(1)}, u32[]{:S(2)}, u32[]{:S(2)}) collective-permute-start(bf16[16,128]{1,0:T(8,128)(2,1)S(1)} %fusion.14), channel_id=1, source_target_pairs={{0,512},{1,513},{2,514},{3,515},{4,516},{5,517},{6,518},{7,519},{8... | collective-permute-start | bytes 12296 | tf_op jit(solution)/shard_map/ppermute | solution.py:132
  42.4 2.1 collective-permute-start.12
  45.4 143.4 %all-gather.7.cloned.1.call-start = ((), (), s32[]{:S(2)}) async-start(), calls=%async_computation.1 | async-start | bytes 3760128 | tf_op jit(solution)/shard_map/all_gather | solution.py:205
  45.5 26.1 %collective-permute-start.1 = (bf16[64,1536]{1,0:T(8,128)(2,1)S(1)}, bf16[64,1536]{1,0:T(8,128)(2,1)S(1)}, u32[]{:S(2)}, u32[]{:S(2)}) collective-permute-start(bf16[64,1536]{1,0:T(8,128)(2,1)S(1)} %get-tuple-element.37), channel_id=1, source_target_pairs={{0,0},{1,3},{2,4},{3,7},{4,1},{5,2},{6,5},{7,6},{8,8},{9,11},{10,1... | collective-permute-start | bytes 589832 | tf_op jit(solution)/shard_map/ppermute | solution.py:132
  51.5 22.2 %collective-permute-start.2 = (bf16[64,1536]{1,0:T(8,128)(2,1)S(1)}, bf16[64,1536]{1,0:T(8,128)(2,1)S(1)}, u32[]{:S(2)}, u32[]{:S(2)}) collective-permute-start(bf16[64,1536]{1,0:T(8,128)(2,1)S(1)} %get-tuple-element.38), channel_id=1, source_target_pairs={{0,3},{1,0},{2,7},{3,4},{4,2},{5,1},{6,6},{7,5},{8,11},{9,8},{10,1... | collective-permute-start | bytes 589832 | tf_op jit(solution)/shard_map/ppermute | solution.py:132
  86.8 14.0 %collective-permute-start = (s32[256]{0:T(256)S(1)}, s32[256]{0:T(256)S(1)}, u32[]{:S(2)}, u32[]{:S(2)}) collective-permute-start(s32[256]{0:T(256)S(1)} %bitcast.100), channel_id=1, source_target_pairs={{0,4},{1,5},{2,6},{3,7},{4,0},{5,1},{6,2},{7,3},{8,12},{9,13},{10,... | collective-permute-start | bytes 3080 | tf_op jit(solution)/shard_map/ppermute | solution.py:132
  100.9 4.6 %collective-permute-start.3 = (bf16[64,1536]{1,0:T(8,128)(2,1)S(1)}, bf16[64,1536]{1,0:T(8,128)(2,1)}, u32[]{:S(2)}, u32[]{:S(2)}) collective-permute-start(bf16[64,1536]{1,0:T(8,128)(2,1)S(1)} %pad_maximum_fusion.1.own_a), channel_id=1, source_target_pairs={{0,4},{1,5},{2,6},{3,7},{4,0},{5,1},{6,2},{7,3},{8,12},{9,13},{10,... | collective-permute-start | bytes 589832 | tf_op jit(solution)/shard_map/ppermute | solution.py:132
  103.3 3.7 %collective-permute-start.4 = (bf16[64,1536]{1,0:T(8,128)(2,1)}, bf16[64,1536]{1,0:T(8,128)(2,1)}, u32[]{:S(2)}, u32[]{:S(2)}) collective-permute-start(bf16[64,1536]{1,0:T(8,128)(2,1)} %pad_maximum_fusion.2.own_b), channel_id=1, source_target_pairs={{0,4},{1,5},{2,6},{3,7},{4,0},{5,1},{6,2},{7,3},{8,12},{9,13},{10,... | collective-permute-start | bytes 589832 | tf_op jit(solution)/shard_map/ppermute | solution.py:132
  151.2 9.3 %collective-permute-start.13 = (bf16[64,1536]{1,0:T(8,128)(2,1)S(1)}, bf16[64,1536]{1,0:T(8,128)(2,1)S(1)}, u32[]{:S(2)}, u32[]{:S(2)}) collective-permute-start(bf16[64,1536]{1,0:T(8,128)(2,1)S(1)} %get-tuple-element.26), channel_id=1, source_target_pairs={{0,256},{1,257},{2,258},{3,259},{4,260},{5,261},{6,262},{7,263},{8... | collective-permute-start | bytes 589832 | tf_op jit(solution)/shard_map/ppermute | solution.py:132
  156.0 5.9 %collective-permute-start.14 = (bf16[64,1536]{1,0:T(8,128)(2,1)S(1)}, bf16[64,1536]{1,0:T(8,128)(2,1)S(1)}, u32[]{:S(2)}, u32[]{:S(2)}) collective-permute-start(bf16[64,1536]{1,0:T(8,128)(2,1)S(1)} %get-tuple-element.27), channel_id=1, source_target_pairs={{0,505},{1,256},{2,259},{3,506},{4,509},{5,260},{6,263},{7,510},{8... | collective-permute-start | bytes 589832 | tf_op jit(solution)/shard_map/ppermute | solution.py:132
  160.5 2.2 collective-permute-start.15
  168.5 2.0 collective-permute-start.17
  169.1 2.7 %collective-permute-start.18 = (bf16[64,1536]{1,0:T(8,128)(2,1)S(1)}, bf16[64,1536]{1,0:T(8,128)(2,1)}, u32[]{:S(2)}, u32[]{:S(2)}) collective-permute-start(bf16[64,1536]{1,0:T(8,128)(2,1)S(1)} %get-tuple-element.29), channel_id=1, source_target_pairs={{256,761},{257,512},{258,515},{259,762},{260,765},{261,516},{262,5... | collective-permute-start | bytes 589832 | tf_op jit(solution)/shard_map/ppermute | solution.py:132
  170.5 2.7 %collective-permute-start.19 = (bf16[64,1536]{1,0:T(8,128)(2,1)S(1)}, bf16[64,1536]{1,0:T(8,128)(2,1)}, u32[]{:S(2)}, u32[]{:S(2)}) collective-permute-start(bf16[64,1536]{1,0:T(8,128)(2,1)S(1)} %collective-permute-done.17.own_a), channel_id=1, source_target_pairs={{512,516},{513,517},{514,518},{515,519},{516,512},{517,513},{518,5... | collective-permute-start | bytes 589832 | tf_op jit(solution)/shard_map/ppermute | solution.py:132
  195.2 4.6 %collective-permute-start.23 = (bf16[2,32,368]{2,1,0:T(8,128)(2,1)S(1)}, bf16[2,32,368]{2,1,0:T(8,128)(2,1)S(1)}, u32[]{:S(2)}, u32[]{:S(2)}) collective-permute-start(bf16[2,32,368]{2,1,0:T(8,128)(2,1)S(1)} %get-tuple-element.41), channel_id=1, source_target_pairs={{512,764},{513,765},{514,766},{515,767},{516,512},{517,513},{518,5... | collective-permute-start | bytes 141320 | tf_op jit(solution)/shard_map/ppermute | solution.py:132
  195.9 4.0 %collective-permute-start.25 = (bf16[2,32,368]{2,1,0:T(8,128)(2,1)S(1)}, bf16[2,32,368]{2,1,0:T(8,128)(2,1)S(1)}, u32[]{:S(2)}, u32[]{:S(2)}) collective-permute-start(bf16[2,32,368]{2,1,0:T(8,128)(2,1)S(1)} %get-tuple-element.43), channel_id=1, source_target_pairs={{512,508},{513,509},{514,510},{515,511},{516,256},{517,257},{518,2... | collective-permute-start | bytes 141320 | tf_op jit(solution)/shard_map/ppermute | solution.py:132
  196.6 3.3 %collective-permute-start.24 = (bf16[2,32,368]{2,1,0:T(8,128)(2,1)S(1)}, bf16[2,32,368]{2,1,0:T(8,128)(2,1)S(1)}, u32[]{:S(2)}, u32[]{:S(2)}) collective-permute-start(bf16[2,32,368]{2,1,0:T(8,128)(2,1)S(1)} %get-tuple-element.42), channel_id=1, source_target_pairs={{512,256},{513,257},{514,258},{515,259},{516,260},{517,261},{518,2... | collective-permute-start | bytes 141320 | tf_op jit(solution)/shard_map/ppermute | solution.py:132
  197.3 39.5 %collective-permute-start.27 = (bf16[2,32,368]{2,1,0:T(8,128)(2,1)S(1)}, bf16[2,32,368]{2,1,0:T(8,128)(2,1)S(1)}, u32[]{:S(2)}, u32[]{:S(2)}) collective-permute-start(bf16[2,32,368]{2,1,0:T(8,128)(2,1)S(1)} %get-tuple-element.44), channel_id=1, source_target_pairs={{512,252},{513,253},{514,254},{515,255},{516,0},{517,1},{518,2},{5... | collective-permute-start | bytes 141320 | tf_op jit(solution)/shard_map/ppermute | solution.py:132
  198.6 46.2 %collective-permute-start.26 = (bf16[2,32,368]{2,1,0:T(8,128)(2,1)S(1)}, bf16[2,32,368]{2,1,0:T(8,128)(2,1)S(1)}, u32[]{:S(2)}, u32[]{:S(2)}) collective-permute-start(bf16[2,32,368]{2,1,0:T(8,128)(2,1)S(1)} %get-tuple-element.39), channel_id=1, source_target_pairs={{512,0},{513,1},{514,2},{515,3},{516,4},{517,5},{518,6},{519,7},{5... | collective-permute-start | bytes 141320 | tf_op jit(solution)/shard_map/ppermute | solution.py:132
  (19 other events, 242.5 us)
Sparse Core Ops, SparseCore 0:
  45.5 94.9 all-gather.4
  143.0 45.8 all-gather.6

commit v4 on v2

--- a/solution.py
+++ b/solution.py
@@ -1,3 +1,5 @@
+import functools
+
 import jax
 import jax.numpy as jnp
 import numpy as np
@@ -94,23 +96,58 @@
 def decode_kernel(gain, part_a, part_b, matrix, out):
     rows = jnp.concatenate([part_a[...], part_b[...]], axis=0).astype(jnp.float32)
     final = norm(rows, gain[...])
-    slices, sections, per, width = matrix.shape
-    for section in range(sections):
-        weight = matrix[:, section].reshape(slices * per, width)
-        out[section] = jnp.dot(final, weight, preferred_element_type=jnp.float32).astype(jnp.bfloat16)
+    for section in range(matrix.shape[0]):
+        out[section] = lax.dot_general(
+            final, matrix[section], (((1,), (1,)), ((), ())), preferred_element_type=jnp.float32
+        ).astype(jnp.bfloat16)
 
 
 def decode(gain, part_a, part_b, matrix):
     vmem = pl.BlockSpec(memory_space=pltpu.VMEM)
     return pl.pallas_call(
         decode_kernel,
-        out_shape=jax.ShapeDtypeStruct((matrix.shape[1], 2 * part_a.shape[0], matrix.shape[3]), jnp.bfloat16),
+        out_shape=jax.ShapeDtypeStruct((matrix.shape[0], 2 * part_a.shape[0], matrix.shape[1]), jnp.bfloat16),
         in_specs=[vmem] * 4,
         out_specs=vmem,
         compiler_params=pltpu.CompilerParams(vmem_limit_bytes=24 << 20),
         cost_estimate=pl.CostEstimate(flops=450_000_000, bytes_accessed=4_500_000, transcendentals=0),
         name="decode",
     )(gain, part_a, part_b, matrix)
+
+
+def gather_kernel(near_keys, far_keys, place, near, far, near_other, far_other, out, sems):
+    chunk = near.shape[2]
+    row, core = place[0], place[1]
+    copies = []
+    for keys, source, side in (
+        (near_keys, near, core), (near_keys, near_other, 1 - core), (far_keys, far, core), (far_keys, far_other, 1 - core)
+    ):
+        for index, (which, at) in enumerate(keys):
+            target = lax.rem(row + (at + 8), 8) * 2 + side
+            copies.append(
+                pltpu.make_async_copy(
+                    source.at[index], out.at[target, :, which * chunk:(which + 1) * chunk, :], sems.at[len(copies)]
+                )
+            )
+    for copy in copies:
+        copy.start()
+    for copy in copies:
+        copy.wait()
+
+
+def gather_blocks(near_keys, far_keys, place, *blocks):
+    _, turns, chunk, width = blocks[0].shape
+    hbm = pl.BlockSpec(memory_space=pl.ANY)
+    return pl.pallas_call(
+        functools.partial(gather_kernel, near_keys, far_keys),
+        out_shape=jax.ShapeDtypeStruct((16, turns, 2 * chunk, width), jnp.bfloat16),
+        in_specs=[pl.BlockSpec(memory_space=pltpu.SMEM)] + [hbm] * 4,
+        out_specs=pl.BlockSpec(memory_space=pltpu.VMEM),
+        scratch_shapes=[pltpu.SemaphoreType.DMA((2 * (len(near_keys) + len(far_keys)),))],
+        compiler_params=pltpu.CompilerParams(vmem_limit_bytes=14 << 20),
+        cost_estimate=pl.CostEstimate(flops=0, bytes_accessed=20_000_000, transcendentals=0),
+        name="gather_blocks",
+    )(place, *blocks)
 
 
 def solution(mesh):
@@ -152,19 +189,54 @@
         def slab(rows, outs):
             return jnp.concatenate([rows, outs[..., :width], outs[..., width:]], axis=-2)
 
+        across = windows // 16
         piece = slab(
             lax.dynamic_slice_in_dim(qkv_weight[0], low, depth // 16, 0).reshape(-1, width),
             lax.dynamic_slice_in_dim(out_weight[0], mine * orows, orows, 0),
         )
-        column = lax.all_gather(piece, "dp", axis=0)
+        share = piece.shape[0] // across
+        piece = lax.dynamic_slice_in_dim(piece, lax.axis_index("x") * share, share, 0)
+        column = lax.all_to_all(jnp.broadcast_to(piece, (bands,) + piece.shape), "dp", 0, 0)
         rolled = lax.dynamic_slice_in_dim(jnp.concatenate([column, column], axis=0), chip + 1, bands - 1, 0)
-        others = lax.all_gather(rolled, ("y", "core"), axis=0)
-        qkv_weight, out_weight, dec_weight, tokens, regions, _ = lax.optimization_barrier(
+        block = lax.all_to_all(jnp.broadcast_to(rolled, (across,) + rolled.shape), "x", 0, 0)
+        block = block.transpose(1, 0, 2, 3).reshape(bands - 1, across * share, width)
+        everywhere = range(sections)
+
+        def along(value, turn):
+            def route(s, w, d):
+                return (s, w // 16 * 16 + (w % 16 // 2 + turn) % 8 * 2 + w % 2, d)
+            return send(value, route, everywhere)
+
+        chunk = block.shape[1] // 2
+        near_blocks, far_blocks = [], []
+        held = [{0: block[:, :chunk]}, {0: block[:, chunk:]}]
+        for hop in range(1, 5):
+            for turn in (1, -1):
+                for which in range(2):
+                    if hop < 4 or (which == 0) == (turn == 1):
+                        held[which][-turn * hop] = along(held[which][-turn * (hop - 1)], turn)
+        near_keys = [(which, at) for which in range(2) for at in held[which] if abs(at) <= 2]
+        far_keys = [(which, at) for which in range(2) for at in held[which] if abs(at) > 2]
+        near_blocks = jnp.stack([held[which][at] for which, at in near_keys])
+        far_blocks = jnp.stack([held[which][at] for which, at in far_keys])
+        others = gather_blocks(
+            near_keys, far_keys, jnp.stack([lax.axis_index("y"), core]).astype(jnp.int32),
+            near_blocks, far_blocks, to_other_core(near_blocks, everywhere), to_other_core(far_blocks, everywhere),
+        )
+        qkv_weight, out_weight, dec_weight, tokens, regions, rolled = lax.optimization_barrier(
             (qkv_weight, out_weight, dec_weight, tokens, regions, rolled)
         )
         native = slab(qkv_weight[0].reshape(16, depth // 16, width), out_weight[0].reshape(16, orows, 2 * width))
-        strip = lax.dynamic_slice_in_dim(dec_weight, low, depth // 16, 0)
-        matrix = lax.all_gather(lax.all_gather(strip, "section", axis=0), ("y", "core"), axis=0)
+        last = sections - 1
+        turned = dec_weight.T
+        wide = turned.shape[0]
+        strip = lax.dynamic_slice_in_dim(turned, core * (wide // 2), wide // 2, 0)
+        strips = jnp.stack(
+            [send(strip, lambda s, w, d: (last, w, d), (source,)) for source in range(last)]
+        )
+        matched = to_other_core(strips, (last,))
+        strips = jnp.stack([jnp.where(core == 0, strips, matched), jnp.where(core == 0, matched, strips)], axis=1)
+        matrix = jnp.concatenate([strips.reshape(last, wide, depth), turned[None]], axis=0)
 
         labels = regions[0, 0]
         labels = jnp.where(parity == core, labels, to_other_core(labels, range(sections)))
@@ -202,7 +274,6 @@
             if step + 1 < sections:
                 own_a = send(out_b, same, (step,))
                 own_b = send(out_a, behind, (step,))
-        last = sections - 1
         values = decode(final_gain[None, :], out_a, out_b, matrix)
 
         values = values.reshape(sections, 2, 2, half, -1)

time: 222 us -> 261 us (1.18)
  starting transfers between devices: 43.3 us -> 112 us
  blocking collectives: 44.3 us -> 0 us
  between operations: 13.9 us -> 0.86 us
  waiting for transfers between devices: 62.9 us -> 72.3 us
  local copies, waits for them, and re-layouts: 25.9 us -> 35.1 us
  Pallas kernels: 20.6 us -> 26.8 us
    ppermute x20 -> x39, starting transfers between devices: 43.3 us -> 92.4 us  [send(): return lax.ppermute(value, AXES, pairs)]
    all_gather x2 -> x0, blocking collectives: 44.3 us -> none  [the longest x1 33.5 us: body(): column = lax.all_gather(piece, 'dp', axis=0)]
    all_gather x2 -> x0, waiting for transfers between devices: 20.5 us -> none  [the longest x1 20.5 us: body(): others = lax.all_gather(rolled, ('y', 'core'), axis=0)]
    ppermute x20 -> x39, waiting for transfers between devices: 42.4 us -> 62.2 us  [send(): return lax.ppermute(value, AXES, pairs)]
    all_to_all x0 -> x2, starting transfers between devices: none -> 19.2 us  [the longest x1 15 us: body(): lax.all_to_all(jnp.broadcast_to(piece, (bands,) + piece.shape), 'dp', 0, 0)]
    all_to_all x0 -> x2, waiting for transfers between devices: none -> 10.1 us  [the longest x1 10.1 us: body(): lax.all_to_all(jnp.broadcast_to(piece, (bands,) + piece.shape), 'dp', 0, 0)]
    pallas_call x0 -> x1, Pallas kernels: none -> 4.5 us  [gather_blocks(): pl.pallas_call(functools.partial(gather_kernel, near_keys, far_keys), out...]
    another operation x0 -> x4, other arithmetic: none -> 4.4 us  [the longest x1 2.4 us: body(): jnp.stack([send(strip, lambda s, w, d: (last, w, d), (source,)) for sourc...]
  transfers between devices with their start and end apart: 22 -> 41, of which waited for: 5 -> 7; matrix products, arithmetic and copies ran while one was open for 7% -> 14% of each run, Pallas kernels for 9% -> 5%
where the time goes in v4:
time: 261 us; the launch traced here: 256 us
  starting transfers between devices  112 us (43%)
  waiting for transfers between devices  72.3 us (28%)
  local copies, waits for them, and re-layouts  35.1 us (13%)
  Pallas kernels  26.8 us (10%)
  other arithmetic  9.16 us (4%)
    ppermute x39, starting transfers between devices, send(): return lax.ppermute(value, AXES, pairs)  92.4 us
    ppermute x39, waiting for transfers between devices, send(): return lax.ppermute(value, AXES, pairs)  62.2 us
    pallas_call x3, Pallas kernels, layer(): pl.pallas_call(layer_kernel, out_shape=(shape, shape), in_specs=[vmem] *...  20.9 us
    unnamed x47, local copies, waits for them, and re-layouts  16 us
    all_to_all x1, starting transfers between devices, body(): lax.all_to_all(jnp.broadcast_to(piece, (bands,) + piece.shape), 'dp', 0, 0)  15 us
    all_to_all x1, waiting for transfers between devices, body(): lax.all_to_all(jnp.broadcast_to(piece, (bands,) + piece.shape), 'dp', 0, 0)  10.1 us
    another operation x2, local copies, waits for them, and re-layouts, body(): qkv_weight[0].reshape(16, depth // 16, width)  8.93 us
  transfers between devices with their start and end apart: 41, of which 7 were waited for; matrix products, arithmetic and copies ran while one was open for 14% of the time, Pallas kernels for 5%

profile of v4, /device:TPU:1, one launch (start us, length us, event | category | flops | bytes accessed | tf_op | source)
XLA Modules:
  0.0 255.9 jit_solution(13231095434185866967)
XLA Ops:
  2.8 15.0 %all-to-all-start = ((bf16[4,32,768]{2,1,0:T(8,128)(2,1)}), bf16[4,32,768]{2,1,0:T(8,128)(2,1)S(1)}, u32[]{:S(2)}, u32[]{:S(2)}) async-start(bf16[4,32,768]{2,1,0:T(8,128)(2,1)} %broadcast_in_dim.17), calls=%async_computation | async-start | bytes 393216 | tf_op jit(solution)/shard_map/all_to_all | solution.py:199
  17.9 10.1 %all-to-all-done = bf16[4,32,768]{2,1,0:T(8,128)(2,1)S(1)} async-done(((bf16[4,32,768]{2,1,0:T(8,128)(2,1)}), bf16[4,32,768]{2,1,0:T(8,128)(2,1)S(1)}, u32[]{:S(2)}, u32[]{:S(2)}) %all-to-all-start) | async-done | bytes 196640 | tf_op jit(solution)/shard_map/all_to_all | solution.py:199
  28.9 4.1 %all-to-all-start.1 = ((bf16[4,3,32,768]{3,2,1,0:T(8,128)(2,1)}), bf16[4,3,32,768]{3,2,1,0:T(8,128)(2,1)}, u32[]{:S(2)}, u32[]{:S(2)}) async-start(bf16[4,3,32,768]{3,2,1,0:T(8,128)(2,1)} %broadcast_in_dim.19), calls=%async_computation.1 | async-start | bytes 1179648 | tf_op jit(solution)/shard_map/all_to_all | solution.py:201
  33.8 4.3 %copy.50 = bf16[1,1536,3,256]{3,2,1,0:T(4,128)(2,1)S(1)} copy(bf16[1,1536,3,256]{3,1,2,0:T(8,128)(2,1)} %param.10) | data formatting | bytes 4718592 | tf_op jit(solution)/shard_map/reshape;squeeze | solution.py:229
  38.2 4.6 %reshape.123 = bf16[16,96,768]{2,1,0:T(8,128)(2,1)} reshape(bf16[1,1536,3,256]{3,2,1,0:T(4,128)(2,1)S(1)} %copy.50) | data formatting | bytes 4718592 | tf_op jit(solution)/shard_map/reshape;squeeze | solution.py:229
  42.8 6.5 %collective-permute-start = (s32[256]{0:T(256)S(1)}, s32[256]{0:T(256)S(1)}, u32[]{:S(2)}, u32[]{:S(2)}) collective-permute-start(s32[256]{0:T(256)S(1)} %bitcast.131), channel_id=1, source_target_pairs={{0,4},{1,5},{2,6},{3,7},{4,0},{5,1},{6,2},{7,3},{8,12},{9,13},{10,... | collective-permute-start | bytes 3080 | tf_op jit(solution)/shard_map/ppermute | solution.py:169
  51.3 4.5 %collective-permute-start.29 = (bf16[184,1536]{1,0:T(8,128)(2,1)}, bf16[184,1536]{1,0:T(8,128)(2,1)}, u32[]{:S(2)}, u32[]{:S(2)}) collective-permute-start(bf16[184,1536]{1,0:T(8,128)(2,1)} %dynamic-slice_bitcast_fusion), channel_id=1, source_target_pairs={{0,512},{1,513},{2,514},{3,515},{4,516},{5,517},{6,518},{7,519},{8... | collective-permute-start | bytes 1695752 | tf_op jit(solution)/shard_map/ppermute | solution.py:169
  64.7 3.9 %collective-permute-start.6 = (bf16[3,64,768]{2,1,0:T(8,128)(2,1)}, bf16[3,64,768]{2,1,0:T(8,128)(2,1)S(1)}, u32[]{:S(2)}, u32[]{:S(2)}) collective-permute-start(bf16[3,64,768]{2,1,0:T(8,128)(2,1)} %get-tuple-element.32), channel_id=1, source_target_pairs={{0,56},{1,57},{2,58},{3,59},{4,60},{5,61},{6,62},{7,63},{8,0},{9,1... | collective-permute-start | bytes 884744 | tf_op jit(solution)/shard_map/ppermute | solution.py:169
  72.3 4.6 %collective-permute-start.10 = (bf16[3,64,768]{2,1,0:T(8,128)(2,1)}, bf16[3,64,768]{2,1,0:T(8,128)(2,1)S(1)}, u32[]{:S(2)}, u32[]{:S(2)}) collective-permute-start(bf16[3,64,768]{2,1,0:T(8,128)(2,1)} %get-tuple-element.31), channel_id=1, source_target_pairs={{0,56},{1,57},{2,58},{3,59},{4,60},{5,61},{6,62},{7,63},{8,0},{9,1... | collective-permute-start | bytes 884744 | tf_op jit(solution)/shard_map/ppermute | solution.py:169
  79.5 4.6 %collective-permute-start.8 = (bf16[3,64,768]{2,1,0:T(8,128)(2,1)S(1)}, bf16[3,64,768]{2,1,0:T(8,128)(2,1)S(1)}, u32[]{:S(2)}, u32[]{:S(2)}) collective-permute-start(bf16[3,64,768]{2,1,0:T(8,128)(2,1)S(1)} %collective-permute-done.6), channel_id=1, source_target_pairs={{0,56},{1,57},{2,58},{3,59},{4,60},{5,61},{6,62},{7,63},{8,0},{9,1... | collective-permute-start | bytes 884744 | tf_op jit(solution)/shard_map/ppermute | solution.py:169
  86.9 4.6 %collective-permute-start.12 = (bf16[3,64,768]{2,1,0:T(8,128)(2,1)S(1)}, bf16[3,64,768]{2,1,0:T(8,128)(2,1)S(1)}, u32[]{:S(2)}, u32[]{:S(2)}) collective-permute-start(bf16[3,64,768]{2,1,0:T(8,128)(2,1)S(1)} %collective-permute-done.10), channel_id=1, source_target_pairs={{0,56},{1,57},{2,58},{3,59},{4,60},{5,61},{6,62},{7,63},{8,0},{9,1... | collective-permute-start | bytes 884744 | tf_op jit(solution)/shard_map/ppermute | solution.py:169
  95.7 4.6 %collective-permute-start.14 = (bf16[3,64,768]{2,1,0:T(8,128)(2,1)S(1)}, bf16[3,64,768]{2,1,0:T(8,128)(2,1)S(1)}, u32[]{:S(2)}, u32[]{:S(2)}) collective-permute-start(bf16[3,64,768]{2,1,0:T(8,128)(2,1)S(1)} %collective-permute-done.8), channel_id=1, source_target_pairs={{0,56},{1,57},{2,58},{3,59},{4,60},{5,61},{6,62},{7,63},{8,0},{9,1... | collective-permute-start | bytes 884744 | tf_op jit(solution)/shard_map/ppermute | solution.py:169
  103.3 4.7 %collective-permute-start.19 = (bf16[10,3,64,768]{3,2,1,0:T(8,128)(2,1)}, bf16[10,3,64,768]{3,2,1,0:T(8,128)(2,1)}, u32[]{:S(2)}, u32[]{:S(2)}) collective-permute-start(bf16[10,3,64,768]{3,2,1,0:T(8,128)(2,1)} %bitcast_dynamic-update-slice_fusion.6.near), channel_id=1, source_target_pairs={{0,4},{1,5},{2,6},{3,7},{4,0},{5,1},{6,2},{7,3},{8,12},{9,13},{10,... | collective-permute-start | bytes 8847368 | tf_op jit(solution)/shard_map/ppermute | solution.py:169
  113.0 4.1 %collective-permute-start.17 = (bf16[3,64,768]{2,1,0:T(8,128)(2,1)S(1)}, bf16[3,64,768]{2,1,0:T(8,128)(2,1)S(1)}, u32[]{:S(2)}, u32[]{:S(2)}) collective-permute-start(bf16[3,64,768]{2,1,0:T(8,128)(2,1)S(1)} %collective-permute-done.12), channel_id=1, source_target_pairs={{0,56},{1,57},{2,58},{3,59},{4,60},{5,61},{6,62},{7,63},{8,0},{9,1... | collective-permute-start | bytes 884744 | tf_op jit(solution)/shard_map/ppermute | solution.py:169
  117.9 8.1 %collective-permute-done.15 = bf16[3,64,768]{2,1,0:T(8,128)(2,1)S(1)} collective-permute-done((bf16[3,64,768]{2,1,0:T(8,128)(2,1)S(1)}, bf16[3,64,768]{2,1,0:T(8,128)(2,1)S(1)}, u32[]{:S(2)}, u32[]{:S(2)}) %collective-permute-start.15) | collective-permute-done | bytes 294944 | tf_op jit(solution)/shard_map/ppermute | solution.py:169
  134.0 6.0 %collective-permute-done.18 = bf16[3,64,768]{2,1,0:T(8,128)(2,1)S(1)} collective-permute-done((bf16[3,64,768]{2,1,0:T(8,128)(2,1)S(1)}, bf16[3,64,768]{2,1,0:T(8,128)(2,1)S(1)}, u32[]{:S(2)}, u32[]{:S(2)}) %collective-permute-start.18) | collective-permute-done | bytes 294944 | tf_op jit(solution)/shard_map/ppermute | solution.py:169
  140.0 7.9 %collective-permute-start.2 = (bf16[64,1536]{1,0:T(8,128)(2,1)S(1)}, bf16[64,1536]{1,0:T(8,128)(2,1)S(1)}, u32[]{:S(2)}, u32[]{:S(2)}) collective-permute-start(bf16[64,1536]{1,0:T(8,128)(2,1)S(1)} %copy-done.9), channel_id=1, source_target_pairs={{0,3},{1,0},{2,7},{3,4},{4,2},{5,1},{6,6},{7,5},{8,11},{9,8},{10,1... | collective-permute-start | bytes 589832 | tf_op jit(solution)/shard_map/ppermute | solution.py:169
  160.1 4.5 %gather_blocks.1.others = bf16[16,3,128,768]{3,2,1,0:T(8,128)(2,1)S(1)} custom-call(s32[2]{0:T(128)S(1)} %pad_add_fusion.place, bf16[10,3,64,768]{3,2,1,0:T(8,128)(2,1)} %bitcast_dynamic-update-slice_fusion.6.near, bf16[6,3,64,768]{3,2,1,0:T(8,128)(2,1)} %bitcast_dynamic-update-slice_fusion.far, bf16[10,3,64,768]{3,2,1,0:T(8,128)(2,1)} %collective-permute-done.19.near_other, ...), custom_call_target="tpu_custom_call" | custom-call | bytes 20000000 | tf_op jit(solution)/shard_map/gather_blocks/pallas_call | solution.py:141
  164.7 8.3 %layer.3 = (bf16[64,1536]{1,0:T(8,128)(2,1)}, bf16[64,1536]{1,0:T(8,128)(2,1)}) custom-call(s32[128,1]{1,0:T(8,128)S(1)} %broadcast_in_dim.21.lq, s32[1,256]{1,0:T(1,128)S(1)} %broadcast_in_dim_reshape.3.lk, f32[1,1536]{1,0:T(1,128)S(1)} %copy-done.2, bf16[64,1536]{1,0:T(8,128)(2,1)} %pad_maximum_fusion.4.own_a, ...), custom_call_target="tpu_custom_call" | custom-call | flops 2600000000 | bytes 14000000 | tf_op jit(solution)/shard_map/layer/pallas_call | solution.py:81
  179.3 3.5 %collective-permute-done.22.own_b = bf16[64,1536]{1,0:T(8,128)(2,1)} collective-permute-done((bf16[64,1536]{1,0:T(8,128)(2,1)}, bf16[64,1536]{1,0:T(8,128)(2,1)}, u32[]{:S(2)}, u32[]{:S(2)}) %collective-permute-start.22) | collective-permute-done | bytes 196640 | tf_op jit(solution)/shard_map/ppermute | solution.py:169
  185.5 3.7 %copy-done.1 = bf16[16,3,128,768]{3,2,1,0:T(8,128)(2,1)S(1)} copy-done((bf16[16,3,128,768]{3,2,1,0:T(8,128)(2,1)S(1)}, bf16[16,3,128,768]{3,2,1,0:T(8,128)(2,1)}, u32[]{:S(2)}) %copy-start.1) | copy-done | bytes 9437208
  189.2 6.9 %layer.4 = (bf16[64,1536]{1,0:T(8,128)(2,1)S(1)}, bf16[64,1536]{1,0:T(8,128)(2,1)S(1)}) custom-call(s32[128,1]{1,0:T(8,128)S(1)} %broadcast_in_dim.21.lq, s32[1,256]{1,0:T(1,128)S(1)} %broadcast_in_dim_reshape.3.lk, f32[1,1536]{1,0:T(1,128)S(1)} %copy-done.2, bf16[64,1536]{1,0:T(8,128)(2,1)S(1)} %collective-permute-done.21.own_a, ...), custom_call_target="tpu_custom_call" | custom-call | flops 2600000000 | bytes 14000000 | tf_op jit(solution)/shard_map/layer/pallas_call | solution.py:81
  199.7 5.8 %layer.5 = (bf16[64,1536]{1,0:T(8,128)(2,1)S(1)}, bf16[64,1536]{1,0:T(8,128)(2,1)S(1)}) custom-call(s32[128,1]{1,0:T(8,128)S(1)} %broadcast_in_dim.21.lq, s32[1,256]{1,0:T(1,128)S(1)} %broadcast_in_dim_reshape.3.lk, f32[1,1536]{1,0:T(1,128)S(1)} %copy-done.2, bf16[64,1536]{1,0:T(8,128)(2,1)S(1)} %collective-permute-done.25.own_a, ...), custom_call_target="tpu_custom_call" | custom-call | flops 2600000000 | bytes 14000000 | tf_op jit(solution)/shard_map/layer/pallas_call | solution.py:81
  213.1 38.6 %collective-permute-done.37 = bf16[2,32,368]{2,1,0:T(8,128)(2,1)S(1)} collective-permute-done((bf16[2,32,368]{2,1,0:T(8,128)(2,1)S(1)}, bf16[2,32,368]{2,1,0:T(8,128)(2,1)S(1)}, u32[]{:S(2)}, u32[]{:S(2)}) %collective-permute-start.37) | collective-permute-done | bytes 47136 | tf_op jit(solution)/shard_map/ppermute | solution.py:169
  (152 shorter events, 81.4 us)
Async XLA Ops:
  2.8 25.2 %all-to-all-start = ((bf16[4,32,768]{2,1,0:T(8,128)(2,1)}), bf16[4,32,768]{2,1,0:T(8,128)(2,1)S(1)}, u32[]{:S(2)}, u32[]{:S(2)}) async-start(bf16[4,32,768]{2,1,0:T(8,128)(2,1)} %broadcast_in_dim.17), calls=%async_computation | async-start | bytes 393216 | tf_op jit(solution)/shard_map/all_to_all | solution.py:199
  28.9 29.7 %all-to-all-start.1 = ((bf16[4,3,32,768]{3,2,1,0:T(8,128)(2,1)}), bf16[4,3,32,768]{3,2,1,0:T(8,128)(2,1)}, u32[]{:S(2)}, u32[]{:S(2)}) async-start(bf16[4,3,32,768]{3,2,1,0:T(8,128)(2,1)} %broadcast_in_dim.19), calls=%async_computation.1 | async-start | bytes 1179648 | tf_op jit(solution)/shard_map/all_to_all | solution.py:201
  42.8 21.8 %collective-permute-start = (s32[256]{0:T(256)S(1)}, s32[256]{0:T(256)S(1)}, u32[]{:S(2)}, u32[]{:S(2)}) collective-permute-start(s32[256]{0:T(256)S(1)} %bitcast.131), channel_id=1, source_target_pairs={{0,4},{1,5},{2,6},{3,7},{4,0},{5,1},{6,2},{7,3},{8,12},{9,13},{10,... | collective-permute-start | bytes 3080 | tf_op jit(solution)/shard_map/ppermute | solution.py:169
  51.3 99.4 %collective-permute-start.29 = (bf16[184,1536]{1,0:T(8,128)(2,1)}, bf16[184,1536]{1,0:T(8,128)(2,1)}, u32[]{:S(2)}, u32[]{:S(2)}) collective-permute-start(bf16[184,1536]{1,0:T(8,128)(2,1)} %dynamic-slice_bitcast_fusion), channel_id=1, source_target_pairs={{0,512},{1,513},{2,514},{3,515},{4,516},{5,517},{6,518},{7,519},{8... | collective-permute-start | bytes 1695752 | tf_op jit(solution)/shard_map/ppermute | solution.py:169
  61.4 15.4 %collective-permute-start.5 = (bf16[3,64,768]{2,1,0:T(8,128)(2,1)}, bf16[3,64,768]{2,1,0:T(8,128)(2,1)S(1)}, u32[]{:S(2)}, u32[]{:S(2)}) collective-permute-start(bf16[3,64,768]{2,1,0:T(8,128)(2,1)} %get-tuple-element.32), channel_id=1, source_target_pairs={{0,8},{1,9},{2,10},{3,11},{4,12},{5,13},{6,14},{7,15},{8,16},{9,17... | collective-permute-start | bytes 884744 | tf_op jit(solution)/shard_map/ppermute | solution.py:169
  64.7 14.8 %collective-permute-start.6 = (bf16[3,64,768]{2,1,0:T(8,128)(2,1)}, bf16[3,64,768]{2,1,0:T(8,128)(2,1)S(1)}, u32[]{:S(2)}, u32[]{:S(2)}) collective-permute-start(bf16[3,64,768]{2,1,0:T(8,128)(2,1)} %get-tuple-element.32), channel_id=1, source_target_pairs={{0,56},{1,57},{2,58},{3,59},{4,60},{5,61},{6,62},{7,63},{8,0},{9,1... | collective-permute-start | bytes 884744 | tf_op jit(solution)/shard_map/ppermute | solution.py:169
  70.4 14.5 %collective-permute-start.9 = (bf16[3,64,768]{2,1,0:T(8,128)(2,1)}, bf16[3,64,768]{2,1,0:T(8,128)(2,1)S(1)}, u32[]{:S(2)}, u32[]{:S(2)}) collective-permute-start(bf16[3,64,768]{2,1,0:T(8,128)(2,1)} %get-tuple-element.31), channel_id=1, source_target_pairs={{0,8},{1,9},{2,10},{3,11},{4,12},{5,13},{6,14},{7,15},{8,16},{9,17... | collective-permute-start | bytes 884744 | tf_op jit(solution)/shard_map/ppermute | solution.py:169
  72.3 14.6 %collective-permute-start.10 = (bf16[3,64,768]{2,1,0:T(8,128)(2,1)}, bf16[3,64,768]{2,1,0:T(8,128)(2,1)S(1)}, u32[]{:S(2)}, u32[]{:S(2)}) collective-permute-start(bf16[3,64,768]{2,1,0:T(8,128)(2,1)} %get-tuple-element.31), channel_id=1, source_target_pairs={{0,56},{1,57},{2,58},{3,59},{4,60},{5,61},{6,62},{7,63},{8,0},{9,1... | collective-permute-start | bytes 884744 | tf_op jit(solution)/shard_map/ppermute | solution.py:169
  76.9 14.6 %collective-permute-start.7 = (bf16[3,64,768]{2,1,0:T(8,128)(2,1)S(1)}, bf16[3,64,768]{2,1,0:T(8,128)(2,1)S(1)}, u32[]{:S(2)}, u32[]{:S(2)}) collective-permute-start(bf16[3,64,768]{2,1,0:T(8,128)(2,1)S(1)} %collective-permute-done.5), channel_id=1, source_target_pairs={{0,8},{1,9},{2,10},{3,11},{4,12},{5,13},{6,14},{7,15},{8,16},{9,17... | collective-permute-start | bytes 884744 | tf_op jit(solution)/shard_map/ppermute | solution.py:169
  79.5 12.7 %collective-permute-start.8 = (bf16[3,64,768]{2,1,0:T(8,128)(2,1)S(1)}, bf16[3,64,768]{2,1,0:T(8,128)(2,1)S(1)}, u32[]{:S(2)}, u32[]{:S(2)}) collective-permute-start(bf16[3,64,768]{2,1,0:T(8,128)(2,1)S(1)} %collective-permute-done.6), channel_id=1, source_target_pairs={{0,56},{1,57},{2,58},{3,59},{4,60},{5,61},{6,62},{7,63},{8,0},{9,1... | collective-permute-start | bytes 884744 | tf_op jit(solution)/shard_map/ppermute | solution.py:169
  84.9 16.9 %collective-permute-start.11 = (bf16[3,64,768]{2,1,0:T(8,128)(2,1)S(1)}, bf16[3,64,768]{2,1,0:T(8,128)(2,1)S(1)}, u32[]{:S(2)}, u32[]{:S(2)}) collective-permute-start(bf16[3,64,768]{2,1,0:T(8,128)(2,1)S(1)} %collective-permute-done.9), channel_id=1, source_target_pairs={{0,8},{1,9},{2,10},{3,11},{4,12},{5,13},{6,14},{7,15},{8,16},{9,17... | collective-permute-start | bytes 884744 | tf_op jit(solution)/shard_map/ppermute | solution.py:169
  86.9 15.6 %collective-permute-start.12 = (bf16[3,64,768]{2,1,0:T(8,128)(2,1)S(1)}, bf16[3,64,768]{2,1,0:T(8,128)(2,1)S(1)}, u32[]{:S(2)}, u32[]{:S(2)}) collective-permute-start(bf16[3,64,768]{2,1,0:T(8,128)(2,1)S(1)} %collective-permute-done.10), channel_id=1, source_target_pairs={{0,56},{1,57},{2,58},{3,59},{4,60},{5,61},{6,62},{7,63},{8,0},{9,1... | collective-permute-start | bytes 884744 | tf_op jit(solution)/shard_map/ppermute | solution.py:169
  93.8 16.1 %collective-permute-start.13 = (bf16[3,64,768]{2,1,0:T(8,128)(2,1)S(1)}, bf16[3,64,768]{2,1,0:T(8,128)(2,1)S(1)}, u32[]{:S(2)}, u32[]{:S(2)}) collective-permute-start(bf16[3,64,768]{2,1,0:T(8,128)(2,1)S(1)} %collective-permute-done.7), channel_id=1, source_target_pairs={{0,8},{1,9},{2,10},{3,11},{4,12},{5,13},{6,14},{7,15},{8,16},{9,17... | collective-permute-start | bytes 884744 | tf_op jit(solution)/shard_map/ppermute | solution.py:169
  95.7 17.3 %collective-permute-start.14 = (bf16[3,64,768]{2,1,0:T(8,128)(2,1)S(1)}, bf16[3,64,768]{2,1,0:T(8,128)(2,1)S(1)}, u32[]{:S(2)}, u32[]{:S(2)}) collective-permute-start(bf16[3,64,768]{2,1,0:T(8,128)(2,1)S(1)} %collective-permute-done.8), channel_id=1, source_target_pairs={{0,56},{1,57},{2,58},{3,59},{4,60},{5,61},{6,62},{7,63},{8,0},{9,1... | collective-permute-start | bytes 884744 | tf_op jit(solution)/shard_map/ppermute | solution.py:169
  103.3 56.9 %collective-permute-start.19 = (bf16[10,3,64,768]{3,2,1,0:T(8,128)(2,1)}, bf16[10,3,64,768]{3,2,1,0:T(8,128)(2,1)}, u32[]{:S(2)}, u32[]{:S(2)}) collective-permute-start(bf16[10,3,64,768]{3,2,1,0:T(8,128)(2,1)} %bitcast_dynamic-update-slice_fusion.6.near), channel_id=1, source_target_pairs={{0,4},{1,5},{2,6},{3,7},{4,0},{5,1},{6,2},{7,3},{8,12},{9,13},{10,... | collective-permute-start | bytes 8847368 | tf_op jit(solution)/shard_map/ppermute | solution.py:169
  108.0 19.5 %collective-permute-start.16 = (bf16[3,64,768]{2,1,0:T(8,128)(2,1)S(1)}, bf16[3,64,768]{2,1,0:T(8,128)(2,1)S(1)}, u32[]{:S(2)}, u32[]{:S(2)}) collective-permute-start(bf16[3,64,768]{2,1,0:T(8,128)(2,1)S(1)} %collective-permute-done.11), channel_id=1, source_target_pairs={{0,8},{1,9},{2,10},{3,11},{4,12},{5,13},{6,14},{7,15},{8,16},{9,17... | collective-permute-start | bytes 884744 | tf_op jit(solution)/shard_map/ppermute | solution.py:169
  109.9 16.1 %collective-permute-start.15 = (bf16[3,64,768]{2,1,0:T(8,128)(2,1)S(1)}, bf16[3,64,768]{2,1,0:T(8,128)(2,1)S(1)}, u32[]{:S(2)}, u32[]{:S(2)}) collective-permute-start(bf16[3,64,768]{2,1,0:T(8,128)(2,1)S(1)} %collective-permute-done.13), channel_id=1, source_target_pairs={{0,8},{1,9},{2,10},{3,11},{4,12},{5,13},{6,14},{7,15},{8,16},{9,17... | collective-permute-start | bytes 884744 | tf_op jit(solution)/shard_map/ppermute | solution.py:169
  113.0 17.6 %collective-permute-start.17 = (bf16[3,64,768]{2,1,0:T(8,128)(2,1)S(1)}, bf16[3,64,768]{2,1,0:T(8,128)(2,1)S(1)}, u32[]{:S(2)}, u32[]{:S(2)}) collective-permute-start(bf16[3,64,768]{2,1,0:T(8,128)(2,1)S(1)} %collective-permute-done.12), channel_id=1, source_target_pairs={{0,56},{1,57},{2,58},{3,59},{4,60},{5,61},{6,62},{7,63},{8,0},{9,1... | collective-permute-start | bytes 884744 | tf_op jit(solution)/shard_map/ppermute | solution.py:169
  126.0 24.7 %collective-permute-start.30 = (bf16[184,1536]{1,0:T(8,128)(2,1)}, bf16[184,1536]{1,0:T(8,128)(2,1)S(1)}, u32[]{:S(2)}, u32[]{:S(2)}) collective-permute-start(bf16[184,1536]{1,0:T(8,128)(2,1)} %dynamic-slice_bitcast_fusion), channel_id=1, source_target_pairs={{256,512},{257,513},{258,514},{259,515},{260,516},{261,517},{262,5... | collective-permute-start | bytes 1695752 | tf_op jit(solution)/shard_map/ppermute | solution.py:169
  127.5 21.3 %collective-permute-start.1 = (bf16[64,1536]{1,0:T(8,128)(2,1)S(1)}, bf16[64,1536]{1,0:T(8,128)(2,1)S(1)}, u32[]{:S(2)}, u32[]{:S(2)}) collective-permute-start(bf16[64,1536]{1,0:T(8,128)(2,1)S(1)} %copy-done.10), channel_id=1, source_target_pairs={{0,0},{1,3},{2,4},{3,7},{4,1},{5,2},{6,5},{7,6},{8,8},{9,11},{10,1... | collective-permute-start | bytes 589832 | tf_op jit(solution)/shard_map/ppermute | solution.py:169
  148.7 11.4 %collective-permute-start.20 = (bf16[6,3,64,768]{3,2,1,0:T(8,128)(2,1)}, bf16[6,3,64,768]{3,2,1,0:T(8,128)(2,1)}, u32[]{:S(2)}, u32[]{:S(2)}) collective-permute-start(bf16[6,3,64,768]{3,2,1,0:T(8,128)(2,1)} %bitcast_dynamic-update-slice_fusion.far), channel_id=1, source_target_pairs={{0,4},{1,5},{2,6},{3,7},{4,0},{5,1},{6,2},{7,3},{8,12},{9,13},{10,... | collective-permute-start | bytes 5308424 | tf_op jit(solution)/shard_map/ppermute | solution.py:169
  153.1 30.6 %collective-permute-start.31 = (bf16[2,184,1536]{2,1,0:T(8,128)(2,1)}, bf16[2,184,1536]{2,1,0:T(8,128)(2,1)}, u32[]{:S(2)}, u32[]{:S(2)}) collective-permute-start(bf16[2,184,1536]{2,1,0:T(8,128)(2,1)} %pad_maximum_fusion.3), channel_id=1, source_target_pairs={{512,516},{513,517},{514,518},{515,519},{516,512},{517,513},{518,5... | collective-permute-start | bytes 3391496 | tf_op jit(solution)/shard_map/ppermute | solution.py:169
  210.4 41.3 %collective-permute-start.37 = (bf16[2,32,368]{2,1,0:T(8,128)(2,1)S(1)}, bf16[2,32,368]{2,1,0:T(8,128)(2,1)S(1)}, u32[]{:S(2)}, u32[]{:S(2)}) collective-permute-start(bf16[2,32,368]{2,1,0:T(8,128)(2,1)S(1)} %get-tuple-element.37), channel_id=1, source_target_pairs={{512,0},{513,1},{514,2},{515,3},{516,4},{517,5},{518,6},{519,7},{5... | collective-permute-start | bytes 141320 | tf_op jit(solution)/shard_map/ppermute | solution.py:169
  211.7 43.4 %collective-permute-start.38 = (bf16[2,32,368]{2,1,0:T(8,128)(2,1)S(1)}, bf16[2,32,368]{2,1,0:T(8,128)(2,1)S(1)}, u32[]{:S(2)}, u32[]{:S(2)}) collective-permute-start(bf16[2,32,368]{2,1,0:T(8,128)(2,1)S(1)} %get-tuple-element.42), channel_id=1, source_target_pairs={{512,252},{513,253},{514,254},{515,255},{516,0},{517,1},{518,2},{5... | collective-permute-start | bytes 141320 | tf_op jit(solution)/shard_map/ppermute | solution.py:169
  (33 other events, 301.5 us)

commit v5 on v2

--- a/solution.py
+++ b/solution.py
@@ -26,22 +26,28 @@
     return (center * lax.rsqrt(spread + 1e-05) * gain).astype(jnp.bfloat16)
 
 
-def layer_kernel(lq, lk, gain, own_a, own_b, far_a, far_b, native, others, out_a, out_b, normed, acc):
-    slices, per, width = native.shape
+def layer_kernel(lq, lk, gain, own_a, own_b, far_a, far_b, native, others, out_a, out_b, held, normed, acc, sems):
+    quarters, slices, per, width = held.shape
     inner = width // 3
     heads = inner // HEAD
     rows = per * 3 // 4
     orows = per // 8
     part = own_a.shape[0]
     half = 2 * part
+    copies = []
+    for step in range(quarters):
+        source = native if step == 0 else others.at[:, step - 1]
+        copies.append(pltpu.make_async_copy(source, held.at[step], sems.at[step]))
+        copies[-1].start()
     for index, ref in enumerate((own_a, own_b, far_a, far_b)):
         normed[index * part:(index + 1) * part, :] = norm(ref[...].astype(jnp.float32), gain[...])
     allowed = lq[...] == lk[...]
     head_of = lax.broadcasted_iota(jnp.int32, (half, inner), 1) // HEAD
-    for step in range(others.shape[1] + 1):
+    for step in range(quarters):
+        copies[step].wait()
+
         def block(low, count):
-            value = native[:, low:low + count, :] if step == 0 else others[:, step - 1, low:low + count, :]
-            return value.reshape(slices * count, width)
+            return held[step, :, low:low + count, :].reshape(slices * count, width)
 
         weight = block(0, rows)
         keyval = jnp.dot(normed[...], weight[:, inner:], preferred_element_type=jnp.float32).astype(jnp.bfloat16)
@@ -74,18 +80,22 @@
 
 def layer(lq, lk, gain, own_a, own_b, far_a, far_b, native, others):
     part, depth = own_a.shape
+    quarters = others.shape[1] + 1
     vmem = pl.BlockSpec(memory_space=pltpu.VMEM)
+    hbm = pl.BlockSpec(memory_space=pl.ANY)
     shape = jax.ShapeDtypeStruct((part, depth), jnp.bfloat16)
     return pl.pallas_call(
         layer_kernel,
         out_shape=(shape, shape),
-        in_specs=[vmem] * 9,
+        in_specs=[vmem] * 7 + [hbm] * 2,
         out_specs=(vmem, vmem),
         scratch_shapes=[
+            pltpu.VMEM((quarters,) + native.shape, jnp.bfloat16),
             pltpu.VMEM((4 * part, depth), jnp.bfloat16),
             pltpu.VMEM((2 * part, depth), jnp.float32),
+            pltpu.SemaphoreType.DMA((quarters,)),
         ],
-        compiler_params=pltpu.CompilerParams(vmem_limit_bytes=14 << 20),
+        compiler_params=pltpu.CompilerParams(vmem_limit_bytes=48 << 20),
         cost_estimate=pl.CostEstimate(flops=2_600_000_000, bytes_accessed=14_000_000, transcendentals=524288),
         name="layer",
     )(lq, lk, gain, own_a, own_b, far_a, far_b, native, others)
@@ -94,17 +104,17 @@
 def decode_kernel(gain, part_a, part_b, matrix, out):
     rows = jnp.concatenate([part_a[...], part_b[...]], axis=0).astype(jnp.float32)
     final = norm(rows, gain[...])
-    slices, sections, per, width = matrix.shape
-    for section in range(sections):
-        weight = matrix[:, section].reshape(slices * per, width)
-        out[section] = jnp.dot(final, weight, preferred_element_type=jnp.float32).astype(jnp.bfloat16)
+    for section in range(matrix.shape[0]):
+        out[section] = lax.dot_general(
+            final, matrix[section], (((1,), (1,)), ((), ())), preferred_element_type=jnp.float32
+        ).astype(jnp.bfloat16)
 
 
 def decode(gain, part_a, part_b, matrix):
     vmem = pl.BlockSpec(memory_space=pltpu.VMEM)
     return pl.pallas_call(
         decode_kernel,
-        out_shape=jax.ShapeDtypeStruct((matrix.shape[1], 2 * part_a.shape[0], matrix.shape[3]), jnp.bfloat16),
+        out_shape=jax.ShapeDtypeStruct((matrix.shape[0], 2 * part_a.shape[0], matrix.shape[1]), jnp.bfloat16),
         in_specs=[vmem] * 4,
         out_specs=vmem,
         compiler_params=pltpu.CompilerParams(vmem_limit_bytes=24 << 20),
@@ -163,8 +173,16 @@
             (qkv_weight, out_weight, dec_weight, tokens, regions, rolled)
         )
         native = slab(qkv_weight[0].reshape(16, depth // 16, width), out_weight[0].reshape(16, orows, 2 * width))
-        strip = lax.dynamic_slice_in_dim(dec_weight, low, depth // 16, 0)
-        matrix = lax.all_gather(lax.all_gather(strip, "section", axis=0), ("y", "core"), axis=0)
+        last = sections - 1
+        turned = dec_weight.T
+        wide = turned.shape[0]
+        strip = lax.dynamic_slice_in_dim(turned, core * (wide // 2), wide // 2, 0)
+        strips = jnp.stack(
+            [send(strip, lambda s, w, d: (last, w, d), (source,)) for source in range(last)]
+        )
+        matched = to_other_core(strips, (last,))
+        strips = jnp.stack([jnp.where(core == 0, strips, matched), jnp.where(core == 0, matched, strips)], axis=1)
+        matrix = jnp.concatenate([strips.reshape(last, wide, depth), turned[None]], axis=0)
 
         labels = regions[0, 0]
         labels = jnp.where(parity == core, labels, to_other_core(labels, range(sections)))
@@ -200,9 +218,8 @@
             far_b = to_other_core(own_b, (step,))
             out_a, out_b = layer(lq, lk, norm_gain, own_a, own_b, far_a, far_b, native, others)
             if step + 1 < sections:
+                own_b = send(out_a, behind, (step,))
                 own_a = send(out_b, same, (step,))
-                own_b = send(out_a, behind, (step,))
-        last = sections - 1
         values = decode(final_gain[None, :], out_a, out_b, matrix)
 
         values = values.reshape(sections, 2, 2, half, -1)

time: 222 us -> 213 us (0.959)
  the two profiles are of different devices: /device:TPU:1 before, /device:TPU:192 now
where the time goes in v5:
time: 213 us; the launch traced here: 212 us
  waiting for transfers between devices  78.1 us (37%)
  starting transfers between devices  39.7 us (19%)
  blocking collectives  31.4 us (15%)
  Pallas kernels  24.9 us (12%)
  between operations  14 us (7%)
  local copies, waits for them, and re-layouts  13.4 us (6%)
  other arithmetic  10.6 us (5%)
    ppermute x23, waiting for transfers between devices, send(): return lax.ppermute(value, AXES, pairs)  53.6 us
    ppermute x23, starting transfers between devices, send(): return lax.ppermute(value, AXES, pairs)  39.7 us
    all_gather x1, blocking collectives, body(): column = lax.all_gather(piece, 'dp', axis=0)  31.4 us
    all_gather x1, waiting for transfers between devices, body(): others = lax.all_gather(rolled, ('y', 'core'), axis=0)  24.5 us
    pallas_call x3, Pallas kernels, layer(): pl.pallas_call(layer_kernel, out_shape=(shape, shape), in_specs=[vmem] *...  23.6 us
    another operation x2, local copies, waits for them, and re-layouts, body(): qkv_weight[0].reshape(16, depth // 16, width)  8.91 us
  transfers between devices with their start and end apart: 24, of which 6 were waited for; matrix products, arithmetic and copies ran while one was open for 10% of the time, Pallas kernels for 4%

profile of v5, /device:TPU:192, one launch (start us, length us, event | category | flops | bytes accessed | tf_op | source)
XLA Modules:
  0.0 212.1 jit_solution(17279196701987355423)
XLA Ops:
  8.6 31.4 %all-gather = bf16[512,768]{1,0:T(8,128)(2,1)S(1)} all-gather(bf16[128,768]{1,0:T(8,128)(2,1)S(1)} %pad_maximum_fusion.4), channel_id=2, replica_groups=mesh['section'=3,'x'=4,'y'=8,'core'=2,'dp'=4] {'dp'}, dimensions={0}, use_global_device_ids=true | all-gather | bytes 983040 | tf_op jit(solution)/shard_map/all_gather | solution.py:169
  41.9 1.5 collective-permute-start.14
  43.4 6.1 %collective-permute-start.13 = (bf16[184,1536]{1,0:T(8,128)(2,1)}, bf16[184,1536]{1,0:T(8,128)(2,1)}, u32[]{:S(2)}, u32[]{:S(2)}) collective-permute-start(bf16[184,1536]{1,0:T(8,128)(2,1)} %dynamic-slice_bitcast_fusion), channel_id=1, source_target_pairs={{0,512},{1,513},{2,514},{3,515},{4,516},{5,517},{6,518},{7,519},{8... | collective-permute-start | bytes 1695752 | tf_op jit(solution)/shard_map/ppermute | solution.py:142
  49.5 1.9 collective-permute-start
  52.2 5.1 %collective-permute-start.1 = (bf16[64,1536]{1,0:T(8,128)(2,1)}, bf16[64,1536]{1,0:T(8,128)(2,1)S(1)}, u32[]{:S(2)}, u32[]{:S(2)}) collective-permute-start(bf16[64,1536]{1,0:T(8,128)(2,1)} %get-tuple-element.33), channel_id=1, source_target_pairs={{0,0},{1,3},{2,4},{3,7},{4,1},{5,2},{6,5},{7,6},{8,8},{9,11},{10,1... | collective-permute-start | bytes 589832 | tf_op jit(solution)/shard_map/ppermute | solution.py:142
  57.3 1.9 collective-permute-start.2
  59.3 4.3 %copy.49 = bf16[1,1536,3,256]{3,2,1,0:T(4,128)(2,1)S(1)} copy(bf16[1,1536,3,256]{3,1,2,0:T(8,128)(2,1)} %param.10) | data formatting | bytes 4718592 | tf_op jit(solution)/shard_map/reshape;squeeze | solution.py:175
  63.6 4.6 %reshape.121 = bf16[16,96,768]{2,1,0:T(8,128)(2,1)} reshape(bf16[1,1536,3,256]{3,2,1,0:T(4,128)(2,1)S(1)} %copy.49) | data formatting | bytes 4718592 | tf_op jit(solution)/shard_map/reshape;squeeze | solution.py:175
  69.3 1.8 pad_maximum_fusion.1.native
  72.3 2.3 %pad_maximum_fusion.3 = bf16[2,184,1536]{2,1,0:T(8,128)(2,1)} fusion(bf16[1,184,1536]{2,1,0:T(8,128)(2,1)} %bitcast.10, bf16[1,184,1536]{2,1,0:T(8,128)(2,1)} %bitcast.9), kind=kLoop, calls=%fused_computation.5 | loop fusion | flops 565248 | bytes 2260992 | tf_op jit(solution)/shard_map/stack | solution.py:180
  74.6 1.7 collective-permute-start.15
  76.3 2.6 %collective-permute-start.3 = (bf16[64,1536]{1,0:T(8,128)(2,1)S(1)}, bf16[64,1536]{1,0:T(8,128)(2,1)}, u32[]{:S(2)}, u32[]{:S(2)}) collective-permute-start(bf16[64,1536]{1,0:T(8,128)(2,1)S(1)} %pad_maximum_fusion.5.own_a), channel_id=1, source_target_pairs={{0,4},{1,5},{2,6},{3,7},{4,0},{5,1},{6,2},{7,3},{8,12},{9,13},{10,... | collective-permute-start | bytes 589832 | tf_op jit(solution)/shard_map/ppermute | solution.py:142
  79.5 1.9 collective-permute-start.4
  81.7 1.5 collective-permute-done.4.far_b
  83.2 24.5 %all-gather.4.cloned.1.call-done = bf16[48,128,768]{2,1,0:T(8,128)(2,1)} async-done(((bf16[3,128,768]{2,1,0:T(8,128)(2,1)}), bf16[48,128,768]{2,1,0:T(8,128)(2,1)}) %all-gather.4.cloned.1.call-update) | async-done | bytes 9437200 | tf_op jit(solution)/shard_map/all_gather | solution.py:171
  107.7 8.8 %layer.3 = (bf16[64,1536]{1,0:T(8,128)(2,1)}, bf16[64,1536]{1,0:T(8,128)(2,1)}) custom-call(s32[128,1]{1,0:T(8,128)S(1)} %broadcast_in_dim.13.lq, s32[1,256]{1,0:T(1,128)S(1)} %broadcast_in_dim_reshape.3.lk, f32[1,1536]{1,0:T(1,128)S(1)} %copy-done, bf16[64,1536]{1,0:T(8,128)(2,1)S(1)} %pad_maximum_fusion.5.own_a, bf16[64,1536]{1,0:T(8,128)(2,1)} %pad_maximum_fusion.6.own_b, ...), custom_call_target="tpu_custom_call" | custom-call | flops 2600000000 | bytes 14000000 | tf_op jit(solution)/shard_map/layer/pallas_call | solution.py:87
  116.5 4.8 %collective-permute-start.5 = (bf16[64,1536]{1,0:T(8,128)(2,1)}, bf16[64,1536]{1,0:T(8,128)(2,1)S(1)}, u32[]{:S(2)}, u32[]{:S(2)}) collective-permute-start(bf16[64,1536]{1,0:T(8,128)(2,1)} %get-tuple-element.20), channel_id=1, source_target_pairs={{0,256},{1,257},{2,258},{3,259},{4,260},{5,261},{6,262},{7,263},{8... | collective-permute-start | bytes 589832 | tf_op jit(solution)/shard_map/ppermute | solution.py:142
  121.3 2.0 collective-permute-start.6
  123.3 2.9 %collective-permute-done.5.own_a = bf16[64,1536]{1,0:T(8,128)(2,1)S(1)} collective-permute-done((bf16[64,1536]{1,0:T(8,128)(2,1)}, bf16[64,1536]{1,0:T(8,128)(2,1)S(1)}, u32[]{:S(2)}, u32[]{:S(2)}) %collective-permute-start.5) | collective-permute-done | bytes 196640 | tf_op jit(solution)/shard_map/ppermute | solution.py:142
  128.3 1.7 select_bitcast_fusion.1
  130.1 7.9 %layer.4 = (bf16[64,1536]{1,0:T(8,128)(2,1)S(1)}, bf16[64,1536]{1,0:T(8,128)(2,1)S(1)}) custom-call(s32[128,1]{1,0:T(8,128)S(1)} %broadcast_in_dim.13.lq, s32[1,256]{1,0:T(1,128)S(1)} %broadcast_in_dim_reshape.3.lk, f32[1,1536]{1,0:T(1,128)S(1)} %copy-done, bf16[64,1536]{1,0:T(8,128)(2,1)S(1)} %collective-permute-done.5.own_a, ...), custom_call_target="tpu_custom_call" | custom-call | flops 2600000000 | bytes 14000000 | tf_op jit(solution)/shard_map/layer/pallas_call | solution.py:87
  141.6 6.9 %layer.5 = (bf16[64,1536]{1,0:T(8,128)(2,1)S(1)}, bf16[64,1536]{1,0:T(8,128)(2,1)S(1)}) custom-call(s32[128,1]{1,0:T(8,128)S(1)} %broadcast_in_dim.13.lq, s32[1,256]{1,0:T(1,128)S(1)} %broadcast_in_dim_reshape.3.lk, f32[1,1536]{1,0:T(1,128)S(1)} %copy-done, bf16[64,1536]{1,0:T(8,128)(2,1)S(1)} %collective-permute-done.9.own_a, ...), custom_call_target="tpu_custom_call" | custom-call | flops 2600000000 | bytes 14000000 | tf_op jit(solution)/shard_map/layer/pallas_call | solution.py:87
  156.1 40.3 %collective-permute-done.22 = bf16[2,32,368]{2,1,0:T(8,128)(2,1)S(1)} collective-permute-done((bf16[2,32,368]{2,1,0:T(8,128)(2,1)S(1)}, bf16[2,32,368]{2,1,0:T(8,128)(2,1)S(1)}, u32[]{:S(2)}, u32[]{:S(2)}) %collective-permute-start.22) | collective-permute-done | bytes 47136 | tf_op jit(solution)/shard_map/ppermute | solution.py:142
  196.4 8.2 %collective-permute-done.21 = bf16[2,32,368]{2,1,0:T(8,128)(2,1)S(1)} collective-permute-done((bf16[2,32,368]{2,1,0:T(8,128)(2,1)S(1)}, bf16[2,32,368]{2,1,0:T(8,128)(2,1)S(1)}, u32[]{:S(2)}, u32[]{:S(2)}) %collective-permute-start.21) | collective-permute-done | bytes 47136 | tf_op jit(solution)/shard_map/ppermute | solution.py:142
  (77 shorter events, 21.6 us)
Async XLA Ops:
  6.5 101.2 %all-gather.4.cloned.1.call-start = ((), (), s32[]{:S(2)}) async-start(), calls=%async_computation | async-start | bytes 10027008 | tf_op jit(solution)/shard_map/all_gather | solution.py:171
  41.9 30.4 %collective-permute-start.14 = (bf16[184,1536]{1,0:T(8,128)(2,1)}, bf16[184,1536]{1,0:T(8,128)(2,1)}, u32[]{:S(2)}, u32[]{:S(2)}) collective-permute-start(bf16[184,1536]{1,0:T(8,128)(2,1)} %dynamic-slice_bitcast_fusion), channel_id=1, source_target_pairs={{256,512},{257,513},{258,514},{259,515},{260,516},{261,517},{262,5... | collective-permute-start | bytes 1695752 | tf_op jit(solution)/shard_map/ppermute | solution.py:142
  43.4 28.9 %collective-permute-start.13 = (bf16[184,1536]{1,0:T(8,128)(2,1)}, bf16[184,1536]{1,0:T(8,128)(2,1)}, u32[]{:S(2)}, u32[]{:S(2)}) collective-permute-start(bf16[184,1536]{1,0:T(8,128)(2,1)} %dynamic-slice_bitcast_fusion), channel_id=1, source_target_pairs={{0,512},{1,513},{2,514},{3,515},{4,516},{5,517},{6,518},{7,519},{8... | collective-permute-start | bytes 1695752 | tf_op jit(solution)/shard_map/ppermute | solution.py:142
  49.5 21.6 %collective-permute-start = (s32[256]{0:T(256)S(1)}, s32[256]{0:T(256)S(1)}, u32[]{:S(2)}, u32[]{:S(2)}) collective-permute-start(s32[256]{0:T(256)S(1)} %bitcast.94), channel_id=1, source_target_pairs={{0,4},{1,5},{2,6},{3,7},{4,0},{5,1},{6,2},{7,3},{8,12},{9,13},{10,... | collective-permute-start | bytes 3080 | tf_op jit(solution)/shard_map/ppermute | solution.py:142
  52.2 19.1 %collective-permute-start.1 = (bf16[64,1536]{1,0:T(8,128)(2,1)}, bf16[64,1536]{1,0:T(8,128)(2,1)S(1)}, u32[]{:S(2)}, u32[]{:S(2)}) collective-permute-start(bf16[64,1536]{1,0:T(8,128)(2,1)} %get-tuple-element.33), channel_id=1, source_target_pairs={{0,0},{1,3},{2,4},{3,7},{4,1},{5,2},{6,5},{7,6},{8,8},{9,11},{10,1... | collective-permute-start | bytes 589832 | tf_op jit(solution)/shard_map/ppermute | solution.py:142
  57.3 13.9 %collective-permute-start.2 = (bf16[64,1536]{1,0:T(8,128)(2,1)S(1)}, bf16[64,1536]{1,0:T(8,128)(2,1)}, u32[]{:S(2)}, u32[]{:S(2)}) collective-permute-start(bf16[64,1536]{1,0:T(8,128)(2,1)S(1)} %get-tuple-element.34), channel_id=1, source_target_pairs={{0,3},{1,0},{2,7},{3,4},{4,2},{5,1},{6,6},{7,5},{8,11},{9,8},{10,1... | collective-permute-start | bytes 589832 | tf_op jit(solution)/shard_map/ppermute | solution.py:142
  74.6 53.7 %collective-permute-start.15 = (bf16[2,184,1536]{2,1,0:T(8,128)(2,1)}, bf16[2,184,1536]{2,1,0:T(8,128)(2,1)}, u32[]{:S(2)}, u32[]{:S(2)}) collective-permute-start(bf16[2,184,1536]{2,1,0:T(8,128)(2,1)} %pad_maximum_fusion.3), channel_id=1, source_target_pairs={{512,516},{513,517},{514,518},{515,519},{516,512},{517,513},{518,5... | collective-permute-start | bytes 3391496 | tf_op jit(solution)/shard_map/ppermute | solution.py:142
  76.3 5.4 %collective-permute-start.3 = (bf16[64,1536]{1,0:T(8,128)(2,1)S(1)}, bf16[64,1536]{1,0:T(8,128)(2,1)}, u32[]{:S(2)}, u32[]{:S(2)}) collective-permute-start(bf16[64,1536]{1,0:T(8,128)(2,1)S(1)} %pad_maximum_fusion.5.own_a), channel_id=1, source_target_pairs={{0,4},{1,5},{2,6},{3,7},{4,0},{5,1},{6,2},{7,3},{8,12},{9,13},{10,... | collective-permute-start | bytes 589832 | tf_op jit(solution)/shard_map/ppermute | solution.py:142
  79.5 3.7 %collective-permute-start.4 = (bf16[64,1536]{1,0:T(8,128)(2,1)}, bf16[64,1536]{1,0:T(8,128)(2,1)}, u32[]{:S(2)}, u32[]{:S(2)}) collective-permute-start(bf16[64,1536]{1,0:T(8,128)(2,1)} %pad_maximum_fusion.6.own_b), channel_id=1, source_target_pairs={{0,4},{1,5},{2,6},{3,7},{4,0},{5,1},{6,2},{7,3},{8,12},{9,13},{10,... | collective-permute-start | bytes 589832 | tf_op jit(solution)/shard_map/ppermute | solution.py:142
  116.5 9.6 %collective-permute-start.5 = (bf16[64,1536]{1,0:T(8,128)(2,1)}, bf16[64,1536]{1,0:T(8,128)(2,1)S(1)}, u32[]{:S(2)}, u32[]{:S(2)}) collective-permute-start(bf16[64,1536]{1,0:T(8,128)(2,1)} %get-tuple-element.20), channel_id=1, source_target_pairs={{0,256},{1,257},{2,258},{3,259},{4,260},{5,261},{6,262},{7,263},{8... | collective-permute-start | bytes 589832 | tf_op jit(solution)/shard_map/ppermute | solution.py:142
  121.3 6.2 %collective-permute-start.6 = (bf16[64,1536]{1,0:T(8,128)(2,1)}, bf16[64,1536]{1,0:T(8,128)(2,1)}, u32[]{:S(2)}, u32[]{:S(2)}) collective-permute-start(bf16[64,1536]{1,0:T(8,128)(2,1)} %get-tuple-element.21), channel_id=1, source_target_pairs={{0,505},{1,256},{2,259},{3,506},{4,509},{5,260},{6,263},{7,510},{8... | collective-permute-start | bytes 589832 | tf_op jit(solution)/shard_map/ppermute | solution.py:142
  126.2 3.9 %collective-permute-start.7 = (bf16[64,1536]{1,0:T(8,128)(2,1)S(1)}, bf16[64,1536]{1,0:T(8,128)(2,1)S(1)}, u32[]{:S(2)}, u32[]{:S(2)}) collective-permute-start(bf16[64,1536]{1,0:T(8,128)(2,1)S(1)} %collective-permute-done.5.own_a), channel_id=1, source_target_pairs={{256,260},{257,261},{258,262},{259,263},{260,256},{261,257},{262,2... | collective-permute-start | bytes 589832 | tf_op jit(solution)/shard_map/ppermute | solution.py:142
  127.5 2.6 %collective-permute-start.8 = (bf16[64,1536]{1,0:T(8,128)(2,1)}, bf16[64,1536]{1,0:T(8,128)(2,1)S(1)}, u32[]{:S(2)}, u32[]{:S(2)}) collective-permute-start(bf16[64,1536]{1,0:T(8,128)(2,1)} %collective-permute-done.6.own_b), channel_id=1, source_target_pairs={{256,260},{257,261},{258,262},{259,263},{260,256},{261,257},{262,2... | collective-permute-start | bytes 589832 | tf_op jit(solution)/shard_map/ppermute | solution.py:142
  137.9 1.8 collective-permute-start.9
  138.6 1.9 collective-permute-start.10
  139.8 1.8 collective-permute-start.11
  140.6 1.0 collective-permute-start.12
  149.9 1.4 collective-permute-start.17
  150.6 0.7 collective-permute-start.16
  151.4 4.6 %collective-permute-start.18 = (bf16[2,32,368]{2,1,0:T(8,128)(2,1)S(1)}, bf16[2,32,368]{2,1,0:T(8,128)(2,1)S(1)}, u32[]{:S(2)}, u32[]{:S(2)}) collective-permute-start(bf16[2,32,368]{2,1,0:T(8,128)(2,1)S(1)} %get-tuple-element.37), channel_id=1, source_target_pairs={{512,764},{513,765},{514,766},{515,767},{516,512},{517,513},{518,5... | collective-permute-start | bytes 141320 | tf_op jit(solution)/shard_map/ppermute | solution.py:142
  152.1 4.0 %collective-permute-start.20 = (bf16[2,32,368]{2,1,0:T(8,128)(2,1)S(1)}, bf16[2,32,368]{2,1,0:T(8,128)(2,1)S(1)}, u32[]{:S(2)}, u32[]{:S(2)}) collective-permute-start(bf16[2,32,368]{2,1,0:T(8,128)(2,1)S(1)} %get-tuple-element.39), channel_id=1, source_target_pairs={{512,508},{513,509},{514,510},{515,511},{516,256},{517,257},{518,2... | collective-permute-start | bytes 141320 | tf_op jit(solution)/shard_map/ppermute | solution.py:142
  152.8 3.3 %collective-permute-start.19 = (bf16[2,32,368]{2,1,0:T(8,128)(2,1)S(1)}, bf16[2,32,368]{2,1,0:T(8,128)(2,1)S(1)}, u32[]{:S(2)}, u32[]{:S(2)}) collective-permute-start(bf16[2,32,368]{2,1,0:T(8,128)(2,1)S(1)} %get-tuple-element.38), channel_id=1, source_target_pairs={{512,256},{513,257},{514,258},{515,259},{516,260},{517,261},{518,2... | collective-permute-start | bytes 141320 | tf_op jit(solution)/shard_map/ppermute | solution.py:142
  153.4 42.9 %collective-permute-start.22 = (bf16[2,32,368]{2,1,0:T(8,128)(2,1)S(1)}, bf16[2,32,368]{2,1,0:T(8,128)(2,1)S(1)}, u32[]{:S(2)}, u32[]{:S(2)}) collective-permute-start(bf16[2,32,368]{2,1,0:T(8,128)(2,1)S(1)} %get-tuple-element.40), channel_id=1, source_target_pairs={{512,252},{513,253},{514,254},{515,255},{516,0},{517,1},{518,2},{5... | collective-permute-start | bytes 141320 | tf_op jit(solution)/shard_map/ppermute | solution.py:142
  154.7 49.9 %collective-permute-start.21 = (bf16[2,32,368]{2,1,0:T(8,128)(2,1)S(1)}, bf16[2,32,368]{2,1,0:T(8,128)(2,1)S(1)}, u32[]{:S(2)}, u32[]{:S(2)}) collective-permute-start(bf16[2,32,368]{2,1,0:T(8,128)(2,1)S(1)} %get-tuple-element.35), channel_id=1, source_target_pairs={{512,0},{513,1},{514,2},{515,3},{516,4},{517,5},{518,6},{519,7},{5... | collective-permute-start | bytes 141320 | tf_op jit(solution)/shard_map/ppermute | solution.py:142
  (6 other events, 172.1 us)
Sparse Core Ops, SparseCore 0:
  41.2 66.5 all-gather.3

commit v6 on v5

--- a/solution.py
+++ b/solution.py
@@ -26,7 +26,7 @@
     return (center * lax.rsqrt(spread + 1e-05) * gain).astype(jnp.bfloat16)
 
 
-def layer_kernel(lq, lk, gain, own_a, own_b, far_a, far_b, native, others, out_a, out_b, held, normed, acc, sems):
+def layer_kernel(lq, lk, gain, own_b, own_a, far_b, far_a, native, others, out_a, out_b, held, normed, acc, sems):
     quarters, slices, per, width = held.shape
     inner = width // 3
     heads = inner // HEAD
@@ -43,8 +43,10 @@
         normed[index * part:(index + 1) * part, :] = norm(ref[...].astype(jnp.float32), gain[...])
     allowed = lq[...] == lk[...]
     head_of = lax.broadcasted_iota(jnp.int32, (half, inner), 1) // HEAD
-    for step in range(quarters):
-        copies[step].wait()
+    acc[...] = jnp.zeros_like(acc)
+
+    def quarter(step, carry):
+        pltpu.make_async_copy(native, held.at[step], sems.at[step]).wait()
 
         def block(low, count):
             return held[step, :, low:low + count, :].reshape(slices * count, width)
@@ -70,10 +72,10 @@
             update = jnp.dot(blended, block(rows + side * orows, orows), preferred_element_type=jnp.float32)
             update = update.astype(jnp.bfloat16).astype(jnp.float32)
             cols = slice(side * width, (side + 1) * width)
-            if step == 0:
-                acc[:, cols] = update
-            else:
-                acc[:, cols] += update
+            acc[:, cols] += update
+        return carry
+
+    lax.fori_loop(0, quarters, quarter, 0)
     out_a[...] = (own_a[...].astype(jnp.float32) + acc[:part, :]).astype(jnp.bfloat16)
     out_b[...] = (own_b[...].astype(jnp.float32) + acc[part:, :]).astype(jnp.bfloat16)
 
@@ -98,7 +100,7 @@
         compiler_params=pltpu.CompilerParams(vmem_limit_bytes=48 << 20),
         cost_estimate=pl.CostEstimate(flops=2_600_000_000, bytes_accessed=14_000_000, transcendentals=524288),
         name="layer",
-    )(lq, lk, gain, own_a, own_b, far_a, far_b, native, others)
+    )(lq, lk, gain, own_b, own_a, far_b, far_a, native, others)
 
 
 def decode_kernel(gain, part_a, part_b, matrix, out):
@@ -236,7 +238,7 @@
             [jnp.where(even, straight, crossed), jnp.where(even, crossed, straight)], axis=1
         )
         shown = None
-        for target in range(sections):
+        for target in reversed(range(sections)):
             ahead = send(result[target, :, 0], lambda s, w, d: (target, w - 1, d), (last,))
             kept = result[target, :, 1]
             if target != last:

time: 213 us -> 208 us (0.977)
  the two profiles are of different devices: /device:TPU:192 before, /device:TPU:128 now
where the time goes in v6:
time: 208 us; the launch traced here: 207 us
  waiting for transfers between devices  70.9 us (34%)
  starting transfers between devices  40.7 us (20%)
  blocking collectives  33.1 us (16%)
  Pallas kernels  24.6 us (12%)
  between operations  13.9 us (7%)
  local copies, waits for them, and re-layouts  13.4 us (6%)
  other arithmetic  10.6 us (5%)
    ppermute x23, waiting for transfers between devices, send(): return lax.ppermute(value, AXES, pairs)  46.2 us
    ppermute x23, starting transfers between devices, send(): return lax.ppermute(value, AXES, pairs)  40.7 us
    all_gather x1, blocking collectives, body(): column = lax.all_gather(piece, 'dp', axis=0)  33.1 us
    all_gather x1, waiting for transfers between devices, body(): others = lax.all_gather(rolled, ('y', 'core'), axis=0)  24.6 us
    pallas_call x3, Pallas kernels, layer(): pl.pallas_call(layer_kernel, out_shape=(shape, shape), in_specs=[vmem] *...  23.2 us
    another operation x2, local copies, waits for them, and re-layouts, body(): qkv_weight[0].reshape(16, depth // 16, width)  8.9 us
  transfers between devices with their start and end apart: 24, of which 7 were waited for; matrix products, arithmetic and copies ran while one was open for 10% of the time, Pallas kernels for 4%

profile of v6, /device:TPU:128, one launch (start us, length us, event | category | flops | bytes accessed | tf_op | source)
XLA Modules:
  0.0 207.2 jit_solution(1511992053861323809)
XLA Ops:
  8.6 33.1 %all-gather = bf16[512,768]{1,0:T(8,128)(2,1)S(1)} all-gather(bf16[128,768]{1,0:T(8,128)(2,1)S(1)} %pad_maximum_fusion.4), channel_id=2, replica_groups=mesh['section'=3,'x'=4,'y'=8,'core'=2,'dp'=4] {'dp'}, dimensions={0}, use_global_device_ids=true | all-gather | bytes 983040 | tf_op jit(solution)/shard_map/all_gather | solution.py:171
  46.2 1.9 collective-permute-start
  49.6 1.4 collective-permute-start.2
  50.9 4.3 %copy.49 = bf16[1,1536,3,256]{3,2,1,0:T(4,128)(2,1)S(1)} copy(bf16[1,1536,3,256]{3,1,2,0:T(8,128)(2,1)} %param.10) | data formatting | bytes 4718592 | tf_op jit(solution)/shard_map/reshape;squeeze | solution.py:177
  55.3 4.6 %reshape.121 = bf16[16,96,768]{2,1,0:T(8,128)(2,1)} reshape(bf16[1,1536,3,256]{3,2,1,0:T(4,128)(2,1)S(1)} %copy.49) | data formatting | bytes 4718592 | tf_op jit(solution)/shard_map/reshape;squeeze | solution.py:177
  61.0 1.8 pad_maximum_fusion.1.native
  63.9 12.0 %collective-permute-done.14 = bf16[184,1536]{1,0:T(8,128)(2,1)} collective-permute-done((bf16[184,1536]{1,0:T(8,128)(2,1)}, bf16[184,1536]{1,0:T(8,128)(2,1)}, u32[]{:S(2)}, u32[]{:S(2)}) %collective-permute-start.14) | collective-permute-done | bytes 565280 | tf_op jit(solution)/shard_map/ppermute | solution.py:144
  75.9 2.3 %pad_maximum_fusion.3 = bf16[2,184,1536]{2,1,0:T(8,128)(2,1)} fusion(bf16[1,184,1536]{2,1,0:T(8,128)(2,1)} %bitcast.10, bf16[1,184,1536]{2,1,0:T(8,128)(2,1)} %bitcast.9), kind=kLoop, calls=%fused_computation.5 | loop fusion | flops 565248 | bytes 2260992 | tf_op jit(solution)/shard_map/stack | solution.py:182
  78.3 1.9 collective-permute-start.15
  80.2 1.4 collective-permute-start.3
  83.8 24.6 %all-gather.4.cloned.1.call-done = bf16[48,128,768]{2,1,0:T(8,128)(2,1)} async-done(((bf16[3,128,768]{2,1,0:T(8,128)(2,1)}), bf16[48,128,768]{2,1,0:T(8,128)(2,1)}) %all-gather.4.cloned.1.call-update) | async-done | bytes 9437200 | tf_op jit(solution)/shard_map/all_gather | solution.py:173
  108.4 8.6 %layer.3 = (bf16[64,1536]{1,0:T(8,128)(2,1)}, bf16[64,1536]{1,0:T(8,128)(2,1)}) custom-call(s32[128,1]{1,0:T(8,128)S(1)} %broadcast_in_dim.13.lq, s32[1,256]{1,0:T(1,128)S(1)} %broadcast_in_dim_reshape.3.lk, f32[1,1536]{1,0:T(1,128)S(1)} %copy-done, bf16[64,1536]{1,0:T(8,128)(2,1)S(1)} %pad_maximum_fusion.5.own_b, bf16[64,1536]{1,0:T(8,128)(2,1)} %pad_maximum_fusion.6.own_a, ...), custom_call_target="tpu_custom_call" | custom-call | flops 2600000000 | bytes 14000000 | tf_op jit(solution)/shard_map/layer/pallas_call | solution.py:89
  120.5 1.7 select_bitcast_fusion.1
  122.2 7.9 %layer.4 = (bf16[64,1536]{1,0:T(8,128)(2,1)S(1)}, bf16[64,1536]{1,0:T(8,128)(2,1)S(1)}) custom-call(s32[128,1]{1,0:T(8,128)S(1)} %broadcast_in_dim.13.lq, s32[1,256]{1,0:T(1,128)S(1)} %broadcast_in_dim_reshape.3.lk, f32[1,1536]{1,0:T(1,128)S(1)} %copy-done, bf16[64,1536]{1,0:T(8,128)(2,1)S(1)} %collective-permute-done.5.own_b, ...), custom_call_target="tpu_custom_call" | custom-call | flops 2600000000 | bytes 14000000 | tf_op jit(solution)/shard_map/layer/pallas_call | solution.py:89
  133.1 22.8 %collective-permute-done.9.own_b = bf16[64,1536]{1,0:T(8,128)(2,1)S(1)} collective-permute-done((bf16[64,1536]{1,0:T(8,128)(2,1)S(1)}, bf16[64,1536]{1,0:T(8,128)(2,1)S(1)}, u32[]{:S(2)}, u32[]{:S(2)}) %collective-permute-start.9) | collective-permute-done | bytes 196640 | tf_op jit(solution)/shard_map/ppermute | solution.py:144
  156.0 1.9 collective-permute-start.11
  157.9 3.1 %collective-permute-done.10.own_a = bf16[64,1536]{1,0:T(8,128)(2,1)S(1)} collective-permute-done((bf16[64,1536]{1,0:T(8,128)(2,1)S(1)}, bf16[64,1536]{1,0:T(8,128)(2,1)S(1)}, u32[]{:S(2)}, u32[]{:S(2)}) %collective-permute-start.10) | collective-permute-done | bytes 196640 | tf_op jit(solution)/shard_map/ppermute | solution.py:144
  161.0 1.9 collective-permute-start.12
  164.3 6.8 %layer.5 = (bf16[64,1536]{1,0:T(8,128)(2,1)S(1)}, bf16[64,1536]{1,0:T(8,128)(2,1)S(1)}) custom-call(s32[128,1]{1,0:T(8,128)S(1)} %broadcast_in_dim.13.lq, s32[1,256]{1,0:T(1,128)S(1)} %broadcast_in_dim_reshape.3.lk, f32[1,1536]{1,0:T(1,128)S(1)} %copy-done, bf16[64,1536]{1,0:T(8,128)(2,1)S(1)} %collective-permute-done.9.own_b, ...), custom_call_target="tpu_custom_call" | custom-call | flops 2600000000 | bytes 14000000 | tf_op jit(solution)/shard_map/layer/pallas_call | solution.py:89
  171.1 1.4 decode.1
  172.5 3.9 %collective-permute-start.17 = (bf16[3,2,32,368]{3,2,1,0:T(8,128)(2,1)S(1)}, bf16[3,2,32,368]{3,2,1,0:T(8,128)(2,1)S(1)}, u32[]{:S(2)}, u32[]{:S(2)}) collective-permute-start(bf16[3,2,32,368]{3,2,1,0:T(8,128)(2,1)S(1)} %get-tuple-element.43), channel_id=1, source_target_pairs={{512,513},{513,517},{514,516},{515,512},{516,515},{517,519},{518,5... | collective-permute-start | bytes 423944 | tf_op jit(solution)/shard_map/ppermute | solution.py:144
  177.0 5.5 %collective-permute-done.17 = bf16[3,2,32,368]{3,2,1,0:T(8,128)(2,1)S(1)} collective-permute-done((bf16[3,2,32,368]{3,2,1,0:T(8,128)(2,1)S(1)}, bf16[3,2,32,368]{3,2,1,0:T(8,128)(2,1)S(1)}, u32[]{:S(2)}, u32[]{:S(2)}) %collective-permute-start.17) | collective-permute-done | bytes 141344 | tf_op jit(solution)/shard_map/ppermute | solution.py:144
  187.8 10.1 %collective-permute-start.22 = (bf16[2,32,368]{2,1,0:T(8,128)(2,1)S(1)}, bf16[2,32,368]{2,1,0:T(8,128)(2,1)S(1)}, u32[]{:S(2)}, u32[]{:S(2)}) collective-permute-start(bf16[2,32,368]{2,1,0:T(8,128)(2,1)S(1)} %get-tuple-element.40), channel_id=1, source_target_pairs={{512,764},{513,765},{514,766},{515,767},{516,512},{517,513},{518,5... | collective-permute-start | bytes 141320 | tf_op jit(solution)/shard_map/ppermute | solution.py:144
  198.0 1.7 collective-permute-done.22
  (77 shorter events, 26.8 us)
Async XLA Ops:
  6.5 101.9 %all-gather.4.cloned.1.call-start = ((), (), s32[]{:S(2)}) async-start(), calls=%async_computation | async-start | bytes 10027008 | tf_op jit(solution)/shard_map/all_gather | solution.py:173
  43.6 32.3 %collective-permute-start.14 = (bf16[184,1536]{1,0:T(8,128)(2,1)}, bf16[184,1536]{1,0:T(8,128)(2,1)}, u32[]{:S(2)}, u32[]{:S(2)}) collective-permute-start(bf16[184,1536]{1,0:T(8,128)(2,1)} %dynamic-slice_bitcast_fusion), channel_id=1, source_target_pairs={{256,512},{257,513},{258,514},{259,515},{260,516},{261,517},{262,5... | collective-permute-start | bytes 1695752 | tf_op jit(solution)/shard_map/ppermute | solution.py:144
  44.9 31.0 %collective-permute-start.13 = (bf16[184,1536]{1,0:T(8,128)(2,1)}, bf16[184,1536]{1,0:T(8,128)(2,1)}, u32[]{:S(2)}, u32[]{:S(2)}) collective-permute-start(bf16[184,1536]{1,0:T(8,128)(2,1)} %dynamic-slice_bitcast_fusion), channel_id=1, source_target_pairs={{0,512},{1,513},{2,514},{3,515},{4,516},{5,517},{6,518},{7,519},{8... | collective-permute-start | bytes 1695752 | tf_op jit(solution)/shard_map/ppermute | solution.py:144
  46.2 16.6 %collective-permute-start = (s32[256]{0:T(256)S(1)}, s32[256]{0:T(256)S(1)}, u32[]{:S(2)}, u32[]{:S(2)}) collective-permute-start(s32[256]{0:T(256)S(1)} %bitcast.94), channel_id=1, source_target_pairs={{0,4},{1,5},{2,6},{3,7},{4,0},{5,1},{6,2},{7,3},{8,12},{9,13},{10,... | collective-permute-start | bytes 3080 | tf_op jit(solution)/shard_map/ppermute | solution.py:144
  48.9 14.0 %collective-permute-start.1 = (bf16[64,1536]{1,0:T(8,128)(2,1)}, bf16[64,1536]{1,0:T(8,128)(2,1)S(1)}, u32[]{:S(2)}, u32[]{:S(2)}) collective-permute-start(bf16[64,1536]{1,0:T(8,128)(2,1)} %get-tuple-element.33), channel_id=1, source_target_pairs={{0,0},{1,3},{2,4},{3,7},{4,1},{5,2},{6,5},{7,6},{8,8},{9,11},{10,1... | collective-permute-start | bytes 589832 | tf_op jit(solution)/shard_map/ppermute | solution.py:144
  49.6 13.4 %collective-permute-start.2 = (bf16[64,1536]{1,0:T(8,128)(2,1)S(1)}, bf16[64,1536]{1,0:T(8,128)(2,1)}, u32[]{:S(2)}, u32[]{:S(2)}) collective-permute-start(bf16[64,1536]{1,0:T(8,128)(2,1)S(1)} %get-tuple-element.34), channel_id=1, source_target_pairs={{0,3},{1,0},{2,7},{3,4},{4,2},{5,1},{6,6},{7,5},{8,11},{9,8},{10,1... | collective-permute-start | bytes 589832 | tf_op jit(solution)/shard_map/ppermute | solution.py:144
  78.3 42.2 %collective-permute-start.15 = (bf16[2,184,1536]{2,1,0:T(8,128)(2,1)}, bf16[2,184,1536]{2,1,0:T(8,128)(2,1)}, u32[]{:S(2)}, u32[]{:S(2)}) collective-permute-start(bf16[2,184,1536]{2,1,0:T(8,128)(2,1)} %pad_maximum_fusion.3), channel_id=1, source_target_pairs={{512,516},{513,517},{514,518},{515,519},{516,512},{517,513},{518,5... | collective-permute-start | bytes 3391496 | tf_op jit(solution)/shard_map/ppermute | solution.py:144
  80.2 3.6 %collective-permute-start.3 = (bf16[64,1536]{1,0:T(8,128)(2,1)S(1)}, bf16[64,1536]{1,0:T(8,128)(2,1)}, u32[]{:S(2)}, u32[]{:S(2)}) collective-permute-start(bf16[64,1536]{1,0:T(8,128)(2,1)S(1)} %pad_maximum_fusion.5.own_b), channel_id=1, source_target_pairs={{0,4},{1,5},{2,6},{3,7},{4,0},{5,1},{6,2},{7,3},{8,12},{9,13},{10,... | collective-permute-start | bytes 589832 | tf_op jit(solution)/shard_map/ppermute | solution.py:144
  82.3 1.5 collective-permute-start.4
  117.0 2.0 collective-permute-start.5
  117.7 2.0 collective-permute-start.6
  119.1 3.1 %collective-permute-start.7 = (bf16[64,1536]{1,0:T(8,128)(2,1)S(1)}, bf16[64,1536]{1,0:T(8,128)(2,1)S(1)}, u32[]{:S(2)}, u32[]{:S(2)}) collective-permute-start(bf16[64,1536]{1,0:T(8,128)(2,1)S(1)} %collective-permute-done.5.own_b), channel_id=1, source_target_pairs={{256,260},{257,261},{258,262},{259,263},{260,256},{261,257},{262,2... | collective-permute-start | bytes 589832 | tf_op jit(solution)/shard_map/ppermute | solution.py:144
  119.8 2.4 %collective-permute-start.8 = (bf16[64,1536]{1,0:T(8,128)(2,1)}, bf16[64,1536]{1,0:T(8,128)(2,1)S(1)}, u32[]{:S(2)}, u32[]{:S(2)}) collective-permute-start(bf16[64,1536]{1,0:T(8,128)(2,1)} %collective-permute-done.6.own_a), channel_id=1, source_target_pairs={{256,260},{257,261},{258,262},{259,263},{260,256},{261,257},{262,2... | collective-permute-start | bytes 589832 | tf_op jit(solution)/shard_map/ppermute | solution.py:144
  130.1 25.9 %collective-permute-start.9 = (bf16[64,1536]{1,0:T(8,128)(2,1)S(1)}, bf16[64,1536]{1,0:T(8,128)(2,1)S(1)}, u32[]{:S(2)}, u32[]{:S(2)}) collective-permute-start(bf16[64,1536]{1,0:T(8,128)(2,1)S(1)} %get-tuple-element.22), channel_id=1, source_target_pairs={{256,761},{257,512},{258,515},{259,762},{260,765},{261,516},{262,5... | collective-permute-start | bytes 589832 | tf_op jit(solution)/shard_map/ppermute | solution.py:144
  131.4 29.6 %collective-permute-start.10 = (bf16[64,1536]{1,0:T(8,128)(2,1)S(1)}, bf16[64,1536]{1,0:T(8,128)(2,1)S(1)}, u32[]{:S(2)}, u32[]{:S(2)}) collective-permute-start(bf16[64,1536]{1,0:T(8,128)(2,1)S(1)} %get-tuple-element.23), channel_id=1, source_target_pairs={{256,512},{257,513},{258,514},{259,515},{260,516},{261,517},{262,5... | collective-permute-start | bytes 589832 | tf_op jit(solution)/shard_map/ppermute | solution.py:144
  156.0 7.2 %collective-permute-start.11 = (bf16[64,1536]{1,0:T(8,128)(2,1)S(1)}, bf16[64,1536]{1,0:T(8,128)(2,1)S(1)}, u32[]{:S(2)}, u32[]{:S(2)}) collective-permute-start(bf16[64,1536]{1,0:T(8,128)(2,1)S(1)} %collective-permute-done.9.own_b), channel_id=1, source_target_pairs={{512,516},{513,517},{514,518},{515,519},{516,512},{517,513},{518,5... | collective-permute-start | bytes 589832 | tf_op jit(solution)/shard_map/ppermute | solution.py:144
  161.0 3.3 %collective-permute-start.12 = (bf16[64,1536]{1,0:T(8,128)(2,1)S(1)}, bf16[64,1536]{1,0:T(8,128)(2,1)S(1)}, u32[]{:S(2)}, u32[]{:S(2)}) collective-permute-start(bf16[64,1536]{1,0:T(8,128)(2,1)S(1)} %collective-permute-done.10.own_a), channel_id=1, source_target_pairs={{512,516},{513,517},{514,518},{515,519},{516,512},{517,513},{518,5... | collective-permute-start | bytes 589832 | tf_op jit(solution)/shard_map/ppermute | solution.py:144
  172.5 10.0 %collective-permute-start.17 = (bf16[3,2,32,368]{3,2,1,0:T(8,128)(2,1)S(1)}, bf16[3,2,32,368]{3,2,1,0:T(8,128)(2,1)S(1)}, u32[]{:S(2)}, u32[]{:S(2)}) collective-permute-start(bf16[3,2,32,368]{3,2,1,0:T(8,128)(2,1)S(1)} %get-tuple-element.43), channel_id=1, source_target_pairs={{512,513},{513,517},{514,516},{515,512},{516,515},{517,519},{518,5... | collective-permute-start | bytes 423944 | tf_op jit(solution)/shard_map/ppermute | solution.py:144
  176.4 6.2 %collective-permute-start.16 = (bf16[3,2,32,368]{3,2,1,0:T(8,128)(2,1)S(1)}, bf16[3,2,32,368]{3,2,1,0:T(8,128)(2,1)S(1)}, u32[]{:S(2)}, u32[]{:S(2)}) collective-permute-start(bf16[3,2,32,368]{3,2,1,0:T(8,128)(2,1)S(1)} %get-tuple-element.44), channel_id=1, source_target_pairs={{512,512},{513,516},{514,517},{515,513},{516,514},{517,518},{518,5... | collective-permute-start | bytes 423944 | tf_op jit(solution)/shard_map/ppermute | solution.py:144
  182.6 15.3 %collective-permute-start.19 = (bf16[2,32,368]{2,1,0:T(8,128)(2,1)S(1)}, bf16[2,32,368]{2,1,0:T(8,128)(2,1)S(1)}, u32[]{:S(2)}, u32[]{:S(2)}) collective-permute-start(bf16[2,32,368]{2,1,0:T(8,128)(2,1)S(1)} %get-tuple-element.37), channel_id=1, source_target_pairs={{512,252},{513,253},{514,254},{515,255},{516,0},{517,1},{518,2},{5... | collective-permute-start | bytes 141320 | tf_op jit(solution)/shard_map/ppermute | solution.py:144
  183.9 14.0 %collective-permute-start.18 = (bf16[2,32,368]{2,1,0:T(8,128)(2,1)S(1)}, bf16[2,32,368]{2,1,0:T(8,128)(2,1)S(1)}, u32[]{:S(2)}, u32[]{:S(2)}) collective-permute-start(bf16[2,32,368]{2,1,0:T(8,128)(2,1)S(1)} %get-tuple-element.36), channel_id=1, source_target_pairs={{512,0},{513,1},{514,2},{515,3},{516,4},{517,5},{518,6},{519,7},{5... | collective-permute-start | bytes 141320 | tf_op jit(solution)/shard_map/ppermute | solution.py:144
  185.2 12.7 %collective-permute-start.21 = (bf16[2,32,368]{2,1,0:T(8,128)(2,1)S(1)}, bf16[2,32,368]{2,1,0:T(8,128)(2,1)S(1)}, u32[]{:S(2)}, u32[]{:S(2)}) collective-permute-start(bf16[2,32,368]{2,1,0:T(8,128)(2,1)S(1)} %get-tuple-element.39), channel_id=1, source_target_pairs={{512,508},{513,509},{514,510},{515,511},{516,256},{517,257},{518,2... | collective-permute-start | bytes 141320 | tf_op jit(solution)/shard_map/ppermute | solution.py:144
  186.5 11.4 %collective-permute-start.20 = (bf16[2,32,368]{2,1,0:T(8,128)(2,1)S(1)}, bf16[2,32,368]{2,1,0:T(8,128)(2,1)S(1)}, u32[]{:S(2)}, u32[]{:S(2)}) collective-permute-start(bf16[2,32,368]{2,1,0:T(8,128)(2,1)S(1)} %get-tuple-element.38), channel_id=1, source_target_pairs={{512,256},{513,257},{514,258},{515,259},{516,260},{517,261},{518,2... | collective-permute-start | bytes 141320 | tf_op jit(solution)/shard_map/ppermute | solution.py:144
  187.8 11.8 %collective-permute-start.22 = (bf16[2,32,368]{2,1,0:T(8,128)(2,1)S(1)}, bf16[2,32,368]{2,1,0:T(8,128)(2,1)S(1)}, u32[]{:S(2)}, u32[]{:S(2)}) collective-permute-start(bf16[2,32,368]{2,1,0:T(8,128)(2,1)S(1)} %get-tuple-element.40), channel_id=1, source_target_pairs={{512,764},{513,765},{514,766},{515,767},{516,512},{517,513},{518,5... | collective-permute-start | bytes 141320 | tf_op jit(solution)/shard_map/ppermute | solution.py:144
  (6 other events, 199.7 us)
Sparse Core Ops, SparseCore 0:
  42.9 65.4 all-gather.3

commit v7 on v6

--- a/solution.py
+++ b/solution.py
@@ -36,7 +36,7 @@
     half = 2 * part
     copies = []
     for step in range(quarters):
-        source = native if step == 0 else others.at[:, step - 1]
+        source = native.at[:slices] if step == 0 else others.at[:, step - 1]
         copies.append(pltpu.make_async_copy(source, held.at[step], sems.at[step]))
         copies[-1].start()
     for index, ref in enumerate((own_a, own_b, far_a, far_b)):
@@ -46,7 +46,7 @@
     acc[...] = jnp.zeros_like(acc)
 
     def quarter(step, carry):
-        pltpu.make_async_copy(native, held.at[step], sems.at[step]).wait()
+        pltpu.make_async_copy(native.at[:slices], held.at[step], sems.at[step]).wait()
 
         def block(low, count):
             return held[step, :, low:low + count, :].reshape(slices * count, width)
@@ -92,12 +92,12 @@
         in_specs=[vmem] * 7 + [hbm] * 2,
         out_specs=(vmem, vmem),
         scratch_shapes=[
-            pltpu.VMEM((quarters,) + native.shape, jnp.bfloat16),
+            pltpu.VMEM((quarters, others.shape[0]) + native.shape[1:], jnp.bfloat16),
             pltpu.VMEM((4 * part, depth), jnp.bfloat16),
             pltpu.VMEM((2 * part, depth), jnp.float32),
             pltpu.SemaphoreType.DMA((quarters,)),
         ],
-        compiler_params=pltpu.CompilerParams(vmem_limit_bytes=48 << 20),
+        compiler_params=pltpu.CompilerParams(vmem_limit_bytes=51 << 20),
         cost_estimate=pl.CostEstimate(flops=2_600_000_000, bytes_accessed=14_000_000, transcendentals=524288),
         name="layer",
     )(lq, lk, gain, own_b, own_a, far_b, far_a, native, others)
@@ -175,6 +175,7 @@
             (qkv_weight, out_weight, dec_weight, tokens, regions, rolled)
         )
         native = slab(qkv_weight[0].reshape(16, depth // 16, width), out_weight[0].reshape(16, orows, 2 * width))
+        native = jnp.pad(native, ((0, 4), (0, 0), (0, 0)))
         last = sections - 1
         turned = dec_weight.T
         wide = turned.shape[0]

time: 208 us -> 208 us (level)
    all_gather x1, waiting for transfers between devices: 24.6 us -> 27.5 us  [body(): others = lax.all_gather(rolled, ('y', 'core'), axis=0)]
where the time goes in v7:
time: 208 us; the launch traced here: 207 us
  waiting for transfers between devices  72.2 us (35%)
  starting transfers between devices  38.9 us (19%)
  blocking collectives  33.1 us (16%)
  Pallas kernels  25.1 us (12%)
  between operations  14 us (7%)
  local copies, waits for them, and re-layouts  13.5 us (6%)
  other arithmetic  10.4 us (5%)
    ppermute x23, waiting for transfers between devices, send(): return lax.ppermute(value, AXES, pairs)  44.6 us
    ppermute x23, starting transfers between devices, send(): return lax.ppermute(value, AXES, pairs)  38.9 us
    all_gather x1, blocking collectives, body(): column = lax.all_gather(piece, 'dp', axis=0)  33.1 us
    all_gather x1, waiting for transfers between devices, body(): others = lax.all_gather(rolled, ('y', 'core'), axis=0)  27.5 us
    pallas_call x3, Pallas kernels, layer(): pl.pallas_call(layer_kernel, out_shape=(shape, shape), in_specs=[vmem] *...  23.7 us
    another operation x2, local copies, waits for them, and re-layouts, body(): qkv_weight[0].reshape(16, depth // 16, width)  8.94 us
  transfers between devices with their start and end apart: 24, of which 7 were waited for; matrix products, arithmetic and copies ran while one was open for 10% of the time, Pallas kernels for 4%

profile of v7, /device:TPU:128, one launch (start us, length us, event | category | flops | bytes accessed | tf_op | source)
XLA Modules:
  0.0 207.1 jit_solution(9485653310863996583)
XLA Ops:
  8.6 33.1 %all-gather = bf16[512,768]{1,0:T(8,128)(2,1)S(1)} all-gather(bf16[128,768]{1,0:T(8,128)(2,1)S(1)} %pad_maximum_fusion.3), channel_id=2, replica_groups=mesh['section'=3,'x'=4,'y'=8,'core'=2,'dp'=4] {'dp'}, dimensions={0}, use_global_device_ids=true | all-gather | bytes 983040 | tf_op jit(solution)/shard_map/all_gather | solution.py:171
  44.9 1.3 collective-permute-start.13
  46.2 1.9 collective-permute-start
  49.6 1.4 collective-permute-start.2
  50.9 4.3 %copy.49 = bf16[1,1536,3,256]{3,2,1,0:T(4,128)(2,1)S(1)} copy(bf16[1,1536,3,256]{3,1,2,0:T(8,128)(2,1)} %param.10) | data formatting | bytes 4718592 | tf_op jit(solution)/shard_map/reshape;squeeze | solution.py:177
  55.3 4.6 %reshape.121 = bf16[16,96,768]{2,1,0:T(8,128)(2,1)} reshape(bf16[1,1536,3,256]{3,2,1,0:T(4,128)(2,1)S(1)} %copy.49) | data formatting | bytes 4718592 | tf_op jit(solution)/shard_map/reshape;squeeze | solution.py:177
  61.0 3.6 %fusion.4.native = bf16[20,128,768]{2,1,0:T(8,128)(2,1)} fusion(bf16[16,16,768]{2,1,0:T(8,128)(2,1)S(1)} %get-tuple-element.30, bf16[16,16,768]{2,1,0:T(8,128)(2,1)S(1)} %get-tuple-element.29, bf16[16,96,768]{2,1,0:T(8,128)(2,1)} %reshape.121), kind=kLoop, calls=%fused_computation.5 | loop fusion | flops 19660800 | bytes 7077888 | tf_op jit(solution)/shard_map/concatenate | solution.py:165
  65.7 10.2 %collective-permute-done.14 = bf16[184,1536]{1,0:T(8,128)(2,1)} collective-permute-done((bf16[184,1536]{1,0:T(8,128)(2,1)}, bf16[184,1536]{1,0:T(8,128)(2,1)}, u32[]{:S(2)}, u32[]{:S(2)}) %collective-permute-start.14) | collective-permute-done | bytes 565280 | tf_op jit(solution)/shard_map/ppermute | solution.py:144
  76.0 1.4 pad_maximum_fusion.2
  77.3 1.9 collective-permute-start.15
  80.9 27.5 %all-gather.4.cloned.1.call-done = bf16[48,128,768]{2,1,0:T(8,128)(2,1)} async-done(((bf16[3,128,768]{2,1,0:T(8,128)(2,1)}), bf16[48,128,768]{2,1,0:T(8,128)(2,1)}) %all-gather.4.cloned.1.call-update) | async-done | bytes 9437200 | tf_op jit(solution)/shard_map/all_gather | solution.py:173
  108.4 7.9 %layer.3 = (bf16[64,1536]{1,0:T(8,128)(2,1)S(1)}, bf16[64,1536]{1,0:T(8,128)(2,1)S(1)}) custom-call(s32[128,1]{1,0:T(8,128)S(1)} %broadcast_in_dim.13.lq, s32[1,256]{1,0:T(1,128)S(1)} %broadcast_in_dim_reshape.3.lk, f32[1,1536]{1,0:T(1,128)S(1)} %copy-done, bf16[64,1536]{1,0:T(8,128)(2,1)S(1)} %pad_maximum_fusion.4.own_b, ...), custom_call_target="tpu_custom_call" | custom-call | flops 2600000000 | bytes 14000000 | tf_op jit(solution)/shard_map/layer/pallas_call | solution.py:89
  119.1 1.4 select_bitcast_fusion.1
  120.5 7.9 %layer.4 = (bf16[64,1536]{1,0:T(8,128)(2,1)S(1)}, bf16[64,1536]{1,0:T(8,128)(2,1)S(1)}) custom-call(s32[128,1]{1,0:T(8,128)S(1)} %broadcast_in_dim.13.lq, s32[1,256]{1,0:T(1,128)S(1)} %broadcast_in_dim_reshape.3.lk, f32[1,1536]{1,0:T(1,128)S(1)} %copy-done, bf16[64,1536]{1,0:T(8,128)(2,1)S(1)} %collective-permute-done.5.own_b, ...), custom_call_target="tpu_custom_call" | custom-call | flops 2600000000 | bytes 14000000 | tf_op jit(solution)/shard_map/layer/pallas_call | solution.py:89
  131.5 23.3 %collective-permute-done.9.own_b = bf16[64,1536]{1,0:T(8,128)(2,1)S(1)} collective-permute-done((bf16[64,1536]{1,0:T(8,128)(2,1)S(1)}, bf16[64,1536]{1,0:T(8,128)(2,1)S(1)}, u32[]{:S(2)}, u32[]{:S(2)}) %collective-permute-start.9) | collective-permute-done | bytes 196640 | tf_op jit(solution)/shard_map/ppermute | solution.py:144
  154.7 1.9 collective-permute-start.11
  156.7 3.0 %collective-permute-done.10.own_a = bf16[64,1536]{1,0:T(8,128)(2,1)S(1)} collective-permute-done((bf16[64,1536]{1,0:T(8,128)(2,1)S(1)}, bf16[64,1536]{1,0:T(8,128)(2,1)S(1)}, u32[]{:S(2)}, u32[]{:S(2)}) %collective-permute-start.10) | collective-permute-done | bytes 196640 | tf_op jit(solution)/shard_map/ppermute | solution.py:144
  159.6 1.9 collective-permute-start.12
  163.0 7.9 %layer.5 = (bf16[64,1536]{1,0:T(8,128)(2,1)S(1)}, bf16[64,1536]{1,0:T(8,128)(2,1)S(1)}) custom-call(s32[128,1]{1,0:T(8,128)S(1)} %broadcast_in_dim.13.lq, s32[1,256]{1,0:T(1,128)S(1)} %broadcast_in_dim_reshape.3.lk, f32[1,1536]{1,0:T(1,128)S(1)} %copy-done, bf16[64,1536]{1,0:T(8,128)(2,1)S(1)} %collective-permute-done.9.own_b, ...), custom_call_target="tpu_custom_call" | custom-call | flops 2600000000 | bytes 14000000 | tf_op jit(solution)/shard_map/layer/pallas_call | solution.py:89
  170.9 1.4 decode.1
  172.3 4.0 %collective-permute-start.17 = (bf16[3,2,32,368]{3,2,1,0:T(8,128)(2,1)S(1)}, bf16[3,2,32,368]{3,2,1,0:T(8,128)(2,1)S(1)}, u32[]{:S(2)}, u32[]{:S(2)}) collective-permute-start(bf16[3,2,32,368]{3,2,1,0:T(8,128)(2,1)S(1)} %get-tuple-element.43), channel_id=1, source_target_pairs={{512,513},{513,517},{514,516},{515,512},{516,515},{517,519},{518,5... | collective-permute-start | bytes 423944 | tf_op jit(solution)/shard_map/ppermute | solution.py:144
  177.0 5.4 %collective-permute-done.17 = bf16[3,2,32,368]{3,2,1,0:T(8,128)(2,1)S(1)} collective-permute-done((bf16[3,2,32,368]{3,2,1,0:T(8,128)(2,1)S(1)}, bf16[3,2,32,368]{3,2,1,0:T(8,128)(2,1)S(1)}, u32[]{:S(2)}, u32[]{:S(2)}) %collective-permute-start.17) | collective-permute-done | bytes 141344 | tf_op jit(solution)/shard_map/ppermute | solution.py:144
  187.7 10.2 %collective-permute-start.22 = (bf16[2,32,368]{2,1,0:T(8,128)(2,1)S(1)}, bf16[2,32,368]{2,1,0:T(8,128)(2,1)S(1)}, u32[]{:S(2)}, u32[]{:S(2)}) collective-permute-start(bf16[2,32,368]{2,1,0:T(8,128)(2,1)S(1)} %get-tuple-element.40), channel_id=1, source_target_pairs={{512,764},{513,765},{514,766},{515,767},{516,512},{517,513},{518,5... | collective-permute-start | bytes 141320 | tf_op jit(solution)/shard_map/ppermute | solution.py:144
  197.9 1.7 collective-permute-done.22
  (77 shorter events, 24.2 us)
Async XLA Ops:
  6.5 101.9 %all-gather.4.cloned.1.call-start = ((), (), s32[]{:S(2)}) async-start(), calls=%async_computation | async-start | bytes 10027008 | tf_op jit(solution)/shard_map/all_gather | solution.py:173
  43.7 32.3 %collective-permute-start.14 = (bf16[184,1536]{1,0:T(8,128)(2,1)}, bf16[184,1536]{1,0:T(8,128)(2,1)}, u32[]{:S(2)}, u32[]{:S(2)}) collective-permute-start(bf16[184,1536]{1,0:T(8,128)(2,1)} %dynamic-slice_bitcast_fusion), channel_id=1, source_target_pairs={{256,512},{257,513},{258,514},{259,515},{260,516},{261,517},{262,5... | collective-permute-start | bytes 1695752 | tf_op jit(solution)/shard_map/ppermute | solution.py:144
  44.9 31.0 %collective-permute-start.13 = (bf16[184,1536]{1,0:T(8,128)(2,1)}, bf16[184,1536]{1,0:T(8,128)(2,1)}, u32[]{:S(2)}, u32[]{:S(2)}) collective-permute-start(bf16[184,1536]{1,0:T(8,128)(2,1)} %dynamic-slice_bitcast_fusion), channel_id=1, source_target_pairs={{0,512},{1,513},{2,514},{3,515},{4,516},{5,517},{6,518},{7,519},{8... | collective-permute-start | bytes 1695752 | tf_op jit(solution)/shard_map/ppermute | solution.py:144
  46.2 18.4 %collective-permute-start = (s32[256]{0:T(256)S(1)}, s32[256]{0:T(256)S(1)}, u32[]{:S(2)}, u32[]{:S(2)}) collective-permute-start(s32[256]{0:T(256)S(1)} %bitcast.94), channel_id=1, source_target_pairs={{0,4},{1,5},{2,6},{3,7},{4,0},{5,1},{6,2},{7,3},{8,12},{9,13},{10,... | collective-permute-start | bytes 3080 | tf_op jit(solution)/shard_map/ppermute | solution.py:144
  48.9 15.8 %collective-permute-start.1 = (bf16[64,1536]{1,0:T(8,128)(2,1)}, bf16[64,1536]{1,0:T(8,128)(2,1)S(1)}, u32[]{:S(2)}, u32[]{:S(2)}) collective-permute-start(bf16[64,1536]{1,0:T(8,128)(2,1)} %get-tuple-element.33), channel_id=1, source_target_pairs={{0,0},{1,3},{2,4},{3,7},{4,1},{5,2},{6,5},{7,6},{8,8},{9,11},{10,1... | collective-permute-start | bytes 589832 | tf_op jit(solution)/shard_map/ppermute | solution.py:144
  49.6 15.2 %collective-permute-start.2 = (bf16[64,1536]{1,0:T(8,128)(2,1)S(1)}, bf16[64,1536]{1,0:T(8,128)(2,1)}, u32[]{:S(2)}, u32[]{:S(2)}) collective-permute-start(bf16[64,1536]{1,0:T(8,128)(2,1)S(1)} %get-tuple-element.34), channel_id=1, source_target_pairs={{0,3},{1,0},{2,7},{3,4},{4,2},{5,1},{6,6},{7,5},{8,11},{9,8},{10,1... | collective-permute-start | bytes 589832 | tf_op jit(solution)/shard_map/ppermute | solution.py:144
  77.3 41.8 %collective-permute-start.15 = (bf16[2,184,1536]{2,1,0:T(8,128)(2,1)S(1)}, bf16[2,184,1536]{2,1,0:T(8,128)(2,1)S(1)}, u32[]{:S(2)}, u32[]{:S(2)}) collective-permute-start(bf16[2,184,1536]{2,1,0:T(8,128)(2,1)S(1)} %pad_maximum_fusion.2), channel_id=1, source_target_pairs={{512,516},{513,517},{514,518},{515,519},{516,512},{517,513},{518,5... | collective-permute-start | bytes 3391496 | tf_op jit(solution)/shard_map/ppermute | solution.py:144
  79.3 1.6 collective-permute-start.3
  80.0 0.9 collective-permute-start.4
  116.3 1.4 collective-permute-start.5
  117.0 1.4 collective-permute-start.6
  117.7 2.8 %collective-permute-start.7 = (bf16[64,1536]{1,0:T(8,128)(2,1)S(1)}, bf16[64,1536]{1,0:T(8,128)(2,1)S(1)}, u32[]{:S(2)}, u32[]{:S(2)}) collective-permute-start(bf16[64,1536]{1,0:T(8,128)(2,1)S(1)} %collective-permute-done.5.own_b), channel_id=1, source_target_pairs={{256,260},{257,261},{258,262},{259,263},{260,256},{261,257},{262,2... | collective-permute-start | bytes 589832 | tf_op jit(solution)/shard_map/ppermute | solution.py:144
  118.4 2.1 %collective-permute-start.8 = (bf16[64,1536]{1,0:T(8,128)(2,1)S(1)}, bf16[64,1536]{1,0:T(8,128)(2,1)S(1)}, u32[]{:S(2)}, u32[]{:S(2)}) collective-permute-start(bf16[64,1536]{1,0:T(8,128)(2,1)S(1)} %collective-permute-done.6.own_a), channel_id=1, source_target_pairs={{256,260},{257,261},{258,262},{259,263},{260,256},{261,257},{262,2... | collective-permute-start | bytes 589832 | tf_op jit(solution)/shard_map/ppermute | solution.py:144
  128.4 26.3 %collective-permute-start.9 = (bf16[64,1536]{1,0:T(8,128)(2,1)S(1)}, bf16[64,1536]{1,0:T(8,128)(2,1)S(1)}, u32[]{:S(2)}, u32[]{:S(2)}) collective-permute-start(bf16[64,1536]{1,0:T(8,128)(2,1)S(1)} %get-tuple-element.22), channel_id=1, source_target_pairs={{256,761},{257,512},{258,515},{259,762},{260,765},{261,516},{262,5... | collective-permute-start | bytes 589832 | tf_op jit(solution)/shard_map/ppermute | solution.py:144
  129.7 29.9 %collective-permute-start.10 = (bf16[64,1536]{1,0:T(8,128)(2,1)S(1)}, bf16[64,1536]{1,0:T(8,128)(2,1)S(1)}, u32[]{:S(2)}, u32[]{:S(2)}) collective-permute-start(bf16[64,1536]{1,0:T(8,128)(2,1)S(1)} %get-tuple-element.23), channel_id=1, source_target_pairs={{256,512},{257,513},{258,514},{259,515},{260,516},{261,517},{262,5... | collective-permute-start | bytes 589832 | tf_op jit(solution)/shard_map/ppermute | solution.py:144
  154.7 7.1 %collective-permute-start.11 = (bf16[64,1536]{1,0:T(8,128)(2,1)S(1)}, bf16[64,1536]{1,0:T(8,128)(2,1)S(1)}, u32[]{:S(2)}, u32[]{:S(2)}) collective-permute-start(bf16[64,1536]{1,0:T(8,128)(2,1)S(1)} %collective-permute-done.9.own_b), channel_id=1, source_target_pairs={{512,516},{513,517},{514,518},{515,519},{516,512},{517,513},{518,5... | collective-permute-start | bytes 589832 | tf_op jit(solution)/shard_map/ppermute | solution.py:144
  159.6 3.3 %collective-permute-start.12 = (bf16[64,1536]{1,0:T(8,128)(2,1)S(1)}, bf16[64,1536]{1,0:T(8,128)(2,1)S(1)}, u32[]{:S(2)}, u32[]{:S(2)}) collective-permute-start(bf16[64,1536]{1,0:T(8,128)(2,1)S(1)} %collective-permute-done.10.own_a), channel_id=1, source_target_pairs={{512,516},{513,517},{514,518},{515,519},{516,512},{517,513},{518,5... | collective-permute-start | bytes 589832 | tf_op jit(solution)/shard_map/ppermute | solution.py:144
  172.3 10.0 %collective-permute-start.17 = (bf16[3,2,32,368]{3,2,1,0:T(8,128)(2,1)S(1)}, bf16[3,2,32,368]{3,2,1,0:T(8,128)(2,1)S(1)}, u32[]{:S(2)}, u32[]{:S(2)}) collective-permute-start(bf16[3,2,32,368]{3,2,1,0:T(8,128)(2,1)S(1)} %get-tuple-element.43), channel_id=1, source_target_pairs={{512,513},{513,517},{514,516},{515,512},{516,515},{517,519},{518,5... | collective-permute-start | bytes 423944 | tf_op jit(solution)/shard_map/ppermute | solution.py:144
  176.3 6.1 %collective-permute-start.16 = (bf16[3,2,32,368]{3,2,1,0:T(8,128)(2,1)S(1)}, bf16[3,2,32,368]{3,2,1,0:T(8,128)(2,1)S(1)}, u32[]{:S(2)}, u32[]{:S(2)}) collective-permute-start(bf16[3,2,32,368]{3,2,1,0:T(8,128)(2,1)S(1)} %get-tuple-element.44), channel_id=1, source_target_pairs={{512,512},{513,516},{514,517},{515,513},{516,514},{517,518},{518,5... | collective-permute-start | bytes 423944 | tf_op jit(solution)/shard_map/ppermute | solution.py:144
  182.5 15.4 %collective-permute-start.19 = (bf16[2,32,368]{2,1,0:T(8,128)(2,1)S(1)}, bf16[2,32,368]{2,1,0:T(8,128)(2,1)S(1)}, u32[]{:S(2)}, u32[]{:S(2)}) collective-permute-start(bf16[2,32,368]{2,1,0:T(8,128)(2,1)S(1)} %get-tuple-element.37), channel_id=1, source_target_pairs={{512,252},{513,253},{514,254},{515,255},{516,0},{517,1},{518,2},{5... | collective-permute-start | bytes 141320 | tf_op jit(solution)/shard_map/ppermute | solution.py:144
  183.8 14.1 %collective-permute-start.18 = (bf16[2,32,368]{2,1,0:T(8,128)(2,1)S(1)}, bf16[2,32,368]{2,1,0:T(8,128)(2,1)S(1)}, u32[]{:S(2)}, u32[]{:S(2)}) collective-permute-start(bf16[2,32,368]{2,1,0:T(8,128)(2,1)S(1)} %get-tuple-element.36), channel_id=1, source_target_pairs={{512,0},{513,1},{514,2},{515,3},{516,4},{517,5},{518,6},{519,7},{5... | collective-permute-start | bytes 141320 | tf_op jit(solution)/shard_map/ppermute | solution.py:144
  185.1 12.8 %collective-permute-start.21 = (bf16[2,32,368]{2,1,0:T(8,128)(2,1)S(1)}, bf16[2,32,368]{2,1,0:T(8,128)(2,1)S(1)}, u32[]{:S(2)}, u32[]{:S(2)}) collective-permute-start(bf16[2,32,368]{2,1,0:T(8,128)(2,1)S(1)} %get-tuple-element.39), channel_id=1, source_target_pairs={{512,508},{513,509},{514,510},{515,511},{516,256},{517,257},{518,2... | collective-permute-start | bytes 141320 | tf_op jit(solution)/shard_map/ppermute | solution.py:144
  186.4 11.5 %collective-permute-start.20 = (bf16[2,32,368]{2,1,0:T(8,128)(2,1)S(1)}, bf16[2,32,368]{2,1,0:T(8,128)(2,1)S(1)}, u32[]{:S(2)}, u32[]{:S(2)}) collective-permute-start(bf16[2,32,368]{2,1,0:T(8,128)(2,1)S(1)} %get-tuple-element.38), channel_id=1, source_target_pairs={{512,256},{513,257},{514,258},{515,259},{516,260},{517,261},{518,2... | collective-permute-start | bytes 141320 | tf_op jit(solution)/shard_map/ppermute | solution.py:144
  187.7 11.9 %collective-permute-start.22 = (bf16[2,32,368]{2,1,0:T(8,128)(2,1)S(1)}, bf16[2,32,368]{2,1,0:T(8,128)(2,1)S(1)}, u32[]{:S(2)}, u32[]{:S(2)}) collective-permute-start(bf16[2,32,368]{2,1,0:T(8,128)(2,1)S(1)} %get-tuple-element.40), channel_id=1, source_target_pairs={{512,764},{513,765},{514,766},{515,767},{516,512},{517,513},{518,5... | collective-permute-start | bytes 141320 | tf_op jit(solution)/shard_map/ppermute | solution.py:144
  (6 other events, 196.9 us)
Sparse Core Ops, SparseCore 0:
  42.9 65.4 all-gather.3

commit v8 on v7

--- a/solution.py
+++ b/solution.py
@@ -97,7 +97,7 @@
             pltpu.VMEM((2 * part, depth), jnp.float32),
             pltpu.SemaphoreType.DMA((quarters,)),
         ],
-        compiler_params=pltpu.CompilerParams(vmem_limit_bytes=51 << 20),
+        compiler_params=pltpu.CompilerParams(vmem_limit_bytes=48 << 20),
         cost_estimate=pl.CostEstimate(flops=2_600_000_000, bytes_accessed=14_000_000, transcendentals=524288),
         name="layer",
     )(lq, lk, gain, own_b, own_a, far_b, far_a, native, others)

time: 208 us -> 206 us (level)
  Pallas kernels: 25.1 us -> 21.6 us
  local copies, waits for them, and re-layouts: 13.5 us -> 15.6 us
    pallas_call x3, Pallas kernels: 23.7 us -> 20.2 us  [layer(): pl.pallas_call(layer_kernel, out_shape=(shape, shape), in_specs=[vmem] *...]
    unnamed x13 -> x17, local copies, waits for them, and re-layouts: 0.05 us -> 2.17 us
  transfers between devices with their start and end apart: 24 -> 24, of which waited for: 7 -> 7; matrix products, arithmetic and copies ran while one was open for 10% -> 10% of each run, Pallas kernels for 4% -> 3%
where the time goes in v8:
time: 206 us
  waiting for transfers between devices  71.9 us (35%)
  starting transfers between devices  39.1 us (19%)
  blocking collectives  33.1 us (16%)
  Pallas kernels  21.6 us (10%)
  local copies, waits for them, and re-layouts  15.6 us (8%)
  between operations  14 us (7%)
  other arithmetic  10.5 us (5%)
    ppermute x23, waiting for transfers between devices, send(): return lax.ppermute(value, AXES, pairs)  44.4 us
    ppermute x23, starting transfers between devices, send(): return lax.ppermute(value, AXES, pairs)  39.1 us
    all_gather x1, blocking collectives, body(): column = lax.all_gather(piece, 'dp', axis=0)  33.1 us
    all_gather x1, waiting for transfers between devices, body(): others = lax.all_gather(rolled, ('y', 'core'), axis=0)  27.5 us
    pallas_call x3, Pallas kernels, layer(): pl.pallas_call(layer_kernel, out_shape=(shape, shape), in_specs=[vmem] *...  20.2 us
    another operation x2, local copies, waits for them, and re-layouts, body(): qkv_weight[0].reshape(16, depth // 16, width)  8.92 us
  transfers between devices with their start and end apart: 24, of which 7 were waited for; matrix products, arithmetic and copies ran while one was open for 10% of the time, Pallas kernels for 3%

profile of v8, /device:TPU:128, one launch (start us, length us, event | category | flops | bytes accessed | tf_op | source)
XLA Modules:
  0.0 205.7 jit_solution(11073697061004919542)
XLA Ops:
  8.6 33.1 %all-gather = bf16[512,768]{1,0:T(8,128)(2,1)S(1)} all-gather(bf16[128,768]{1,0:T(8,128)(2,1)S(1)} %pad_maximum_fusion.3), channel_id=2, replica_groups=mesh['section'=3,'x'=4,'y'=8,'core'=2,'dp'=4] {'dp'}, dimensions={0}, use_global_device_ids=true | all-gather | bytes 983040 | tf_op jit(solution)/shard_map/all_gather | solution.py:171
  46.3 1.9 collective-permute-start
  49.6 1.3 collective-permute-start.2
  50.9 4.3 %copy.49 = bf16[1,1536,3,256]{3,2,1,0:T(4,128)(2,1)S(1)} copy(bf16[1,1536,3,256]{3,1,2,0:T(8,128)(2,1)} %param.10) | data formatting | bytes 4718592 | tf_op jit(solution)/shard_map/reshape;squeeze | solution.py:177
  55.3 4.6 %reshape.121 = bf16[16,96,768]{2,1,0:T(8,128)(2,1)} reshape(bf16[1,1536,3,256]{3,2,1,0:T(4,128)(2,1)S(1)} %copy.49) | data formatting | bytes 4718592 | tf_op jit(solution)/shard_map/reshape;squeeze | solution.py:177
  61.0 3.6 %fusion.4.native = bf16[20,128,768]{2,1,0:T(8,128)(2,1)} fusion(bf16[16,16,768]{2,1,0:T(8,128)(2,1)S(1)} %get-tuple-element.30, bf16[16,16,768]{2,1,0:T(8,128)(2,1)S(1)} %get-tuple-element.29, bf16[16,96,768]{2,1,0:T(8,128)(2,1)} %reshape.121), kind=kLoop, calls=%fused_computation.5 | loop fusion | flops 19660800 | bytes 7077888 | tf_op jit(solution)/shard_map/concatenate | solution.py:165
  65.8 10.2 %collective-permute-done.14 = bf16[184,1536]{1,0:T(8,128)(2,1)} collective-permute-done((bf16[184,1536]{1,0:T(8,128)(2,1)}, bf16[184,1536]{1,0:T(8,128)(2,1)}, u32[]{:S(2)}, u32[]{:S(2)}) %collective-permute-start.14) | collective-permute-done | bytes 565280 | tf_op jit(solution)/shard_map/ppermute | solution.py:144
  76.0 1.4 pad_maximum_fusion.2
  77.3 1.9 collective-permute-start.15
  80.9 27.5 %all-gather.4.cloned.1.call-done = bf16[48,128,768]{2,1,0:T(8,128)(2,1)} async-done(((bf16[3,128,768]{2,1,0:T(8,128)(2,1)}), bf16[48,128,768]{2,1,0:T(8,128)(2,1)}) %all-gather.4.cloned.1.call-update) | async-done | bytes 9437200 | tf_op jit(solution)/shard_map/all_gather | solution.py:173
  108.5 2.1 %copy-done = bf16[20,128,768]{2,1,0:T(8,128)(2,1)S(1)} copy-done((bf16[20,128,768]{2,1,0:T(8,128)(2,1)S(1)}, bf16[20,128,768]{2,1,0:T(8,128)(2,1)}, u32[]{:S(2)}) %copy-start) | copy-done | bytes 3932184
  110.6 6.7 %layer.3 = (bf16[64,1536]{1,0:T(8,128)(2,1)S(1)}, bf16[64,1536]{1,0:T(8,128)(2,1)S(1)}) custom-call(s32[128,1]{1,0:T(8,128)S(1)} %broadcast_in_dim.13.lq, s32[1,256]{1,0:T(1,128)S(1)} %broadcast_in_dim_reshape.3.lk, f32[1,1536]{1,0:T(1,128)S(1)} %copy-done.2, bf16[64,1536]{1,0:T(8,128)(2,1)S(1)} %pad_maximum_fusion.4.own_b, ...), custom_call_target="tpu_custom_call" | custom-call | flops 2600000000 | bytes 14000000 | tf_op jit(solution)/shard_map/layer/pallas_call | solution.py:89
  120.4 1.4 select_bitcast_fusion.1
  121.8 6.7 %layer.4 = (bf16[64,1536]{1,0:T(8,128)(2,1)S(1)}, bf16[64,1536]{1,0:T(8,128)(2,1)S(1)}) custom-call(s32[128,1]{1,0:T(8,128)S(1)} %broadcast_in_dim.13.lq, s32[1,256]{1,0:T(1,128)S(1)} %broadcast_in_dim_reshape.3.lk, f32[1,1536]{1,0:T(1,128)S(1)} %copy-done.2, bf16[64,1536]{1,0:T(8,128)(2,1)S(1)} %collective-permute-done.5.own_b, ...), custom_call_target="tpu_custom_call" | custom-call | flops 2600000000 | bytes 14000000 | tf_op jit(solution)/shard_map/layer/pallas_call | solution.py:89
  131.6 23.0 %collective-permute-done.9.own_b = bf16[64,1536]{1,0:T(8,128)(2,1)S(1)} collective-permute-done((bf16[64,1536]{1,0:T(8,128)(2,1)S(1)}, bf16[64,1536]{1,0:T(8,128)(2,1)S(1)}, u32[]{:S(2)}, u32[]{:S(2)}) %collective-permute-start.9) | collective-permute-done | bytes 196640 | tf_op jit(solution)/shard_map/ppermute | solution.py:144
  154.5 1.9 collective-permute-start.11
  156.4 3.0 %collective-permute-done.10.own_a = bf16[64,1536]{1,0:T(8,128)(2,1)S(1)} collective-permute-done((bf16[64,1536]{1,0:T(8,128)(2,1)S(1)}, bf16[64,1536]{1,0:T(8,128)(2,1)S(1)}, u32[]{:S(2)}, u32[]{:S(2)}) %collective-permute-start.10) | collective-permute-done | bytes 196640 | tf_op jit(solution)/shard_map/ppermute | solution.py:144
  159.4 1.9 collective-permute-start.12
  162.8 6.8 %layer.5 = (bf16[64,1536]{1,0:T(8,128)(2,1)S(1)}, bf16[64,1536]{1,0:T(8,128)(2,1)S(1)}) custom-call(s32[128,1]{1,0:T(8,128)S(1)} %broadcast_in_dim.13.lq, s32[1,256]{1,0:T(1,128)S(1)} %broadcast_in_dim_reshape.3.lk, f32[1,1536]{1,0:T(1,128)S(1)} %copy-done.2, bf16[64,1536]{1,0:T(8,128)(2,1)S(1)} %collective-permute-done.9.own_b, ...), custom_call_target="tpu_custom_call" | custom-call | flops 2600000000 | bytes 14000000 | tf_op jit(solution)/shard_map/layer/pallas_call | solution.py:89
  169.5 1.4 decode.1
  170.9 4.0 %collective-permute-start.17 = (bf16[3,2,32,368]{3,2,1,0:T(8,128)(2,1)S(1)}, bf16[3,2,32,368]{3,2,1,0:T(8,128)(2,1)S(1)}, u32[]{:S(2)}, u32[]{:S(2)}) collective-permute-start(bf16[3,2,32,368]{3,2,1,0:T(8,128)(2,1)S(1)} %get-tuple-element.43), channel_id=1, source_target_pairs={{512,513},{513,517},{514,516},{515,512},{516,515},{517,519},{518,5... | collective-permute-start | bytes 423944 | tf_op jit(solution)/shard_map/ppermute | solution.py:144
  175.6 5.4 %collective-permute-done.17 = bf16[3,2,32,368]{3,2,1,0:T(8,128)(2,1)S(1)} collective-permute-done((bf16[3,2,32,368]{3,2,1,0:T(8,128)(2,1)S(1)}, bf16[3,2,32,368]{3,2,1,0:T(8,128)(2,1)S(1)}, u32[]{:S(2)}, u32[]{:S(2)}) %collective-permute-start.17) | collective-permute-done | bytes 141344 | tf_op jit(solution)/shard_map/ppermute | solution.py:144
  186.3 10.2 %collective-permute-start.22 = (bf16[2,32,368]{2,1,0:T(8,128)(2,1)S(1)}, bf16[2,32,368]{2,1,0:T(8,128)(2,1)S(1)}, u32[]{:S(2)}, u32[]{:S(2)}) collective-permute-start(bf16[2,32,368]{2,1,0:T(8,128)(2,1)S(1)} %get-tuple-element.40), channel_id=1, source_target_pairs={{512,764},{513,765},{514,766},{515,767},{516,512},{517,513},{518,5... | collective-permute-start | bytes 141320 | tf_op jit(solution)/shard_map/ppermute | solution.py:144
  196.5 1.7 collective-permute-done.22
  (81 shorter events, 25.8 us)
Async XLA Ops:
  6.5 101.9 %all-gather.4.cloned.1.call-start = ((), (), s32[]{:S(2)}) async-start(), calls=%async_computation | async-start | bytes 10027008 | tf_op jit(solution)/shard_map/all_gather | solution.py:173
  43.7 32.3 %collective-permute-start.14 = (bf16[184,1536]{1,0:T(8,128)(2,1)}, bf16[184,1536]{1,0:T(8,128)(2,1)}, u32[]{:S(2)}, u32[]{:S(2)}) collective-permute-start(bf16[184,1536]{1,0:T(8,128)(2,1)} %dynamic-slice_bitcast_fusion), channel_id=1, source_target_pairs={{256,512},{257,513},{258,514},{259,515},{260,516},{261,517},{262,5... | collective-permute-start | bytes 1695752 | tf_op jit(solution)/shard_map/ppermute | solution.py:144
  44.9 31.0 %collective-permute-start.13 = (bf16[184,1536]{1,0:T(8,128)(2,1)}, bf16[184,1536]{1,0:T(8,128)(2,1)}, u32[]{:S(2)}, u32[]{:S(2)}) collective-permute-start(bf16[184,1536]{1,0:T(8,128)(2,1)} %dynamic-slice_bitcast_fusion), channel_id=1, source_target_pairs={{0,512},{1,513},{2,514},{3,515},{4,516},{5,517},{6,518},{7,519},{8... | collective-permute-start | bytes 1695752 | tf_op jit(solution)/shard_map/ppermute | solution.py:144
  46.3 18.4 %collective-permute-start = (s32[256]{0:T(256)S(1)}, s32[256]{0:T(256)S(1)}, u32[]{:S(2)}, u32[]{:S(2)}) collective-permute-start(s32[256]{0:T(256)S(1)} %bitcast.94), channel_id=1, source_target_pairs={{0,4},{1,5},{2,6},{3,7},{4,0},{5,1},{6,2},{7,3},{8,12},{9,13},{10,... | collective-permute-start | bytes 3080 | tf_op jit(solution)/shard_map/ppermute | solution.py:144
  48.9 15.8 %collective-permute-start.1 = (bf16[64,1536]{1,0:T(8,128)(2,1)}, bf16[64,1536]{1,0:T(8,128)(2,1)S(1)}, u32[]{:S(2)}, u32[]{:S(2)}) collective-permute-start(bf16[64,1536]{1,0:T(8,128)(2,1)} %get-tuple-element.33), channel_id=1, source_target_pairs={{0,0},{1,3},{2,4},{3,7},{4,1},{5,2},{6,5},{7,6},{8,8},{9,11},{10,1... | collective-permute-start | bytes 589832 | tf_op jit(solution)/shard_map/ppermute | solution.py:144
  49.6 15.2 %collective-permute-start.2 = (bf16[64,1536]{1,0:T(8,128)(2,1)S(1)}, bf16[64,1536]{1,0:T(8,128)(2,1)}, u32[]{:S(2)}, u32[]{:S(2)}) collective-permute-start(bf16[64,1536]{1,0:T(8,128)(2,1)S(1)} %get-tuple-element.34), channel_id=1, source_target_pairs={{0,3},{1,0},{2,7},{3,4},{4,2},{5,1},{6,6},{7,5},{8,11},{9,8},{10,1... | collective-permute-start | bytes 589832 | tf_op jit(solution)/shard_map/ppermute | solution.py:144
  77.3 43.0 %collective-permute-start.15 = (bf16[2,184,1536]{2,1,0:T(8,128)(2,1)S(1)}, bf16[2,184,1536]{2,1,0:T(8,128)(2,1)S(1)}, u32[]{:S(2)}, u32[]{:S(2)}) collective-permute-start(bf16[2,184,1536]{2,1,0:T(8,128)(2,1)S(1)} %pad_maximum_fusion.2), channel_id=1, source_target_pairs={{512,516},{513,517},{514,518},{515,519},{516,512},{517,513},{518,5... | collective-permute-start | bytes 3391496 | tf_op jit(solution)/shard_map/ppermute | solution.py:144
  79.3 1.6 collective-permute-start.3
  80.0 0.9 collective-permute-start.4
  117.3 1.4 collective-permute-start.5
  118.0 1.5 collective-permute-start.6
  118.7 3.0 %collective-permute-start.7 = (bf16[64,1536]{1,0:T(8,128)(2,1)S(1)}, bf16[64,1536]{1,0:T(8,128)(2,1)S(1)}, u32[]{:S(2)}, u32[]{:S(2)}) collective-permute-start(bf16[64,1536]{1,0:T(8,128)(2,1)S(1)} %collective-permute-done.5.own_b), channel_id=1, source_target_pairs={{256,260},{257,261},{258,262},{259,263},{260,256},{261,257},{262,2... | collective-permute-start | bytes 589832 | tf_op jit(solution)/shard_map/ppermute | solution.py:144
  119.5 2.2 %collective-permute-start.8 = (bf16[64,1536]{1,0:T(8,128)(2,1)S(1)}, bf16[64,1536]{1,0:T(8,128)(2,1)S(1)}, u32[]{:S(2)}, u32[]{:S(2)}) collective-permute-start(bf16[64,1536]{1,0:T(8,128)(2,1)S(1)} %collective-permute-done.6.own_a), channel_id=1, source_target_pairs={{256,260},{257,261},{258,262},{259,263},{260,256},{261,257},{262,2... | collective-permute-start | bytes 589832 | tf_op jit(solution)/shard_map/ppermute | solution.py:144
  128.5 26.0 %collective-permute-start.9 = (bf16[64,1536]{1,0:T(8,128)(2,1)S(1)}, bf16[64,1536]{1,0:T(8,128)(2,1)S(1)}, u32[]{:S(2)}, u32[]{:S(2)}) collective-permute-start(bf16[64,1536]{1,0:T(8,128)(2,1)S(1)} %get-tuple-element.22), channel_id=1, source_target_pairs={{256,761},{257,512},{258,515},{259,762},{260,765},{261,516},{262,5... | collective-permute-start | bytes 589832 | tf_op jit(solution)/shard_map/ppermute | solution.py:144
  129.8 29.6 %collective-permute-start.10 = (bf16[64,1536]{1,0:T(8,128)(2,1)S(1)}, bf16[64,1536]{1,0:T(8,128)(2,1)S(1)}, u32[]{:S(2)}, u32[]{:S(2)}) collective-permute-start(bf16[64,1536]{1,0:T(8,128)(2,1)S(1)} %get-tuple-element.23), channel_id=1, source_target_pairs={{256,512},{257,513},{258,514},{259,515},{260,516},{261,517},{262,5... | collective-permute-start | bytes 589832 | tf_op jit(solution)/shard_map/ppermute | solution.py:144
  154.5 7.1 %collective-permute-start.11 = (bf16[64,1536]{1,0:T(8,128)(2,1)S(1)}, bf16[64,1536]{1,0:T(8,128)(2,1)S(1)}, u32[]{:S(2)}, u32[]{:S(2)}) collective-permute-start(bf16[64,1536]{1,0:T(8,128)(2,1)S(1)} %collective-permute-done.9.own_b), channel_id=1, source_target_pairs={{512,516},{513,517},{514,518},{515,519},{516,512},{517,513},{518,5... | collective-permute-start | bytes 589832 | tf_op jit(solution)/shard_map/ppermute | solution.py:144
  159.4 3.3 %collective-permute-start.12 = (bf16[64,1536]{1,0:T(8,128)(2,1)S(1)}, bf16[64,1536]{1,0:T(8,128)(2,1)S(1)}, u32[]{:S(2)}, u32[]{:S(2)}) collective-permute-start(bf16[64,1536]{1,0:T(8,128)(2,1)S(1)} %collective-permute-done.10.own_a), channel_id=1, source_target_pairs={{512,516},{513,517},{514,518},{515,519},{516,512},{517,513},{518,5... | collective-permute-start | bytes 589832 | tf_op jit(solution)/shard_map/ppermute | solution.py:144
  170.9 10.0 %collective-permute-start.17 = (bf16[3,2,32,368]{3,2,1,0:T(8,128)(2,1)S(1)}, bf16[3,2,32,368]{3,2,1,0:T(8,128)(2,1)S(1)}, u32[]{:S(2)}, u32[]{:S(2)}) collective-permute-start(bf16[3,2,32,368]{3,2,1,0:T(8,128)(2,1)S(1)} %get-tuple-element.43), channel_id=1, source_target_pairs={{512,513},{513,517},{514,516},{515,512},{516,515},{517,519},{518,5... | collective-permute-start | bytes 423944 | tf_op jit(solution)/shard_map/ppermute | solution.py:144
  174.9 6.1 %collective-permute-start.16 = (bf16[3,2,32,368]{3,2,1,0:T(8,128)(2,1)S(1)}, bf16[3,2,32,368]{3,2,1,0:T(8,128)(2,1)S(1)}, u32[]{:S(2)}, u32[]{:S(2)}) collective-permute-start(bf16[3,2,32,368]{3,2,1,0:T(8,128)(2,1)S(1)} %get-tuple-element.44), channel_id=1, source_target_pairs={{512,512},{513,516},{514,517},{515,513},{516,514},{517,518},{518,5... | collective-permute-start | bytes 423944 | tf_op jit(solution)/shard_map/ppermute | solution.py:144
  181.1 15.4 %collective-permute-start.19 = (bf16[2,32,368]{2,1,0:T(8,128)(2,1)S(1)}, bf16[2,32,368]{2,1,0:T(8,128)(2,1)S(1)}, u32[]{:S(2)}, u32[]{:S(2)}) collective-permute-start(bf16[2,32,368]{2,1,0:T(8,128)(2,1)S(1)} %get-tuple-element.37), channel_id=1, source_target_pairs={{512,252},{513,253},{514,254},{515,255},{516,0},{517,1},{518,2},{5... | collective-permute-start | bytes 141320 | tf_op jit(solution)/shard_map/ppermute | solution.py:144
  182.4 14.1 %collective-permute-start.18 = (bf16[2,32,368]{2,1,0:T(8,128)(2,1)S(1)}, bf16[2,32,368]{2,1,0:T(8,128)(2,1)S(1)}, u32[]{:S(2)}, u32[]{:S(2)}) collective-permute-start(bf16[2,32,368]{2,1,0:T(8,128)(2,1)S(1)} %get-tuple-element.36), channel_id=1, source_target_pairs={{512,0},{513,1},{514,2},{515,3},{516,4},{517,5},{518,6},{519,7},{5... | collective-permute-start | bytes 141320 | tf_op jit(solution)/shard_map/ppermute | solution.py:144
  183.7 12.8 %collective-permute-start.21 = (bf16[2,32,368]{2,1,0:T(8,128)(2,1)S(1)}, bf16[2,32,368]{2,1,0:T(8,128)(2,1)S(1)}, u32[]{:S(2)}, u32[]{:S(2)}) collective-permute-start(bf16[2,32,368]{2,1,0:T(8,128)(2,1)S(1)} %get-tuple-element.39), channel_id=1, source_target_pairs={{512,508},{513,509},{514,510},{515,511},{516,256},{517,257},{518,2... | collective-permute-start | bytes 141320 | tf_op jit(solution)/shard_map/ppermute | solution.py:144
  185.0 11.5 %collective-permute-start.20 = (bf16[2,32,368]{2,1,0:T(8,128)(2,1)S(1)}, bf16[2,32,368]{2,1,0:T(8,128)(2,1)S(1)}, u32[]{:S(2)}, u32[]{:S(2)}) collective-permute-start(bf16[2,32,368]{2,1,0:T(8,128)(2,1)S(1)} %get-tuple-element.38), channel_id=1, source_target_pairs={{512,256},{513,257},{514,258},{515,259},{516,260},{517,261},{518,2... | collective-permute-start | bytes 141320 | tf_op jit(solution)/shard_map/ppermute | solution.py:144
  186.3 11.9 %collective-permute-start.22 = (bf16[2,32,368]{2,1,0:T(8,128)(2,1)S(1)}, bf16[2,32,368]{2,1,0:T(8,128)(2,1)S(1)}, u32[]{:S(2)}, u32[]{:S(2)}) collective-permute-start(bf16[2,32,368]{2,1,0:T(8,128)(2,1)S(1)} %get-tuple-element.40), channel_id=1, source_target_pairs={{512,764},{513,765},{514,766},{515,767},{516,512},{517,513},{518,5... | collective-permute-start | bytes 141320 | tf_op jit(solution)/shard_map/ppermute | solution.py:144
  (8 other events, 200.7 us)
Sparse Core Ops, SparseCore 0:
  42.9 65.4 all-gather.3
